TPU v7x, 128 devices: a whole 4x4x4 slice. The times are simulated.
128 devices in a mesh: col: 16 (over y, x), row: 8 (over z, core).
Axes of the slice: x: 4, y: 4, z: 4, core: 2. Of those that a mesh axis runs over, the one named last changes fastest.
Arguments:
- matrix: float32 [24, 512, 8192], P(None, 'row', 'col'), may hold values from -0.4 to 2.4, as said below
- pivots: int32 [16, 512], replicated, may hold values from 0 to 511, as said below
- seeds: float32 [16, 512, 512], P('col'), may hold values from -1 to 2, as said below
Outputs:
- factors: float32 [24, 512, 8192], P(None, 'row', 'col')
Inputs may be any that keep to these rules, and one draw needn't show every extreme that they name: Each row of pivots is an ordering of 0 .. 511. Block (r, j) of matrix is zero where r and j differ by more than 8. seeds[k] approximates the inverse of block (k, k) of matrix after the replacement of rows by pivots[k].
All inputs are finite; a program needn't handle non-finite values.
Results may differ from a plain program's by a relative error of at most 0.0001.
Values sent between devices are 32-bit elements; how exact they have to be, the bound alone decides.
No kernel may reach another device: no remote copies, remote signals or barrier semaphores. Data moves between devices by JAX's collectives and lax.ppermute only.
A program may use at most 64 MiB of HBM per device.

v0:
```python
import jax
import jax.numpy as jnp
from jax import lax
from jax.sharding import PartitionSpec as P

HB = 8
SWEEPS = 2


def sent_to_all(array, axis):
    length = lax.axis_size(axis)
    return lax.all_to_all(
        jnp.broadcast_to(array[None], (length, *array.shape)), axis, 0, 0, tiled=True
    )


def in_order(parts, dim):
    lengths = list(parts.shape[1:])
    lengths[dim] *= parts.shape[0]
    return jnp.moveaxis(parts, 0, dim).reshape(lengths)


def collect(array, axis, dim):
    parts = sent_to_all(array, axis)
    return in_order(parts, dim)


def from_root(block, axis, source):
    block = jnp.where(lax.axis_index(axis) == source, block, jnp.zeros_like(block))
    return lax.psum(block, axis)


def dot_high(left, right):
    return jnp.dot(left, right, precision=lax.Precision.HIGHEST, preferred_element_type=jnp.float32)


def refine(pivot_block, approx, identity):
    for sweep_index in range(SWEEPS):
        approx = dot_high(approx, 2.0 * identity - dot_high(pivot_block, approx))
    return approx


def local(matrix, pivots, seeds):
    col_count = lax.axis_size("col")
    col_index = lax.axis_index("col")
    row_index = lax.axis_index("row")
    row_share = matrix.shape[1]
    panel_width = matrix.shape[2]
    identity = jnp.eye(panel_width, dtype=jnp.float32)
    seed_block = seeds[0]

    def eliminate(panel_index, factors):
        local_row = lax.dynamic_index_in_dim(factors, panel_index, 0, keepdims=False)
        block_row = collect(local_row, "row", 0)
        ordering = lax.dynamic_index_in_dim(pivots, panel_index, 0, keepdims=False)
        swapped = jnp.take(block_row, ordering, axis=0)
        block_row = jnp.where(col_index >= panel_index, swapped, block_row)
        local_row = lax.dynamic_slice_in_dim(block_row, row_index * row_share, row_share, 0)
        factors = lax.dynamic_update_index_in_dim(factors, local_row, panel_index, 0)
        is_owner = col_index == panel_index
        approx = lax.cond(
            is_owner, lambda: refine(block_row, seed_block, identity), lambda: seed_block
        )
        below_rows = lax.dynamic_slice_in_dim(factors, panel_index + 1, HB, 0)
        below_flat = below_rows.reshape(HB * row_share, panel_width)
        scaled = lax.cond(is_owner, lambda: dot_high(below_flat, approx), lambda: below_flat)
        in_reach = (col_index > panel_index) & (col_index <= panel_index + HB)
        arrived = from_root(scaled, "col", panel_index)
        updated = below_flat - dot_high(arrived, block_row)
        result = jnp.where(is_owner, scaled, jnp.where(in_reach, updated, below_flat))
        return lax.dynamic_update_slice_in_dim(
            factors, result.reshape(HB, row_share, panel_width), panel_index + 1, 0
        )

    return lax.fori_loop(0, col_count, eliminate, matrix)


def solution(mesh):
    return jax.shard_map(
        local,
        mesh=mesh,
        in_specs=(P(None, "row", "col"), P(), P("col", None, None)),
        out_specs=P(None, "row", "col"),
        check_vma=False,
    )
```

profile of v0, /device:TPU:31, one launch (start us, length us, event | category | flops | bytes accessed | tf_op | source)
XLA Modules:
  0.0 2139.8 jit_solution(5086388667008317163)
XLA Ops:
  10.7 2122.6 %while.17 = (s32[]{:T(128)}, f32[24,64,512]{2,1,0:T(8,128)}, s32[]{:T(128)}, s32[16,512]{1,0:T(8,128)}, s32[]{:T(128)}, /*index=5*/f32[512,512]{1,0:T(8,128)S(1)...) while((s32[]{:T(128)}, f32[24,64,512]{2,1,0:T(8,128)}, ...), condition=%wide.region_6.7_spmd.clone.clone, body=%wide.region_0.6_spmd.clone.clone.sunk | while | flops 9667090432 | bytes 55199700 | solution.py:75
  20.5 13.2 all-to-all-done
  42.7 92.2 %all-reduce.2.cloned.1.call-done = f32[512,512]{1,0:T(8,128)} async-done(((f32[512,512]{1,0:T(8,128)}), f32[512,512]{1,0:T(8,128)}) %all-reduce.2.cloned.1.call-update) | async-done | bytes 1048592 | tf_op jit(solution)/shard_map/while/body/eval_jaxpr/psum | solution.py:30
  149.5 13.2 all-to-all-done
  171.6 95.1 %all-reduce.2.cloned.1.call-done = f32[512,512]{1,0:T(8,128)} async-done(((f32[512,512]{1,0:T(8,128)}), f32[512,512]{1,0:T(8,128)}) %all-reduce.2.cloned.1.call-update) | async-done | bytes 1048592 | tf_op jit(solution)/shard_map/while/body/eval_jaxpr/psum | solution.py:30
  281.4 13.2 all-to-all-done
  303.5 95.8 %all-reduce.2.cloned.1.call-done = f32[512,512]{1,0:T(8,128)} async-done(((f32[512,512]{1,0:T(8,128)}), f32[512,512]{1,0:T(8,128)}) %all-reduce.2.cloned.1.call-update) | async-done | bytes 1048592 | tf_op jit(solution)/shard_map/while/body/eval_jaxpr/psum | solution.py:30
  414.0 13.2 all-to-all-done
  436.1 96.3 %all-reduce.2.cloned.1.call-done = f32[512,512]{1,0:T(8,128)} async-done(((f32[512,512]{1,0:T(8,128)}), f32[512,512]{1,0:T(8,128)}) %all-reduce.2.cloned.1.call-update) | async-done | bytes 1048592 | tf_op jit(solution)/shard_map/while/body/eval_jaxpr/psum | solution.py:30
  547.1 13.2 all-to-all-done
  569.3 95.1 %all-reduce.2.cloned.1.call-done = f32[512,512]{1,0:T(8,128)} async-done(((f32[512,512]{1,0:T(8,128)}), f32[512,512]{1,0:T(8,128)}) %all-reduce.2.cloned.1.call-update) | async-done | bytes 1048592 | tf_op jit(solution)/shard_map/while/body/eval_jaxpr/psum | solution.py:30
  701.2 94.8 %all-reduce.2.cloned.1.call-done = f32[512,512]{1,0:T(8,128)} async-done(((f32[512,512]{1,0:T(8,128)}), f32[512,512]{1,0:T(8,128)}) %all-reduce.2.cloned.1.call-update) | async-done | bytes 1048592 | tf_op jit(solution)/shard_map/while/body/eval_jaxpr/psum | solution.py:30
  832.7 96.0 %all-reduce.2.cloned.1.call-done = f32[512,512]{1,0:T(8,128)} async-done(((f32[512,512]{1,0:T(8,128)}), f32[512,512]{1,0:T(8,128)}) %all-reduce.2.cloned.1.call-update) | async-done | bytes 1048592 | tf_op jit(solution)/shard_map/while/body/eval_jaxpr/psum | solution.py:30
  965.6 96.0 %all-reduce.2.cloned.1.call-done = f32[512,512]{1,0:T(8,128)} async-done(((f32[512,512]{1,0:T(8,128)}), f32[512,512]{1,0:T(8,128)}) %all-reduce.2.cloned.1.call-update) | async-done | bytes 1048592 | tf_op jit(solution)/shard_map/while/body/eval_jaxpr/psum | solution.py:30
  1076.2 13.2 all-to-all-done
  1098.3 95.7 %all-reduce.2.cloned.1.call-done = f32[512,512]{1,0:T(8,128)} async-done(((f32[512,512]{1,0:T(8,128)}), f32[512,512]{1,0:T(8,128)}) %all-reduce.2.cloned.1.call-update) | async-done | bytes 1048592 | tf_op jit(solution)/shard_map/while/body/eval_jaxpr/psum | solution.py:30
  1230.8 96.1 %all-reduce.2.cloned.1.call-done = f32[512,512]{1,0:T(8,128)} async-done(((f32[512,512]{1,0:T(8,128)}), f32[512,512]{1,0:T(8,128)}) %all-reduce.2.cloned.1.call-update) | async-done | bytes 1048592 | tf_op jit(solution)/shard_map/while/body/eval_jaxpr/psum | solution.py:30
  1363.7 97.5 %all-reduce.2.cloned.1.call-done = f32[512,512]{1,0:T(8,128)} async-done(((f32[512,512]{1,0:T(8,128)}), f32[512,512]{1,0:T(8,128)}) %all-reduce.2.cloned.1.call-update) | async-done | bytes 1048592 | tf_op jit(solution)/shard_map/while/body/eval_jaxpr/psum | solution.py:30
  1498.1 97.2 %all-reduce.2.cloned.1.call-done = f32[512,512]{1,0:T(8,128)} async-done(((f32[512,512]{1,0:T(8,128)}), f32[512,512]{1,0:T(8,128)}) %all-reduce.2.cloned.1.call-update) | async-done | bytes 1048592 | tf_op jit(solution)/shard_map/while/body/eval_jaxpr/psum | solution.py:30
  1610.0 13.2 all-to-all-done
  1632.1 96.3 %all-reduce.2.cloned.1.call-done = f32[512,512]{1,0:T(8,128)} async-done(((f32[512,512]{1,0:T(8,128)}), f32[512,512]{1,0:T(8,128)}) %all-reduce.2.cloned.1.call-update) | async-done | bytes 1048592 | tf_op jit(solution)/shard_map/while/body/eval_jaxpr/psum | solution.py:30
  1765.2 95.9 %all-reduce.2.cloned.1.call-done = f32[512,512]{1,0:T(8,128)} async-done(((f32[512,512]{1,0:T(8,128)}), f32[512,512]{1,0:T(8,128)}) %all-reduce.2.cloned.1.call-update) | async-done | bytes 1048592 | tf_op jit(solution)/shard_map/while/body/eval_jaxpr/psum | solution.py:30
  1897.9 97.3 %all-reduce.2.cloned.1.call-done = f32[512,512]{1,0:T(8,128)} async-done(((f32[512,512]{1,0:T(8,128)}), f32[512,512]{1,0:T(8,128)}) %all-reduce.2.cloned.1.call-update) | async-done | bytes 1048592 | tf_op jit(solution)/shard_map/while/body/eval_jaxpr/psum | solution.py:30
  2046.6 82.2 %all-reduce.2.cloned.1.call-done = f32[512,512]{1,0:T(8,128)} async-done(((f32[512,512]{1,0:T(8,128)}), f32[512,512]{1,0:T(8,128)}) %all-reduce.2.cloned.1.call-update) | async-done | bytes 1048592 | tf_op jit(solution)/shard_map/while/body/eval_jaxpr/psum | solution.py:30
  (369 shorter events, 544.0 us)
Async XLA Ops:
  18.7 116.2 %all-reduce.2.cloned.1.call-start = ((), (), s32[]{:S(2)}) async-start(), calls=%async_computation.1 | async-start | bytes 2097152 | tf_op jit(solution)/shard_map/while/body/eval_jaxpr/psum | solution.py:30
  141.0 21.7 %all-to-all-start = ((f32[8,64,512]{2,1,0:T(8,128)}), f32[8,64,512]{2,1,0:T(8,128)S(1)}, u32[]{:S(2)}, u32[]{:S(2)}) async-start(f32[8,64,512]{2,1,0:T(8,128)} %broadcast_in_dim.78), calls=%async_computation | async-start | bytes 2097152 | tf_op jit(solution)/shard_map/while/body/eval_jaxpr/all_to_all | solution.py:12
  147.6 119.1 %all-reduce.2.cloned.1.call-start = ((), (), s32[]{:S(2)}) async-start(), calls=%async_computation.1 | async-start | bytes 2097152 | tf_op jit(solution)/shard_map/while/body/eval_jaxpr/psum | solution.py:30
  272.9 21.7 %all-to-all-start = ((f32[8,64,512]{2,1,0:T(8,128)}), f32[8,64,512]{2,1,0:T(8,128)S(1)}, u32[]{:S(2)}, u32[]{:S(2)}) async-start(f32[8,64,512]{2,1,0:T(8,128)} %broadcast_in_dim.78), calls=%async_computation | async-start | bytes 2097152 | tf_op jit(solution)/shard_map/while/body/eval_jaxpr/all_to_all | solution.py:12
  279.5 119.8 %all-reduce.2.cloned.1.call-start = ((), (), s32[]{:S(2)}) async-start(), calls=%async_computation.1 | async-start | bytes 2097152 | tf_op jit(solution)/shard_map/while/body/eval_jaxpr/psum | solution.py:30
  405.5 21.7 %all-to-all-start = ((f32[8,64,512]{2,1,0:T(8,128)}), f32[8,64,512]{2,1,0:T(8,128)S(1)}, u32[]{:S(2)}, u32[]{:S(2)}) async-start(f32[8,64,512]{2,1,0:T(8,128)} %broadcast_in_dim.78), calls=%async_computation | async-start | bytes 2097152 | tf_op jit(solution)/shard_map/while/body/eval_jaxpr/all_to_all | solution.py:12
  412.1 120.3 %all-reduce.2.cloned.1.call-start = ((), (), s32[]{:S(2)}) async-start(), calls=%async_computation.1 | async-start | bytes 2097152 | tf_op jit(solution)/shard_map/while/body/eval_jaxpr/psum | solution.py:30
  545.3 119.1 %all-reduce.2.cloned.1.call-start = ((), (), s32[]{:S(2)}) async-start(), calls=%async_computation.1 | async-start | bytes 2097152 | tf_op jit(solution)/shard_map/while/body/eval_jaxpr/psum | solution.py:30
  677.2 118.8 %all-reduce.2.cloned.1.call-start = ((), (), s32[]{:S(2)}) async-start(), calls=%async_computation.1 | async-start | bytes 2097152 | tf_op jit(solution)/shard_map/while/body/eval_jaxpr/psum | solution.py:30
  802.1 21.7 %all-to-all-start = ((f32[8,64,512]{2,1,0:T(8,128)}), f32[8,64,512]{2,1,0:T(8,128)S(1)}, u32[]{:S(2)}, u32[]{:S(2)}) async-start(f32[8,64,512]{2,1,0:T(8,128)} %broadcast_in_dim.78), calls=%async_computation | async-start | bytes 2097152 | tf_op jit(solution)/shard_map/while/body/eval_jaxpr/all_to_all | solution.py:12
  808.7 120.0 %all-reduce.2.cloned.1.call-start = ((), (), s32[]{:S(2)}) async-start(), calls=%async_computation.1 | async-start | bytes 2097152 | tf_op jit(solution)/shard_map/while/body/eval_jaxpr/psum | solution.py:30
  941.6 120.0 %all-reduce.2.cloned.1.call-start = ((), (), s32[]{:S(2)}) async-start(), calls=%async_computation.1 | async-start | bytes 2097152 | tf_op jit(solution)/shard_map/while/body/eval_jaxpr/psum | solution.py:30
  1067.7 21.7 %all-to-all-start = ((f32[8,64,512]{2,1,0:T(8,128)}), f32[8,64,512]{2,1,0:T(8,128)S(1)}, u32[]{:S(2)}, u32[]{:S(2)}) async-start(f32[8,64,512]{2,1,0:T(8,128)} %broadcast_in_dim.78), calls=%async_computation | async-start | bytes 2097152 | tf_op jit(solution)/shard_map/while/body/eval_jaxpr/all_to_all | solution.py:12
  1074.3 119.7 %all-reduce.2.cloned.1.call-start = ((), (), s32[]{:S(2)}) async-start(), calls=%async_computation.1 | async-start | bytes 2097152 | tf_op jit(solution)/shard_map/while/body/eval_jaxpr/psum | solution.py:30
  1206.8 120.1 %all-reduce.2.cloned.1.call-start = ((), (), s32[]{:S(2)}) async-start(), calls=%async_computation.1 | async-start | bytes 2097152 | tf_op jit(solution)/shard_map/while/body/eval_jaxpr/psum | solution.py:30
  1339.7 121.5 %all-reduce.2.cloned.1.call-start = ((), (), s32[]{:S(2)}) async-start(), calls=%async_computation.1 | async-start | bytes 2097152 | tf_op jit(solution)/shard_map/while/body/eval_jaxpr/psum | solution.py:30
  1474.1 121.2 %all-reduce.2.cloned.1.call-start = ((), (), s32[]{:S(2)}) async-start(), calls=%async_computation.1 | async-start | bytes 2097152 | tf_op jit(solution)/shard_map/while/body/eval_jaxpr/psum | solution.py:30
  1601.5 21.7 %all-to-all-start = ((f32[8,64,512]{2,1,0:T(8,128)}), f32[8,64,512]{2,1,0:T(8,128)S(1)}, u32[]{:S(2)}, u32[]{:S(2)}) async-start(f32[8,64,512]{2,1,0:T(8,128)} %broadcast_in_dim.78), calls=%async_computation | async-start | bytes 2097152 | tf_op jit(solution)/shard_map/while/body/eval_jaxpr/all_to_all | solution.py:12
  1608.1 120.3 %all-reduce.2.cloned.1.call-start = ((), (), s32[]{:S(2)}) async-start(), calls=%async_computation.1 | async-start | bytes 2097152 | tf_op jit(solution)/shard_map/while/body/eval_jaxpr/psum | solution.py:30
  1734.6 21.7 %all-to-all-start = ((f32[8,64,512]{2,1,0:T(8,128)}), f32[8,64,512]{2,1,0:T(8,128)S(1)}, u32[]{:S(2)}, u32[]{:S(2)}) async-start(f32[8,64,512]{2,1,0:T(8,128)} %broadcast_in_dim.78), calls=%async_computation | async-start | bytes 2097152 | tf_op jit(solution)/shard_map/while/body/eval_jaxpr/all_to_all | solution.py:12
  1741.2 119.9 %all-reduce.2.cloned.1.call-start = ((), (), s32[]{:S(2)}) async-start(), calls=%async_computation.1 | async-start | bytes 2097152 | tf_op jit(solution)/shard_map/while/body/eval_jaxpr/psum | solution.py:30
  1873.9 121.3 %all-reduce.2.cloned.1.call-start = ((), (), s32[]{:S(2)}) async-start(), calls=%async_computation.1 | async-start | bytes 2097152 | tf_op jit(solution)/shard_map/while/body/eval_jaxpr/psum | solution.py:30
  2001.3 21.7 %all-to-all-start = ((f32[8,64,512]{2,1,0:T(8,128)}), f32[8,64,512]{2,1,0:T(8,128)S(1)}, u32[]{:S(2)}, u32[]{:S(2)}) async-start(f32[8,64,512]{2,1,0:T(8,128)} %broadcast_in_dim.78), calls=%async_computation | async-start | bytes 2097152 | tf_op jit(solution)/shard_map/while/body/eval_jaxpr/all_to_all | solution.py:12
  2008.0 120.8 %all-reduce.2.cloned.1.call-start = ((), (), s32[]{:S(2)}) async-start(), calls=%async_computation.1 | async-start | bytes 2097152 | tf_op jit(solution)/shard_map/while/body/eval_jaxpr/psum | solution.py:30
  (26 other events, 199.5 us)
Sparse Core Ops, SparseCore 0:
  42.8 92.0 all-reduce.1
  171.8 94.9 all-reduce.1
  303.6 95.6 all-reduce.1
  436.3 96.1 all-reduce.1
  569.4 94.9 all-reduce.1
  701.3 94.6 all-reduce.1
  832.9 95.8 all-reduce.1
  965.7 95.8 all-reduce.1
  1098.5 95.4 all-reduce.1
  1230.9 95.9 all-reduce.1
  1363.9 97.3 all-reduce.1
  1498.2 97.0 all-reduce.1
  1632.2 96.1 all-reduce.1
  1765.3 95.7 all-reduce.1
  1898.0 97.0 all-reduce.1
  2046.7 82.0 all-reduce.1
where the time goes:
time: 2150 us; the launch traced here: 2140 us
  waiting for transfers between devices  1730 us (80%)
  local copies, waits for them, and re-layouts  153 us (7%)
  starting transfers between devices  106 us (5%)
  other arithmetic  70.7 us (3%)
  matrix products  64.5 us (3%)
    psum x16, waiting for transfers between devices, from_root(): return lax.psum(block, axis)  1520 us
    all_to_all x16, waiting for transfers between devices, sent_to_all(): lax.all_to_all(jnp.broadcast_to(array[None], (length, *array.shape)), axi...  212 us
    all_to_all x16, starting transfers between devices, sent_to_all(): lax.all_to_all(jnp.broadcast_to(array[None], (length, *array.shape)), axi...  106 us
    dot_general x21, matrix products, dot_high(): jnp.dot(left, right, precision=lax.Precision.HIGHEST, preferred_element_t...  64.5 us
  transfers between devices with their start and end apart: 32, of which 32 were waited for; matrix products, arithmetic and copies ran while one was open for 1% of the time, Pallas kernels for 0%

commit v1 on v0

v1 whole, which is shorter than its diff:
```python
import functools

import jax
import jax.numpy as jnp
from jax import lax
from jax.experimental import pallas as pl
from jax.experimental.pallas import tpu as pltpu
from jax.sharding import PartitionSpec as P

HB = 8
PANELS = 16
B = 512
ROWS = 8
SHARE = B // ROWS
TALL = HB * SHARE

SLOT_X = {1: (0, 0), 2: (1, -1), 4: (2, -2), 5: (2, 3), 6: (2, 2)}
SLOT_Y = {2: (0, 0), 3: (1, -1), 4: (1, 2)}


def split(value):
    high = value.astype(jnp.bfloat16)
    low = (value - high.astype(jnp.float32)).astype(jnp.bfloat16)
    return high, low


def dot(left, right):
    return jnp.dot(left, right, preferred_element_type=jnp.float32)


def dot3(left, right):
    return dot(left[0], right[0]) + (dot(left[0], right[1]) + dot(left[1], right[0]))


def exact_rows(onehot, value):
    high = value.astype(jnp.bfloat16)
    rest = value - high.astype(jnp.float32)
    mid = rest.astype(jnp.bfloat16)
    low = (rest - mid.astype(jnp.float32)).astype(jnp.bfloat16)
    return dot(onehot, high) + (dot(onehot, mid) + dot(onehot, low))


def slice_offset(place, turn, swap):
    z = place // 2
    core = place % 2
    other = core if swap == 0 else 1 - core
    return (2 * ((z + 4 - turn) % 4) + other) * SHARE


def gather_copies(parts, buffer, sems, place):
    copies = []
    for index, part in enumerate(parts):
        offset = pl.multiple_of(slice_offset(place, index % 4, index // 4), SHARE)
        copies.append(pltpu.make_async_copy(part, buffer.at[pl.ds(offset, SHARE)], sems.at[index]))
    return copies


def invert_kernel(step, scal, factors_in, cur_in, y_high_ref, y_low_ref, *rest):
    parts, (factors, cur), (pivot, below, y_high, y_low, high, low, other_high, other_low, result, sems) = (
        rest[:8], rest[8:10], rest[10:])
    panel = scal[0]
    place = scal[1]

    @pl.when(panel == step)
    def _():
        copies = gather_copies(parts, pivot, sems, place)
        copies.append(pltpu.make_async_copy(y_high_ref, y_high, sems.at[8]))
        copies.append(pltpu.make_async_copy(y_low_ref, y_low, sems.at[9]))
        rows = pl.ds((step + 1) * SHARE, TALL)
        copies.append(pltpu.make_async_copy(factors_in.at[rows], below, sems.at[10]))
        for copy in copies:
            copy.start()
        for copy in copies:
            copy.wait()
        chunk = 128
        y_pair = (y_high[...], y_low[...])
        for first in range(0, B, chunk):
            block = pl.ds(first, chunk)
            product = dot3(split(pivot[block]), y_pair)
            row_ids = lax.broadcasted_iota(jnp.int32, (chunk, B), 0) + first
            col_ids = lax.broadcasted_iota(jnp.int32, (chunk, B), 1)
            error = jnp.where(row_ids == col_ids, 1.0, 0.0) - product
            high[block], low[block] = split(error)
        error_pair = (high[...], low[...])
        for first in range(0, B, chunk):
            block = pl.ds(first, chunk)
            other_high[block], other_low[block] = split(dot3((high[block], low[block]), error_pair))
            base = y_high[block].astype(jnp.float32) + y_low[block].astype(jnp.float32)
            result[block] = base + dot3((y_high[block], y_low[block]), error_pair)
        square_pair = (other_high[...], other_low[...])
        for first in range(0, B, chunk):
            block = pl.ds(first, chunk)
            base = result[block]
            high[block], low[block] = split(base + dot3(split(base), square_pair))
        inverse_pair = (high[...], low[...])
        for first in range(0, TALL, chunk):
            block = pl.ds(first, chunk)
            result[block] = dot3(split(below[block]), inverse_pair)
        to_cur = pltpu.make_async_copy(result, cur, sems.at[0])
        to_factors = pltpu.make_async_copy(result, factors.at[rows], sems.at[1])
        to_cur.start()
        to_factors.start()
        to_cur.wait()
        to_factors.wait()


def update_kernel(step, slot, scal, factors_in, cur_in, following_in, received, pivot_ref, *rest):
    parts, (factors, cur, following), (upper, multipliers, target, high, low, swapped, picks, sems) = (
        rest[:8], rest[8:11], rest[11:])
    panel = scal[0]
    place = scal[1]
    table = SLOT_X if slot == 0 else SLOT_Y
    lag = jnp.int32(0)
    takes = jnp.bool_(False)
    for distance, (amount, _) in table.items():
        if step - amount >= 0:
            here = panel == step + distance
            takes = takes | here
            lag = jnp.where(here, amount, lag)
    source = step - lag
    owns = (panel == step) if slot == 0 else jnp.bool_(False)

    @pl.when(takes | owns)
    def _():
        copies = gather_copies(parts, upper, sems, place)
        copies.append(pltpu.make_async_copy(pivot_ref.at[source], picks, sems.at[8]))
        for copy in copies:
            copy.start()

        @pl.when(takes)
        def _():
            rows = pl.ds(pl.multiple_of((source + 1) * SHARE, SHARE), TALL)
            load_m = pltpu.make_async_copy(received, multipliers, sems.at[9])
            load_t = pltpu.make_async_copy(factors_in.at[rows], target, sems.at[10])
            load_m.start()
            load_t.start()
            load_m.wait()
            load_t.wait()
        for copy in copies:
            copy.wait()

        @pl.when(takes)
        def _():
            rows = pl.ds(pl.multiple_of((source + 1) * SHARE, SHARE), TALL)
            keep = pltpu.make_async_copy(multipliers, cur, sems.at[0])
            keep.start()
            high[...], low[...] = split(upper[...])
            upper_pair = (high[...], low[...])
            for first in range(0, TALL, 128):
                block = pl.ds(first, 128)
                target[block] = target[block] - dot3(split(multipliers[block]), upper_pair)
            store_t = pltpu.make_async_copy(target, factors.at[rows], sems.at[1])
            store_n = pltpu.make_async_copy(target.at[pl.ds(0, SHARE)], following, sems.at[2])
            store_t.start()
            store_n.start()
            store_n.wait()
            store_t.wait()
            keep.wait()

        lanes = lax.broadcasted_iota(jnp.int32, (SHARE, 128), 1)
        pick = picks[...]
        onehot = jnp.concatenate(
            [jnp.where(pick == lanes + 128 * group, 1.0, 0.0) for group in range(B // 128)], axis=1
        ).astype(jnp.bfloat16)
        swapped[...] = exact_rows(onehot, upper[...])
        store = pltpu.make_async_copy(
            swapped, factors.at[pl.ds(pl.multiple_of(source * SHARE, SHARE), SHARE)], sems.at[3]
        )
        store.start()
        store.wait()


ANY = pl.BlockSpec(memory_space=pl.ANY)
SMEM = pl.BlockSpec(memory_space=pltpu.SMEM)


def f32(*shape):
    return pltpu.VMEM(shape, jnp.float32)


def b16(*shape):
    return pltpu.VMEM(shape, jnp.bfloat16)


def invert(step, scal, factors, cur, y_high, y_low, parts):
    return pl.pallas_call(
        functools.partial(invert_kernel, step),
        out_shape=[jax.ShapeDtypeStruct(a.shape, a.dtype) for a in (factors, cur)],
        in_specs=[SMEM] + [ANY] * 12,
        out_specs=[ANY] * 2,
        scratch_shapes=[f32(B, B), f32(TALL, B), b16(B, B), b16(B, B), b16(B, B), b16(B, B), b16(B, B), b16(B, B), f32(B, B),
                        pltpu.SemaphoreType.DMA((11,))],
        input_output_aliases={1: 0, 2: 1},
        compiler_params=pltpu.CompilerParams(vmem_limit_bytes=48 << 20),
    )(scal, factors, cur, y_high, y_low, *parts)


def update(step, slot, scal, factors, cur, following, received, picks, parts):
    return pl.pallas_call(
        functools.partial(update_kernel, step, slot),
        out_shape=[jax.ShapeDtypeStruct(a.shape, a.dtype) for a in (factors, cur, following)],
        in_specs=[SMEM] + [ANY] * 13,
        out_specs=[ANY] * 3,
        scratch_shapes=[f32(B, B), f32(TALL, B), f32(TALL, B), b16(B, B), b16(B, B), f32(SHARE, B),
                        pltpu.VMEM((SHARE, 128), jnp.int32), pltpu.SemaphoreType.DMA((11,))],
        input_output_aliases={1: 0, 2: 1, 3: 2},
        compiler_params=pltpu.CompilerParams(vmem_limit_bytes=48 << 20),
    )(scal, factors, cur, following, received, picks, *parts)


def gather(share, panels):
    def move(array, target):
        pairs = [(c * ROWS + r, c * ROWS + target(r)) for c in panels for r in range(ROWS)]
        return lax.ppermute(array, ("col", "row"), pairs)

    turned = [share] + [move(share, lambda r, t=turn: (r + 2 * t) % ROWS) for turn in (1, 2, 3)]
    return turned + [move(part, lambda r: r ^ 1) for part in turned]


def send(cur, step, table):
    pairs = []
    for distance, (lag, sender) in table.items():
        if step - lag >= 0 and step + distance < PANELS:
            for r in range(ROWS):
                pairs.append(((step + sender) * ROWS + r, (step + distance) * ROWS + r))
    return lax.ppermute(cur, ("col", "row"), pairs)


def in_slot(step, table):
    return [step + d for d, (lag, _) in table.items() if step - lag >= 0 and step + d < PANELS]


def local(matrix, pivots, seeds):
    panel = lax.axis_index("col")
    place = lax.axis_index("row")
    scal = jnp.stack([panel, place]).astype(jnp.int32)
    factors = matrix.reshape(-1, B)
    own_pivots = lax.dynamic_index_in_dim(pivots, panel, 0, keepdims=False)
    onehot = (own_pivots[:, None] == jnp.arange(B, dtype=jnp.int32)[None, :]).astype(jnp.float32)
    start = jnp.dot(seeds[0], onehot, precision=lax.Precision.HIGHEST, preferred_element_type=jnp.float32)
    y_high, y_low = split(start)
    picks = jnp.broadcast_to(
        lax.dynamic_slice_in_dim(pivots, place * SHARE, SHARE, 1)[:, :, None], (PANELS, SHARE, 128)
    )
    first = jnp.maximum(panel - HB, 0)
    following = lax.dynamic_slice_in_dim(factors, first * SHARE, SHARE, 0)
    cur = jnp.zeros((TALL, B), jnp.float32)
    for step in range(PANELS):
        parts = gather(following, [step] + in_slot(step, SLOT_X))
        factors, cur = invert(step, scal, factors, cur, y_high, y_low, parts)
        panels = in_slot(step, SLOT_X)
        received = send(cur, step, SLOT_X) if panels else cur
        factors, cur, following = update(step, 0, scal, factors, cur, following, received, picks, parts)
        panels = in_slot(step, SLOT_Y)
        if panels:
            parts = gather(following, panels)
            received = send(cur, step, SLOT_Y)
            factors, cur, following = update(step, 1, scal, factors, cur, following, received, picks, parts)
    at = (panel + 1) * SHARE
    own = lax.dynamic_slice_in_dim(factors, at, TALL, 0)
    own = lax.dot_general(
        own, onehot, (((1,), (1,)), ((), ())), precision=lax.Precision.HIGHEST, preferred_element_type=jnp.float32
    )
    factors = lax.dynamic_update_slice_in_dim(factors, own, at, 0)
    return factors.reshape(matrix.shape)


def solution(mesh):
    return jax.shard_map(
        local,
        mesh=mesh,
        in_specs=(P(None, "row", "col"), P(), P("col", None, None)),
        out_specs=P(None, "row", "col"),
        check_vma=False,
    )
```

time: 2150 us -> 2690 us (1.25)
  starting transfers between devices: 106 us -> 2320 us
  waiting for transfers between devices: 1730 us -> 134 us
  Pallas kernels: 0 us -> 92 us
  other arithmetic: 70.7 us -> 0.08 us
  matrix products: 64.5 us -> 3.32 us
    ppermute x0 -> x239, starting transfers between devices: none -> 2320 us  [the longest x210 1710 us: move(): return lax.ppermute(array, ('col', 'row'), pairs)]
    psum x16 -> x0, waiting for transfers between devices: 1520 us -> none  [from_root(): return lax.psum(block, axis)]
    all_to_all x16 -> x0, waiting for transfers between devices: 212 us -> none  [sent_to_all(): lax.all_to_all(jnp.broadcast_to(array[None], (length, *array.shape)), axi...]
    ppermute x0 -> x239, waiting for transfers between devices: none -> 134 us  [the longest x29 127 us: send(): return lax.ppermute(cur, ('col', 'row'), pairs)]
    unnamed x3 -> x262, local copies, waits for them, and re-layouts: 4.12 us -> 123 us
    all_to_all x16 -> x0, starting transfers between devices: 106 us -> none  [sent_to_all(): lax.all_to_all(jnp.broadcast_to(array[None], (length, *array.shape)), axi...]
    pallas_call x0 -> x46, Pallas kernels: none -> 92 us  [the longest x30 69.6 us: update(): pl.pallas_call(functools.partial(update_kernel, step, slot), out_shape=[j...]
    dot_general x21 -> x2, matrix products: 64.5 us -> 3.32 us  [the longest x1 2.14 us: local(): lax.dot_general(own, onehot, (((1,), (1,)), ((), ())), precision=lax.Prec...]
  transfers between devices with their start and end apart: 32 -> 239, of which waited for: 32 -> 14; matrix products, arithmetic and copies ran while one was open for 1% -> 2% of each run, Pallas kernels for 0% -> 0%
where the time goes in v1:
time: 2690 us; the launch traced here: 2680 us
  starting transfers between devices  2320 us (86%)
  waiting for transfers between devices  134 us (5%)
  local copies, waits for them, and re-layouts  127 us (5%)
  Pallas kernels  92 us (3%)
    ppermute x210, starting transfers between devices, move(): return lax.ppermute(array, ('col', 'row'), pairs)  1710 us
    ppermute x29, starting transfers between devices, send(): return lax.ppermute(cur, ('col', 'row'), pairs)  609 us
    ppermute x29, waiting for transfers between devices, send(): return lax.ppermute(cur, ('col', 'row'), pairs)  127 us
    unnamed x262, local copies, waits for them, and re-layouts  123 us
    pallas_call x30, Pallas kernels, update(): pl.pallas_call(functools.partial(update_kernel, step, slot), out_shape=[j...  69.6 us
  transfers between devices with their start and end apart: 239, of which 14 were waited for; matrix products, arithmetic and copies ran while one was open for 2% of the time, Pallas kernels for 0%

profile of v1, /device:TPU:31, one launch (start us, length us, event | category | flops | bytes accessed | tf_op | source)
XLA Modules:
  0.0 2680.4 jit_solution(11854890273662458528)
XLA Ops:
  86.9 43.5 %collective-permute-start.11 = (f32[64,512]{1,0:T(8,128)S(1)}, f32[64,512]{1,0:T(8,128)S(1)}, u32[]{:S(2)}, u32[]{:S(2)}) collective-permute-start(f32[64,512]{1,0:T(8,128)S(1)} %get-tuple-element.129.rest_0_), channel_id=1, source_target_pairs={{16,22},{17,23},{18,16},{19,17},{20,18},{21,19},{22,20},{23,21}} | collective-permute-start | bytes 393224 | tf_op jit(solution)/shard_map/ppermute | solution.py:214
  135.9 25.6 collective-permute-start.18
  239.0 35.9 %collective-permute-start.24 = (f32[512,512]{1,0:T(8,128)S(1)}, f32[512,512]{1,0:T(8,128)S(1)}, u32[]{:S(2)}, u32[]{:S(2)}) collective-permute-start(f32[512,512]{1,0:T(8,128)S(1)} %get-tuple-element.136.cur_in), channel_id=1, source_target_pairs={{8,24},{9,25},{10,26},{11,27},{12,28},{13,29},{14,30},{15,31},{0,3... | collective-permute-start | bytes 3145736 | tf_op jit(solution)/shard_map/ppermute | solution.py:226
  418.9 16.9 collective-permute-start.39
  439.6 37.6 %collective-permute-start.40 = (f32[512,512]{1,0:T(8,128)S(1)}, f32[512,512]{1,0:T(8,128)S(1)}, u32[]{:S(2)}, u32[]{:S(2)}) collective-permute-start(f32[512,512]{1,0:T(8,128)S(1)} %get-tuple-element.144.cur_in), channel_id=1, source_target_pairs={{16,32},{17,33},{18,34},{19,35},{20,36},{21,37},{22,38},{23,39},{8... | collective-permute-start | bytes 3145736 | tf_op jit(solution)/shard_map/ppermute | solution.py:226
  642.9 38.5 %collective-permute-start.56 = (f32[512,512]{1,0:T(8,128)S(1)}, f32[512,512]{1,0:T(8,128)S(1)}, u32[]{:S(2)}, u32[]{:S(2)}) collective-permute-start(f32[512,512]{1,0:T(8,128)S(1)} %get-tuple-element.152.cur_in), channel_id=1, source_target_pairs={{24,40},{25,41},{26,42},{27,43},{28,44},{29,45},{30,46},{31,47},{1... | collective-permute-start | bytes 3145736 | tf_op jit(solution)/shard_map/ppermute | solution.py:226
  849.8 38.5 %collective-permute-start.72 = (f32[512,512]{1,0:T(8,128)S(1)}, f32[512,512]{1,0:T(8,128)S(1)}, u32[]{:S(2)}, u32[]{:S(2)}) collective-permute-start(f32[512,512]{1,0:T(8,128)S(1)} %get-tuple-element.160.cur_in), channel_id=1, source_target_pairs={{32,48},{33,49},{34,50},{35,51},{36,52},{37,53},{38,54},{39,55},{2... | collective-permute-start | bytes 3145736 | tf_op jit(solution)/shard_map/ppermute | solution.py:226
  1057.8 38.5 %collective-permute-start.88 = (f32[512,512]{1,0:T(8,128)S(1)}, f32[512,512]{1,0:T(8,128)S(1)}, u32[]{:S(2)}, u32[]{:S(2)}) collective-permute-start(f32[512,512]{1,0:T(8,128)S(1)} %get-tuple-element.168.cur_in), channel_id=1, source_target_pairs={{40,56},{41,57},{42,58},{43,59},{44,60},{45,61},{46,62},{47,63},{3... | collective-permute-start | bytes 3145736 | tf_op jit(solution)/shard_map/ppermute | solution.py:226
  1245.5 17.9 collective-permute-start.103
  1267.1 39.1 %collective-permute-start.104 = (f32[512,512]{1,0:T(8,128)S(1)}, f32[512,512]{1,0:T(8,128)S(1)}, u32[]{:S(2)}, u32[]{:S(2)}) collective-permute-start(f32[512,512]{1,0:T(8,128)S(1)} %get-tuple-element.176.cur_in), channel_id=1, source_target_pairs={{48,64},{49,65},{50,66},{51,67},{52,68},{53,69},{54,70},{55,71},{4... | collective-permute-start | bytes 3145736 | tf_op jit(solution)/shard_map/ppermute | solution.py:226
  1459.1 17.6 collective-permute-start.119
  1480.4 39.1 %collective-permute-start.120 = (f32[512,512]{1,0:T(8,128)S(1)}, f32[512,512]{1,0:T(8,128)S(1)}, u32[]{:S(2)}, u32[]{:S(2)}) collective-permute-start(f32[512,512]{1,0:T(8,128)S(1)} %get-tuple-element.184.cur_in), channel_id=1, source_target_pairs={{56,72},{57,73},{58,74},{59,75},{60,76},{61,77},{62,78},{63,79},{4... | collective-permute-start | bytes 3145736 | tf_op jit(solution)/shard_map/ppermute | solution.py:226
  1674.0 17.0 collective-permute-start.135
  1694.8 39.1 %collective-permute-start.136 = (f32[512,512]{1,0:T(8,128)S(1)}, f32[512,512]{1,0:T(8,128)S(1)}, u32[]{:S(2)}, u32[]{:S(2)}) collective-permute-start(f32[512,512]{1,0:T(8,128)S(1)} %get-tuple-element.192.cur_in), channel_id=1, source_target_pairs={{64,80},{65,81},{66,82},{67,83},{68,84},{69,85},{70,86},{71,87},{5... | collective-permute-start | bytes 3145736 | tf_op jit(solution)/shard_map/ppermute | solution.py:226
  1908.6 22.8 collective-permute-done.151.received
  2104.6 17.6 collective-permute-start.167
  2123.8 23.4 collective-permute-done.167.received
  2174.5 34.3 %collective-permute-start.178 = (f32[64,512]{1,0:T(8,128)}, f32[64,512]{1,0:T(8,128)S(1)}, u32[]{:S(2)}, u32[]{:S(2)}) collective-permute-start(f32[64,512]{1,0:T(8,128)} %copy-done.41), channel_id=1, source_target_pairs={{88,94},{89,95},{90,88},{91,89},{92,90},{93,91},{94,92},{95,93},{9... | collective-permute-start | bytes 393224 | tf_op jit(solution)/shard_map/ppermute | solution.py:214
  2271.3 17.3 collective-permute-start.183
  2290.2 23.7 collective-permute-done.183.received
  2372.2 23.4 collective-permute-start.199
  2399.4 39.1 %collective-permute-start.200 = (f32[512,512]{1,0:T(8,128)S(1)}, f32[512,512]{1,0:T(8,128)S(1)}, u32[]{:S(2)}, u32[]{:S(2)}) collective-permute-start(f32[512,512]{1,0:T(8,128)S(1)} %get-tuple-element.224.cur_in), channel_id=1, source_target_pairs={{96,112},{97,113},{98,114},{99,115},{100,116},{101,117},{102,118},... | collective-permute-start | bytes 3145736 | tf_op jit(solution)/shard_map/ppermute | solution.py:226
  2504.1 22.5 collective-permute-done.215.received
  2610.5 22.8 collective-permute-done.231.received
  (771 shorter events, 1985.1 us)
Async XLA Ops:
  86.2 49.0 %collective-permute-start.8 = (f32[512,512]{1,0:T(8,128)S(1)}, f32[512,512]{1,0:T(8,128)S(1)}, u32[]{:S(2)}, u32[]{:S(2)}) collective-permute-start(f32[512,512]{1,0:T(8,128)S(1)} %get-tuple-element.128.cur_in), channel_id=1, source_target_pairs={{0,16},{1,17},{2,18},{3,19},{4,20},{5,21},{6,22},{7,23}} | collective-permute-start | bytes 3145736 | tf_op jit(solution)/shard_map/ppermute | solution.py:226
  86.9 45.5 %collective-permute-start.11 = (f32[64,512]{1,0:T(8,128)S(1)}, f32[64,512]{1,0:T(8,128)S(1)}, u32[]{:S(2)}, u32[]{:S(2)}) collective-permute-start(f32[64,512]{1,0:T(8,128)S(1)} %get-tuple-element.129.rest_0_), channel_id=1, source_target_pairs={{16,22},{17,23},{18,16},{19,17},{20,18},{21,19},{22,20},{23,21}} | collective-permute-start | bytes 393224 | tf_op jit(solution)/shard_map/ppermute | solution.py:214
  135.9 54.3 %collective-permute-start.18 = (f32[64,512]{1,0:T(8,128)}, f32[64,512]{1,0:T(8,128)S(1)}, u32[]{:S(2)}, u32[]{:S(2)}) collective-permute-start(f32[64,512]{1,0:T(8,128)} %get-tuple-element.132.rest_0_), channel_id=1, source_target_pairs={{8,14},{9,15},{10,8},{11,9},{12,10},{13,11},{14,12},{15,13},{16,22... | collective-permute-start | bytes 393224 | tf_op jit(solution)/shard_map/ppermute | solution.py:214
  239.0 104.4 %collective-permute-start.24 = (f32[512,512]{1,0:T(8,128)S(1)}, f32[512,512]{1,0:T(8,128)S(1)}, u32[]{:S(2)}, u32[]{:S(2)}) collective-permute-start(f32[512,512]{1,0:T(8,128)S(1)} %get-tuple-element.136.cur_in), channel_id=1, source_target_pairs={{8,24},{9,25},{10,26},{11,27},{12,28},{13,29},{14,30},{15,31},{0,3... | collective-permute-start | bytes 3145736 | tf_op jit(solution)/shard_map/ppermute | solution.py:226
  439.6 106.1 %collective-permute-start.40 = (f32[512,512]{1,0:T(8,128)S(1)}, f32[512,512]{1,0:T(8,128)S(1)}, u32[]{:S(2)}, u32[]{:S(2)}) collective-permute-start(f32[512,512]{1,0:T(8,128)S(1)} %get-tuple-element.144.cur_in), channel_id=1, source_target_pairs={{16,32},{17,33},{18,34},{19,35},{20,36},{21,37},{22,38},{23,39},{8... | collective-permute-start | bytes 3145736 | tf_op jit(solution)/shard_map/ppermute | solution.py:226
  548.8 43.2 %collective-permute-start.50 = (f32[64,512]{1,0:T(8,128)}, f32[64,512]{1,0:T(8,128)S(1)}, u32[]{:S(2)}, u32[]{:S(2)}) collective-permute-start(f32[64,512]{1,0:T(8,128)} %copy-done.9), channel_id=1, source_target_pairs={{24,30},{25,31},{26,24},{27,25},{28,26},{29,27},{30,28},{31,29},{3... | collective-permute-start | bytes 393224 | tf_op jit(solution)/shard_map/ppermute | solution.py:214
  642.9 107.0 %collective-permute-start.56 = (f32[512,512]{1,0:T(8,128)S(1)}, f32[512,512]{1,0:T(8,128)S(1)}, u32[]{:S(2)}, u32[]{:S(2)}) collective-permute-start(f32[512,512]{1,0:T(8,128)S(1)} %get-tuple-element.152.cur_in), channel_id=1, source_target_pairs={{24,40},{25,41},{26,42},{27,43},{28,44},{29,45},{30,46},{31,47},{1... | collective-permute-start | bytes 3145736 | tf_op jit(solution)/shard_map/ppermute | solution.py:226
  753.0 45.1 %collective-permute-start.66 = (f32[64,512]{1,0:T(8,128)}, f32[64,512]{1,0:T(8,128)S(1)}, u32[]{:S(2)}, u32[]{:S(2)}) collective-permute-start(f32[64,512]{1,0:T(8,128)} %copy-done.13), channel_id=1, source_target_pairs={{32,38},{33,39},{34,32},{35,33},{36,34},{37,35},{38,36},{39,37},{4... | collective-permute-start | bytes 393224 | tf_op jit(solution)/shard_map/ppermute | solution.py:214
  849.8 107.0 %collective-permute-start.72 = (f32[512,512]{1,0:T(8,128)S(1)}, f32[512,512]{1,0:T(8,128)S(1)}, u32[]{:S(2)}, u32[]{:S(2)}) collective-permute-start(f32[512,512]{1,0:T(8,128)S(1)} %get-tuple-element.160.cur_in), channel_id=1, source_target_pairs={{32,48},{33,49},{34,50},{35,51},{36,52},{37,53},{38,54},{39,55},{2... | collective-permute-start | bytes 3145736 | tf_op jit(solution)/shard_map/ppermute | solution.py:226
  959.9 45.1 %collective-permute-start.82 = (f32[64,512]{1,0:T(8,128)}, f32[64,512]{1,0:T(8,128)S(1)}, u32[]{:S(2)}, u32[]{:S(2)}) collective-permute-start(f32[64,512]{1,0:T(8,128)} %copy-done.17), channel_id=1, source_target_pairs={{40,46},{41,47},{42,40},{43,41},{44,42},{45,43},{46,44},{47,45},{4... | collective-permute-start | bytes 393224 | tf_op jit(solution)/shard_map/ppermute | solution.py:214
  1057.8 107.0 %collective-permute-start.88 = (f32[512,512]{1,0:T(8,128)S(1)}, f32[512,512]{1,0:T(8,128)S(1)}, u32[]{:S(2)}, u32[]{:S(2)}) collective-permute-start(f32[512,512]{1,0:T(8,128)S(1)} %get-tuple-element.168.cur_in), channel_id=1, source_target_pairs={{40,56},{41,57},{42,58},{43,59},{44,60},{45,61},{46,62},{47,63},{3... | collective-permute-start | bytes 3145736 | tf_op jit(solution)/shard_map/ppermute | solution.py:226
  1167.9 45.2 %collective-permute-start.98 = (f32[64,512]{1,0:T(8,128)}, f32[64,512]{1,0:T(8,128)S(1)}, u32[]{:S(2)}, u32[]{:S(2)}) collective-permute-start(f32[64,512]{1,0:T(8,128)} %copy-done.21), channel_id=1, source_target_pairs={{48,54},{49,55},{50,48},{51,49},{52,50},{53,51},{54,52},{55,53},{5... | collective-permute-start | bytes 393224 | tf_op jit(solution)/shard_map/ppermute | solution.py:214
  1267.1 111.4 %collective-permute-start.104 = (f32[512,512]{1,0:T(8,128)S(1)}, f32[512,512]{1,0:T(8,128)S(1)}, u32[]{:S(2)}, u32[]{:S(2)}) collective-permute-start(f32[512,512]{1,0:T(8,128)S(1)} %get-tuple-element.176.cur_in), channel_id=1, source_target_pairs={{48,64},{49,65},{50,66},{51,67},{52,68},{53,69},{54,70},{55,71},{4... | collective-permute-start | bytes 3145736 | tf_op jit(solution)/shard_map/ppermute | solution.py:226
  1381.6 45.9 %collective-permute-start.114 = (f32[64,512]{1,0:T(8,128)}, f32[64,512]{1,0:T(8,128)S(1)}, u32[]{:S(2)}, u32[]{:S(2)}) collective-permute-start(f32[64,512]{1,0:T(8,128)} %copy-done.25), channel_id=1, source_target_pairs={{56,62},{57,63},{58,56},{59,57},{60,58},{61,59},{62,60},{63,61},{6... | collective-permute-start | bytes 393224 | tf_op jit(solution)/shard_map/ppermute | solution.py:214
  1480.4 111.3 %collective-permute-start.120 = (f32[512,512]{1,0:T(8,128)S(1)}, f32[512,512]{1,0:T(8,128)S(1)}, u32[]{:S(2)}, u32[]{:S(2)}) collective-permute-start(f32[512,512]{1,0:T(8,128)S(1)} %get-tuple-element.184.cur_in), channel_id=1, source_target_pairs={{56,72},{57,73},{58,74},{59,75},{60,76},{61,77},{62,78},{63,79},{4... | collective-permute-start | bytes 3145736 | tf_op jit(solution)/shard_map/ppermute | solution.py:226
  1594.8 46.7 %collective-permute-start.130 = (f32[64,512]{1,0:T(8,128)}, f32[64,512]{1,0:T(8,128)S(1)}, u32[]{:S(2)}, u32[]{:S(2)}) collective-permute-start(f32[64,512]{1,0:T(8,128)} %copy-done.29), channel_id=1, source_target_pairs={{64,70},{65,71},{66,64},{67,65},{68,66},{69,67},{70,68},{71,69},{7... | collective-permute-start | bytes 393224 | tf_op jit(solution)/shard_map/ppermute | solution.py:214
  1694.8 112.0 %collective-permute-start.136 = (f32[512,512]{1,0:T(8,128)S(1)}, f32[512,512]{1,0:T(8,128)S(1)}, u32[]{:S(2)}, u32[]{:S(2)}) collective-permute-start(f32[512,512]{1,0:T(8,128)S(1)} %get-tuple-element.192.cur_in), channel_id=1, source_target_pairs={{64,80},{65,81},{66,82},{67,83},{68,84},{69,85},{70,86},{71,87},{5... | collective-permute-start | bytes 3145736 | tf_op jit(solution)/shard_map/ppermute | solution.py:226
  1809.9 47.3 %collective-permute-start.146 = (f32[64,512]{1,0:T(8,128)}, f32[64,512]{1,0:T(8,128)S(1)}, u32[]{:S(2)}, u32[]{:S(2)}) collective-permute-start(f32[64,512]{1,0:T(8,128)} %copy-done.33), channel_id=1, source_target_pairs={{72,78},{73,79},{74,72},{75,73},{76,74},{77,75},{78,76},{79,77},{8... | collective-permute-start | bytes 393224 | tf_op jit(solution)/shard_map/ppermute | solution.py:214
  1939.6 81.4 %collective-permute-start.152 = (f32[512,512]{1,0:T(8,128)S(1)}, f32[512,512]{1,0:T(8,128)S(1)}, u32[]{:S(2)}, u32[]{:S(2)}) collective-permute-start(f32[512,512]{1,0:T(8,128)S(1)} %get-tuple-element.200.cur_in), channel_id=1, source_target_pairs={{72,88},{73,89},{74,90},{75,91},{76,92},{77,93},{78,94},{79,95},{6... | collective-permute-start | bytes 3145736 | tf_op jit(solution)/shard_map/ppermute | solution.py:226
  2024.1 47.0 %collective-permute-start.162 = (f32[64,512]{1,0:T(8,128)}, f32[64,512]{1,0:T(8,128)S(1)}, u32[]{:S(2)}, u32[]{:S(2)}) collective-permute-start(f32[64,512]{1,0:T(8,128)} %copy-done.37), channel_id=1, source_target_pairs={{80,86},{81,87},{82,80},{83,81},{84,82},{85,83},{86,84},{87,85},{8... | collective-permute-start | bytes 393224 | tf_op jit(solution)/shard_map/ppermute | solution.py:214
  2104.6 42.6 %collective-permute-start.167 = (f32[512,512]{1,0:T(8,128)S(1)}, f32[512,512]{1,0:T(8,128)S(1)}, u32[]{:S(2)}, u32[]{:S(2)}) collective-permute-start(f32[512,512]{1,0:T(8,128)S(1)} %get-tuple-element.206.cur_in), channel_id=1, source_target_pairs={{80,88},{81,89},{82,90},{83,91},{84,92},{85,93},{86,94},{87,95},{7... | collective-permute-start | bytes 3145736 | tf_op jit(solution)/shard_map/ppermute | solution.py:226
  2174.5 64.1 %collective-permute-start.178 = (f32[64,512]{1,0:T(8,128)}, f32[64,512]{1,0:T(8,128)S(1)}, u32[]{:S(2)}, u32[]{:S(2)}) collective-permute-start(f32[64,512]{1,0:T(8,128)} %copy-done.41), channel_id=1, source_target_pairs={{88,94},{89,95},{90,88},{91,89},{92,90},{93,91},{94,92},{95,93},{9... | collective-permute-start | bytes 393224 | tf_op jit(solution)/shard_map/ppermute | solution.py:214
  2271.3 42.5 %collective-permute-start.183 = (f32[512,512]{1,0:T(8,128)S(1)}, f32[512,512]{1,0:T(8,128)S(1)}, u32[]{:S(2)}, u32[]{:S(2)}) collective-permute-start(f32[512,512]{1,0:T(8,128)S(1)} %get-tuple-element.214.cur_in), channel_id=1, source_target_pairs={{88,96},{89,97},{90,98},{91,99},{92,100},{93,101},{94,102},{95,103... | collective-permute-start | bytes 3145736 | tf_op jit(solution)/shard_map/ppermute | solution.py:226
  2399.4 63.5 %collective-permute-start.200 = (f32[512,512]{1,0:T(8,128)S(1)}, f32[512,512]{1,0:T(8,128)S(1)}, u32[]{:S(2)}, u32[]{:S(2)}) collective-permute-start(f32[512,512]{1,0:T(8,128)S(1)} %get-tuple-element.224.cur_in), channel_id=1, source_target_pairs={{96,112},{97,113},{98,114},{99,115},{100,116},{101,117},{102,118},... | collective-permute-start | bytes 3145736 | tf_op jit(solution)/shard_map/ppermute | solution.py:226
  (330 other events, 5675.8 us)

commit v2 on v0

v2 whole, which is shorter than its diff:
```python
import functools

import jax
import jax.numpy as jnp
from jax import lax
from jax.experimental import pallas as pl
from jax.experimental.pallas import tpu as pltpu
from jax.sharding import PartitionSpec as P

HB = 8
PANELS = 16
B = 512
ROWS = 8
SHARE = B // ROWS
TALL = HB * SHARE
TILE = 9

SLOT_X = {1: (0, 0), 2: (1, -1), 4: (2, -2), 5: (2, 3), 6: (2, 2)}
SLOT_Y = {2: (0, 0), 3: (1, -1), 4: (1, 2)}


def split(value):
    high = value.astype(jnp.bfloat16)
    low = (value - high.astype(jnp.float32)).astype(jnp.bfloat16)
    return high, low


def dot(left, right):
    return jnp.dot(left, right, preferred_element_type=jnp.float32)


def dot3(left, right):
    return dot(left[0], right[0]) + (dot(left[0], right[1]) + dot(left[1], right[0]))


def exact_rows(onehot, value):
    high = value.astype(jnp.bfloat16)
    rest = value - high.astype(jnp.float32)
    mid = rest.astype(jnp.bfloat16)
    low = (rest - mid.astype(jnp.float32)).astype(jnp.bfloat16)
    return dot(onehot, high) + (dot(onehot, mid) + dot(onehot, low))


def invert_kernel(step, scal, factors_in, cur_in, upper_in, y_high_ref, y_low_ref, factors, cur,
                  pivot, below, y_high, y_low, high, low, other_high, other_low, result, sems):
    rows = pl.ds((step + 1) * SHARE, TALL)
    load = [
        pltpu.make_async_copy(upper_in, pivot, sems.at[0]),
        pltpu.make_async_copy(y_high_ref, y_high, sems.at[1]),
        pltpu.make_async_copy(y_low_ref, y_low, sems.at[2]),
        pltpu.make_async_copy(factors_in.at[rows], below, sems.at[3]),
    ]
    for copy in load:
        copy.start()
    for copy in load[:3]:
        copy.wait()
    chunk = 256

    def errors(index, _):
        first = pl.multiple_of(index * chunk, chunk)
        block = pl.ds(first, chunk)
        product = dot3(split(pivot[block]), (y_high[...], y_low[...]))
        row_ids = lax.broadcasted_iota(jnp.int32, (chunk, B), 0) + first
        col_ids = lax.broadcasted_iota(jnp.int32, (chunk, B), 1)
        high[block], low[block] = split(jnp.where(row_ids == col_ids, 1.0, 0.0) - product)
        return 0

    def squares(index, _):
        block = pl.ds(pl.multiple_of(index * chunk, chunk), chunk)
        other_high[block], other_low[block] = split(dot3((high[block], low[block]), (high[...], low[...])))
        base = y_high[block].astype(jnp.float32) + y_low[block].astype(jnp.float32)
        result[block] = base + dot3((y_high[block], y_low[block]), (high[...], low[...]))
        return 0

    def inverses(index, _):
        block = pl.ds(pl.multiple_of(index * chunk, chunk), chunk)
        base = result[block]
        high[block], low[block] = split(base + dot3(split(base), (other_high[...], other_low[...])))
        return 0

    def multipliers(index, _):
        block = pl.ds(pl.multiple_of(index * chunk, chunk), chunk)
        result[block] = dot3(split(below[block]), (high[...], low[...]))
        return 0

    lax.fori_loop(0, B // chunk, errors, 0)
    lax.fori_loop(0, B // chunk, squares, 0)
    lax.fori_loop(0, B // chunk, inverses, 0)
    load[3].wait()
    lax.fori_loop(0, TALL // chunk, multipliers, 0)
    store = [pltpu.make_async_copy(result, cur, sems.at[0]), pltpu.make_async_copy(result, factors.at[rows], sems.at[1])]
    for copy in store:
        copy.start()
    for copy in store:
        copy.wait()


def lag_of(step, table, panel):
    lag = jnp.int32(0)
    for distance, (amount, _) in table.items():
        if amount:
            lag = jnp.where(panel == step + distance, amount, lag)
    return lag


def update_kernel(step, slot, scal, factors_in, cur_in, upper_in, received, factors, cur, following,
                  upper, multipliers, target, high, low, sems):
    panel = scal[0]
    table = SLOT_X if slot == 0 else SLOT_Y
    source = step - lag_of(step, table, panel)
    rows = pl.ds(pl.multiple_of((source + 1) * SHARE, SHARE), TALL)
    load = [
        pltpu.make_async_copy(upper_in, upper, sems.at[0]),
        pltpu.make_async_copy(received, multipliers, sems.at[1]),
        pltpu.make_async_copy(factors_in.at[rows], target, sems.at[2]),
    ]
    for copy in load:
        copy.start()
    load[0].wait()
    high[...], low[...] = split(upper[...])
    load[1].wait()
    keep = pltpu.make_async_copy(multipliers, cur, sems.at[3])
    keep.start()
    load[2].wait()
    chunk = 256

    def subtract(index, _):
        block = pl.ds(pl.multiple_of(index * chunk, chunk), chunk)
        target[block] = target[block] - dot3(split(multipliers[block]), (high[...], low[...]))
        return 0

    lax.fori_loop(0, TALL // chunk, subtract, 0)
    store = [
        pltpu.make_async_copy(target.at[pl.ds(0, SHARE)], following, sems.at[0]),
        pltpu.make_async_copy(target, factors.at[rows], sems.at[1]),
    ]
    for copy in store:
        copy.start()
    for copy in store:
        copy.wait()
    keep.wait()


def place_kernel(scal, factors_in, upper_in, pivot_ref, *rest):
    parts, (factors, upper_out), (upper, swapped, picks, sems) = rest[:8], rest[8:10], rest[10:]
    del upper_in
    place = scal[1]
    source = scal[2]
    z = place // 2
    core = place % 2
    load = []
    for index, part in enumerate(parts):
        other = core if index < 4 else 1 - core
        offset = (2 * ((z + 4 - index % 4) % 4) + other) * SHARE
        load.append(pltpu.make_async_copy(part, upper.at[pl.ds(pl.multiple_of(offset, SHARE), SHARE)], sems.at[index]))
    load.append(pltpu.make_async_copy(pivot_ref.at[source], picks, sems.at[8]))
    for copy in load:
        copy.start()
    for copy in load:
        copy.wait()
    keep = pltpu.make_async_copy(upper, upper_out, sems.at[0])
    keep.start()
    lanes = lax.broadcasted_iota(jnp.int32, (SHARE, 128), 1)
    pick = picks[...]
    onehot = jnp.concatenate(
        [jnp.where(pick == lanes + 128 * group, 1.0, 0.0) for group in range(B // 128)], axis=1
    ).astype(jnp.bfloat16)
    swapped[...] = exact_rows(onehot, upper[...])
    at = pl.ds(pl.multiple_of(source * SHARE, SHARE), SHARE)
    store = pltpu.make_async_copy(swapped, factors.at[at], sems.at[1])
    store.start()
    store.wait()
    keep.wait()


ANY = pl.BlockSpec(memory_space=pl.ANY)
SMEM = pl.BlockSpec(memory_space=pltpu.SMEM)


def f32(*shape):
    return pltpu.VMEM(shape, jnp.float32)


def b16(*shape):
    return pltpu.VMEM(shape, jnp.bfloat16)


def like(*arrays):
    return [jax.ShapeDtypeStruct(a.shape, a.dtype) for a in arrays]


def invert(step, scal, factors, cur, upper, y_high, y_low):
    return pl.pallas_call(
        functools.partial(invert_kernel, step),
        out_shape=like(factors, cur),
        in_specs=[SMEM] + [ANY] * 5,
        out_specs=[ANY] * 2,
        scratch_shapes=[f32(B, B), f32(TALL, B)] + [b16(B, B)] * 6 + [f32(B, B), pltpu.SemaphoreType.DMA((4,))],
        input_output_aliases={1: 0, 2: 1},
        compiler_params=pltpu.CompilerParams(vmem_limit_bytes=48 << 20),
    )(scal, factors, cur, upper, y_high, y_low)


def update(step, slot, scal, factors, cur, upper, received):
    return pl.pallas_call(
        functools.partial(update_kernel, step, slot),
        out_shape=like(factors, cur) + [jax.ShapeDtypeStruct((SHARE, B), jnp.float32)],
        in_specs=[SMEM] + [ANY] * 4,
        out_specs=[ANY] * 3,
        scratch_shapes=[f32(B, B), f32(TALL, B), f32(TALL, B), b16(B, B), b16(B, B), pltpu.SemaphoreType.DMA((4,))],
        input_output_aliases={1: 0, 2: 1},
        compiler_params=pltpu.CompilerParams(vmem_limit_bytes=48 << 20),
    )(scal, factors, cur, upper, received)


def put_in_place(scal, factors, upper, picks, parts):
    return pl.pallas_call(
        place_kernel,
        out_shape=like(factors, upper),
        in_specs=[SMEM] + [ANY] * 11,
        out_specs=[ANY] * 2,
        scratch_shapes=[f32(B, B), f32(SHARE, B), pltpu.VMEM((SHARE, 128), jnp.int32), pltpu.SemaphoreType.DMA((9,))],
        input_output_aliases={1: 0, 2: 1},
        compiler_params=pltpu.CompilerParams(vmem_limit_bytes=48 << 20),
    )(scal, factors, upper, picks, *parts)


def gather(share):
    turned = [share] + [
        lax.ppermute(share, "row", [(r, (r + 2 * turn) % ROWS) for r in range(ROWS)]) for turn in (1, 2, 3)
    ]
    return turned + [lax.ppermute(part, "row", [(r, r ^ 1) for r in range(ROWS)]) for part in turned]


def send(cur, step, table):
    first = step % TILE - TILE
    pairs = []
    for at in range(first, PANELS + TILE, TILE):
        for distance, (_, sender) in table.items():
            if at + sender in range(PANELS) and at + distance in range(PANELS):
                pairs += [((at + sender) * ROWS + r, (at + distance) * ROWS + r) for r in range(ROWS)]
    return lax.ppermute(cur, ("col", "row"), pairs)


def members(step, table):
    takers = [step + d for d, (lag, _) in table.items() if step - lag >= 0 and step + d < PANELS]
    inside = set(takers)
    grown = True
    while grown:
        grown = False
        for distance, (_, sender) in table.items():
            pair = {step + sender, step + distance}
            if pair <= set(range(PANELS)) and pair & inside and not pair <= inside:
                inside |= pair
                grown = True
    return takers, sorted(inside)


def among(panel, panels):
    hit = panel == panels[0]
    for other in panels[1:]:
        hit = hit | (panel == other)
    return hit


def local(matrix, pivots, seeds):
    panel = lax.axis_index("col").astype(jnp.int32)
    place = lax.axis_index("row").astype(jnp.int32)
    factors = matrix.reshape(-1, B)
    own_pivots = lax.dynamic_index_in_dim(pivots, panel, 0, keepdims=False)
    onehot = (own_pivots[:, None] == jnp.arange(B, dtype=jnp.int32)[None, :]).astype(jnp.float32)
    start = jnp.dot(seeds[0], onehot, precision=lax.Precision.HIGHEST, preferred_element_type=jnp.float32)
    y_high, y_low = split(start)
    picks = jnp.broadcast_to(
        lax.dynamic_slice_in_dim(pivots, place * SHARE, SHARE, 1)[:, :, None], (PANELS, SHARE, 128)
    )
    first = jnp.maximum(panel - HB, 0)
    following = lax.dynamic_slice_in_dim(factors, first * SHARE, SHARE, 0)
    cur = jnp.zeros((TALL, B), jnp.float32)
    upper = jnp.zeros((B, B), jnp.float32)
    factors, upper = put_in_place(jnp.stack([panel, place, first]), factors, upper, picks, gather(following))

    def slot(step, index, factors, cur, upper):
        table = (SLOT_X, SLOT_Y)[index]
        takers, inside = members(step, table)
        if not takers:
            return factors, cur, upper

        def exchange(factors, cur, upper):
            received = send(cur, step, table)

            def take(factors, cur, upper, received):
                new_factors, new_cur, following = update(
                    step, index, jnp.stack([panel, place]), factors, cur, upper, received
                )
                at = jnp.stack([panel, place, step + 1 - lag_of(step, table, panel)])
                new_factors, new_upper = put_in_place(at, new_factors, upper, picks, gather(following))
                return new_factors, new_cur, new_upper

            return lax.cond(
                among(panel, takers), take, lambda factors, cur, upper, received: (factors, cur, upper),
                factors, cur, upper, received,
            )

        return lax.cond(among(panel, inside), exchange, lambda *state: state, factors, cur, upper)

    for step in range(PANELS):
        factors, cur = lax.cond(
            panel == step,
            lambda factors, cur, upper: tuple(invert(step, jnp.stack([panel, place]), factors, cur, upper, y_high, y_low)),
            lambda factors, cur, upper: (factors, cur),
            factors, cur, upper,
        )
        factors, cur, upper = slot(step, 0, factors, cur, upper)
        factors, cur, upper = slot(step, 1, factors, cur, upper)
    at = (panel + 1) * SHARE
    own = lax.dynamic_slice_in_dim(factors, at, TALL, 0)
    own = lax.dot_general(
        own, onehot, (((1,), (1,)), ((), ())), precision=lax.Precision.HIGHEST, preferred_element_type=jnp.float32
    )
    factors = lax.dynamic_update_slice_in_dim(factors, own, at, 0)
    return factors.reshape(matrix.shape)


def solution(mesh):
    return jax.shard_map(
        local,
        mesh=mesh,
        in_specs=(P(None, "row", "col"), P(), P("col", None, None)),
        out_specs=P(None, "row", "col"),
        check_vma=False,
    )
```

time: 2150 us -> 1260 us (0.59)
  waiting for transfers between devices: 1730 us -> 984 us
  local copies, waits for them, and re-layouts: 153 us -> 18.6 us
  Pallas kernels: 0 us -> 74.7 us
  other arithmetic: 70.7 us -> 1.36 us
  loops' own time: 1.4 us -> 65.1 us
  matrix products: 64.5 us -> 4.25 us
    psum x16 -> x0, waiting for transfers between devices: 1520 us -> none  [from_root(): return lax.psum(block, axis)]
    ppermute x0 -> x71, waiting for transfers between devices: none -> 984 us  [the longest x8 969 us: send(): return lax.ppermute(cur, ('col', 'row'), pairs)]
    all_to_all x16 -> x0, waiting for transfers between devices: 212 us -> none  [sent_to_all(): lax.all_to_all(jnp.broadcast_to(array[None], (length, *array.shape)), axi...]
    all_to_all x16 -> x0, starting transfers between devices: 106 us -> none  [sent_to_all(): lax.all_to_all(jnp.broadcast_to(array[None], (length, *array.shape)), axi...]
    ppermute x0 -> x71, starting transfers between devices: none -> 99.8 us  [the longest x36 57.2 us: gather(): lax.ppermute(part, 'row', [(r, r ^ 1) for r in range(ROWS)])]
    pallas_call x0 -> x18, Pallas kernels: none -> 74.7 us  [the longest x8 37.5 us: update(): pl.pallas_call(functools.partial(update_kernel, step, slot), out_shape=li...]
    another operation x33 -> x53, loops' own time: 1.4 us -> 65.1 us  [the longest x29 63.7 us: slot(): lax.cond(among(panel, inside), exchange, lambda *state: state, factors, c...]
    dot_general x21 -> x2, matrix products: 64.5 us -> 4.25 us  [the longest x1 2.14 us: local(): lax.dot_general(own, onehot, (((1,), (1,)), ((), ())), precision=lax.Prec...]
  transfers between devices with their start and end apart: 32 -> 71, of which waited for: 32 -> 33; matrix products, arithmetic and copies ran while one was open for 1% -> 0% of each run, Pallas kernels for 0% -> 0%
where the time goes in v2:
time: 1260 us; the launch traced here: 1250 us
  waiting for transfers between devices  984 us (78%)
  starting transfers between devices  99.8 us (8%)
  Pallas kernels  74.7 us (6%)
  loops' own time  65.1 us (5%)
  local copies, waits for them, and re-layouts  18.6 us (1%)
    ppermute x8, waiting for transfers between devices, send(): return lax.ppermute(cur, ('col', 'row'), pairs)  969 us
    another operation x29, loops' own time, slot(): lax.cond(among(panel, inside), exchange, lambda *state: state, factors, c...  63.7 us
    ppermute x36, starting transfers between devices, gather(): lax.ppermute(part, 'row', [(r, r ^ 1) for r in range(ROWS)])  57.2 us
    pallas_call x8, Pallas kernels, update(): pl.pallas_call(functools.partial(update_kernel, step, slot), out_shape=li...  37.5 us
    ppermute x27, starting transfers between devices, gather(): lax.ppermute(share, 'row', [(r, (r + 2 * turn) % ROWS) for r in range(ROW...  32.3 us
    pallas_call x9, Pallas kernels, put_in_place(): pl.pallas_call(place_kernel, out_shape=like(factors, upper), in_specs=[SM...  29.6 us
  transfers between devices with their start and end apart: 71, of which 33 were waited for; matrix products, arithmetic and copies ran while one was open for 0% of the time, Pallas kernels for 0%

profile of v2, /device:TPU:31, one launch (start us, length us, event | category | flops | bytes accessed | tf_op | source)
XLA Modules:
  0.0 1248.7 jit_solution(3397612275008660324)
XLA Ops:
  74.7 736.1 %conditional.102 = ((f32[1536,512]{1,0:T(8,128)}, f32[512,512]{1,0:T(8,128)}, f32[512,512]{1,0:T(8,128)S(1)})) conditional(s32[]{:T(128)} %convert_element_type.248, (f32[1536,512]{1,0:T(8,128)}, f32[512,512]{1,0:T(8,128)}, f32[512,512]{1,0:T(8,128)S(1)}) %tuple.521, (s32[]{:T(128)}, f32[512,512]{1,0:T(8,128)}, f32[1536,512]{1,0:T(8,128)}, ...), branch_computations={%region_92.93_spmd, %region_93.96_spmd} | conditional | flops 27 | bytes 7864954 | solution.py:305
  76.0 714.8 %collective-permute-done.151 = f32[512,512]{1,0:T(8,128)S(1)} collective-permute-done((f32[512,512]{1,0:T(8,128)}, f32[512,512]{1,0:T(8,128)S(1)}, u32[]{:S(2)}, u32[]{:S(2)}) %collective-permute-start.151) | collective-permute-done | bytes 1048608 | tf_op jit(solution)/shard_map/cond/branch_1_fun/ppermute | solution.py:242
  790.9 19.9 %conditional.18 = ((f32[1536,512]{1,0:T(8,128)}, f32[512,512]{1,0:T(8,128)}, f32[512,512]{1,0:T(8,128)S(1)})) conditional(s32[]{:T(128)} %convert_element_type.173, (f32[1536,512]{1,0:T(8,128)}, f32[512,512]{1,0:T(8,128)}, f32[512,512]{1,0:T(8,128)S(1)}) %tuple.367, (s32[]{:T(128)}, s32[]{:T(128)}, f32[1536,512]{1,0:T(8,128)}, ...), branch_computations={%region_94.94_spmd, %region_95.95_spmd} | conditional | flops 17 | bytes 3670468 | solution.py:300
  811.1 95.4 %conditional.105 = ((f32[1536,512]{1,0:T(8,128)}, f32[512,512]{1,0:T(8,128)}, f32[512,512]{1,0:T(8,128)S(1)})) conditional(s32[]{:T(128)} %convert_element_type.245, (f32[1536,512]{1,0:T(8,128)}, f32[512,512]{1,0:T(8,128)}, f32[512,512]{1,0:T(8,128)S(1)}) %tuple.526, (s32[]{:T(128)}, f32[512,512]{1,0:T(8,128)}, f32[1536,512]{1,0:T(8,128)}, ...), branch_computations={%region_102.103_spmd, %region_103.106_spmd} | conditional | flops 25 | bytes 7864942 | solution.py:305
  812.4 74.1 %collective-permute-done.167 = f32[512,512]{1,0:T(8,128)S(1)} collective-permute-done((f32[512,512]{1,0:T(8,128)}, f32[512,512]{1,0:T(8,128)S(1)}, u32[]{:S(2)}, u32[]{:S(2)}) %collective-permute-start.167) | collective-permute-done | bytes 1048608 | tf_op jit(solution)/shard_map/cond/branch_1_fun/ppermute | solution.py:242
  886.5 20.0 %conditional.20 = ((f32[1536,512]{1,0:T(8,128)}, f32[512,512]{1,0:T(8,128)}, f32[512,512]{1,0:T(8,128)S(1)})) conditional(s32[]{:T(128)} %convert_element_type.175, (f32[1536,512]{1,0:T(8,128)}, f32[512,512]{1,0:T(8,128)}, f32[512,512]{1,0:T(8,128)S(1)}) %tuple.373, (s32[]{:T(128)}, s32[]{:T(128)}, f32[1536,512]{1,0:T(8,128)}, ...), branch_computations={%region_104.104_spmd, %region_105.105_spmd} | conditional | flops 17 | bytes 3670468 | solution.py:300
  906.5 57.5 %conditional.108 = ((f32[1536,512]{1,0:T(8,128)}, f32[512,512]{1,0:T(8,128)}, f32[512,512]{1,0:T(8,128)S(1)})) conditional(s32[]{:T(128)} %convert_element_type.242, (f32[1536,512]{1,0:T(8,128)}, f32[512,512]{1,0:T(8,128)}, f32[512,512]{1,0:T(8,128)S(1)}) %tuple.531, (s32[]{:T(128)}, f32[512,512]{1,0:T(8,128)}, f32[1536,512]{1,0:T(8,128)}, ...), branch_computations={%region_112.113_spmd, %region_113.116_spmd} | conditional | flops 23 | bytes 7864930 | solution.py:305
  907.8 26.7 %collective-permute-done.183 = f32[512,512]{1,0:T(8,128)S(1)} collective-permute-done((f32[512,512]{1,0:T(8,128)}, f32[512,512]{1,0:T(8,128)S(1)}, u32[]{:S(2)}, u32[]{:S(2)}) %collective-permute-start.183) | collective-permute-done | bytes 1048608 | tf_op jit(solution)/shard_map/cond/branch_1_fun/ppermute | solution.py:242
  934.5 20.8 %conditional.22 = ((f32[1536,512]{1,0:T(8,128)}, f32[512,512]{1,0:T(8,128)}, f32[512,512]{1,0:T(8,128)S(1)})) conditional(s32[]{:T(128)} %convert_element_type.177, (f32[1536,512]{1,0:T(8,128)}, f32[512,512]{1,0:T(8,128)}, f32[512,512]{1,0:T(8,128)S(1)}) %tuple.379, (s32[]{:T(128)}, s32[]{:T(128)}, f32[1536,512]{1,0:T(8,128)}, ...), branch_computations={%region_114.114_spmd, %region_115.115_spmd} | conditional | flops 17 | bytes 3670468 | solution.py:300
  964.0 70.2 %conditional.109 = ((f32[1536,512]{1,0:T(8,128)}, f32[512,512]{1,0:T(8,128)}, f32[512,512]{1,0:T(8,128)S(1)})) conditional(s32[]{:T(128)} %convert_element_type.241, (f32[1536,512]{1,0:T(8,128)}, f32[512,512]{1,0:T(8,128)}, f32[512,512]{1,0:T(8,128)S(1)}) %get-tuple-element.2868, (s32[]{:T(128)}, f32[512,512]{1,0:T(8,128)}, ...), branch_computations={%region_116.117_spmd, %region_117.120_spmd} | conditional | flops 19 | bytes 7864886 | solution.py:305
  965.3 49.1 %collective-permute-done.191 = f32[512,512]{1,0:T(8,128)S(1)} collective-permute-done((f32[512,512]{1,0:T(8,128)}, f32[512,512]{1,0:T(8,128)S(1)}, u32[]{:S(2)}, u32[]{:S(2)}) %collective-permute-start.191) | collective-permute-done | bytes 1048608 | tf_op jit(solution)/shard_map/cond/branch_1_fun/ppermute | solution.py:242
  1014.4 19.7 %conditional.23 = ((f32[1536,512]{1,0:T(8,128)}, f32[512,512]{1,0:T(8,128)}, f32[512,512]{1,0:T(8,128)S(1)})) conditional(s32[]{:T(128)} %convert_element_type.178, (f32[1536,512]{1,0:T(8,128)}, f32[512,512]{1,0:T(8,128)}, f32[512,512]{1,0:T(8,128)S(1)}) %tuple.382, (s32[]{:T(128)}, s32[]{:T(128)}, f32[1536,512]{1,0:T(8,128)}, ...), branch_computations={%region_118.118_spmd, %region_119.119_spmd} | conditional | flops 13 | bytes 3670424 | solution.py:300
  1034.2 47.2 %conditional.112 = ((f32[1536,512]{1,0:T(8,128)}, f32[512,512]{1,0:T(8,128)}, f32[512,512]{1,0:T(8,128)S(1)})) conditional(s32[]{:T(128)} %convert_element_type.238, (f32[1536,512]{1,0:T(8,128)}, f32[512,512]{1,0:T(8,128)}, f32[512,512]{1,0:T(8,128)S(1)}) %get-tuple-element.2871, (s32[]{:T(128)}, f32[512,512]{1,0:T(8,128)}, ...), branch_computations={%region_126.127_spmd, %region_127.130_spmd} | conditional | flops 17 | bytes 7864874 | solution.py:305
  1035.5 25.8 %collective-permute-done.207 = f32[512,512]{1,0:T(8,128)S(1)} collective-permute-done((f32[512,512]{1,0:T(8,128)}, f32[512,512]{1,0:T(8,128)S(1)}, u32[]{:S(2)}, u32[]{:S(2)}) %collective-permute-start.207) | collective-permute-done | bytes 1048608 | tf_op jit(solution)/shard_map/cond/branch_1_fun/ppermute | solution.py:242
  1061.4 19.8 %conditional.25 = ((f32[1536,512]{1,0:T(8,128)}, f32[512,512]{1,0:T(8,128)}, f32[512,512]{1,0:T(8,128)S(1)})) conditional(s32[]{:T(128)} %convert_element_type.180, (f32[1536,512]{1,0:T(8,128)}, f32[512,512]{1,0:T(8,128)}, f32[512,512]{1,0:T(8,128)S(1)}) %tuple.388, (s32[]{:T(128)}, s32[]{:T(128)}, f32[1536,512]{1,0:T(8,128)}, ...), branch_computations={%region_128.128_spmd, %region_129.129_spmd} | conditional | flops 13 | bytes 3670424 | solution.py:300
  1081.4 48.0 %conditional.114 = ((f32[1536,512]{1,0:T(8,128)}, f32[512,512]{1,0:T(8,128)}, f32[512,512]{1,0:T(8,128)S(1)})) conditional(s32[]{:T(128)} %convert_element_type.236, (f32[1536,512]{1,0:T(8,128)}, f32[512,512]{1,0:T(8,128)}, f32[512,512]{1,0:T(8,128)S(1)}) %tuple.541, (s32[]{:T(128)}, f32[512,512]{1,0:T(8,128)}, f32[1536,512]{1,0:T(8,128)}, ...), branch_computations={%region_132.133_spmd, %region_133.136_spmd} | conditional | flops 21 | bytes 7864918 | solution.py:305
  1082.8 26.7 %collective-permute-done.215 = f32[512,512]{1,0:T(8,128)S(1)} collective-permute-done((f32[512,512]{1,0:T(8,128)}, f32[512,512]{1,0:T(8,128)S(1)}, u32[]{:S(2)}, u32[]{:S(2)}) %collective-permute-start.215) | collective-permute-done | bytes 1048608 | tf_op jit(solution)/shard_map/cond/branch_1_fun/ppermute | solution.py:242
  1109.4 20.0 %conditional.26 = ((f32[1536,512]{1,0:T(8,128)}, f32[512,512]{1,0:T(8,128)}, f32[512,512]{1,0:T(8,128)S(1)})) conditional(s32[]{:T(128)} %convert_element_type.181, (f32[1536,512]{1,0:T(8,128)}, f32[512,512]{1,0:T(8,128)}, f32[512,512]{1,0:T(8,128)S(1)}) %tuple.391, (s32[]{:T(128)}, s32[]{:T(128)}, f32[1536,512]{1,0:T(8,128)}, ...), branch_computations={%region_134.134_spmd, %region_135.135_spmd} | conditional | flops 17 | bytes 3670468 | solution.py:300
  1129.5 47.7 %conditional.115 = ((f32[1536,512]{1,0:T(8,128)}, f32[512,512]{1,0:T(8,128)}, f32[512,512]{1,0:T(8,128)S(1)})) conditional(s32[]{:T(128)} %convert_element_type.235, (f32[1536,512]{1,0:T(8,128)}, f32[512,512]{1,0:T(8,128)}, f32[512,512]{1,0:T(8,128)S(1)}) %get-tuple-element.2874, (s32[]{:T(128)}, f32[512,512]{1,0:T(8,128)}, ...), branch_computations={%region_136.137_spmd, %region_137.140_spmd} | conditional | flops 15 | bytes 7864862 | solution.py:305
  1130.8 26.8 %collective-permute-done.223 = f32[512,512]{1,0:T(8,128)S(1)} collective-permute-done((f32[512,512]{1,0:T(8,128)}, f32[512,512]{1,0:T(8,128)S(1)}, u32[]{:S(2)}, u32[]{:S(2)}) %collective-permute-start.223) | collective-permute-done | bytes 1048608 | tf_op jit(solution)/shard_map/cond/branch_1_fun/ppermute | solution.py:242
  1157.5 19.6 %conditional.27 = ((f32[1536,512]{1,0:T(8,128)}, f32[512,512]{1,0:T(8,128)}, f32[512,512]{1,0:T(8,128)S(1)})) conditional(s32[]{:T(128)} %convert_element_type.182, (f32[1536,512]{1,0:T(8,128)}, f32[512,512]{1,0:T(8,128)}, f32[512,512]{1,0:T(8,128)S(1)}) %tuple.394, (s32[]{:T(128)}, s32[]{:T(128)}, f32[1536,512]{1,0:T(8,128)}, ...), branch_computations={%region_138.138_spmd, %region_139.139_spmd} | conditional | flops 13 | bytes 3670424 | solution.py:300
  1177.2 54.5 %conditional.117 = ((f32[1536,512]{1,0:T(8,128)}, f32[512,512]{1,0:T(8,128)}, f32[512,512]{1,0:T(8,128)S(1)}, f32[1536,512]{1,0:T(8,128)})) conditional(s32[]{:T(128)} %convert_element_type.233, (f32[1536,512]{1,0:T(8,128)}, f32[512,512]{1,0:T(8,128)}, f32[512,512]{1,0:T(8,128)S(1)}) %tuple.546, (s32[]{:T(128)}, f32[512,512]{1,0:T(8,128)}, ...), branch_computations={%region_142.143_spmd, %region_143.146_spmd} | conditional | flops 19 | bytes 14156370 | solution.py:305
  1178.5 25.2 %collective-permute-done.231 = f32[512,512]{1,0:T(8,128)S(1)} collective-permute-done((f32[512,512]{1,0:T(8,128)}, f32[512,512]{1,0:T(8,128)S(1)}, u32[]{:S(2)}, u32[]{:S(2)}) %collective-permute-start.231) | collective-permute-done | bytes 1048608 | tf_op jit(solution)/shard_map/cond/branch_1_fun/ppermute | solution.py:242
  1203.7 24.6 %conditional.28 = (f32[1536,512]{1,0:T(8,128)}, f32[512,512]{1,0:T(8,128)}, f32[512,512]{1,0:T(8,128)S(1)}, f32[1536,512]{1,0:T(8,128)}) conditional(s32[]{:T(128)} %convert_element_type.183, (f32[1536,512]{1,0:T(8,128)}, f32[512,512]{1,0:T(8,128)}, f32[512,512]{1,0:T(8,128)S(1)}) %tuple.399, (s32[]{:T(128)}, s32[]{:T(128)}, ...), branch_computations={%region_144.144_spmd, %region_145.145_spmd} | conditional | flops 17 | bytes 9961924 | solution.py:300
  (225 shorter events, 278.7 us)
Async XLA Ops:
  5.1 10.1 collective-permute-start.232
  6.8 9.0 collective-permute-start.233
  10.8 7.7 collective-permute-start.235
  74.7 716.2 %collective-permute-start.151 = (f32[512,512]{1,0:T(8,128)}, f32[512,512]{1,0:T(8,128)S(1)}, u32[]{:S(2)}, u32[]{:S(2)}) collective-permute-start(f32[512,512]{1,0:T(8,128)} %get-tuple-element.1808), channel_id=1, source_target_pairs={{0,8},{1,9},{2,10},{3,11},{4,12},{5,13},{6,14},{7,15},{24,40},{25,... | collective-permute-start | bytes 3145736 | tf_op jit(solution)/shard_map/cond/branch_1_fun/ppermute | solution.py:242
  795.7 8.6 collective-permute-start.145
  811.1 75.4 %collective-permute-start.167 = (f32[512,512]{1,0:T(8,128)}, f32[512,512]{1,0:T(8,128)S(1)}, u32[]{:S(2)}, u32[]{:S(2)}) collective-permute-start(f32[512,512]{1,0:T(8,128)} %get-tuple-element.1851), channel_id=1, source_target_pairs={{8,16},{9,17},{10,18},{11,19},{12,20},{13,21},{14,22},{15,23},{0,2... | collective-permute-start | bytes 3145736 | tf_op jit(solution)/shard_map/cond/branch_1_fun/ppermute | solution.py:242
  891.4 8.7 collective-permute-start.161
  906.5 28.0 %collective-permute-start.183 = (f32[512,512]{1,0:T(8,128)}, f32[512,512]{1,0:T(8,128)S(1)}, u32[]{:S(2)}, u32[]{:S(2)}) collective-permute-start(f32[512,512]{1,0:T(8,128)} %get-tuple-element.1894), channel_id=1, source_target_pairs={{16,24},{17,25},{18,26},{19,27},{20,28},{21,29},{22,30},{23,31},{8... | collective-permute-start | bytes 3145736 | tf_op jit(solution)/shard_map/cond/branch_1_fun/ppermute | solution.py:242
  939.6 9.1 collective-permute-start.177
  942.8 7.8 collective-permute-start.179
  964.0 50.5 %collective-permute-start.191 = (f32[512,512]{1,0:T(8,128)}, f32[512,512]{1,0:T(8,128)S(1)}, u32[]{:S(2)}, u32[]{:S(2)}) collective-permute-start(f32[512,512]{1,0:T(8,128)} %get-tuple-element.1912), channel_id=1, source_target_pairs={{16,32},{17,33},{18,34},{19,35},{20,36},{21,37},{22,38},{23,39},{8... | collective-permute-start | bytes 3145736 | tf_op jit(solution)/shard_map/cond/branch_1_fun/ppermute | solution.py:242
  1019.4 8.3 collective-permute-start.185
  1022.1 7.8 collective-permute-start.187
  1034.2 27.2 %collective-permute-start.207 = (f32[512,512]{1,0:T(8,128)}, f32[512,512]{1,0:T(8,128)S(1)}, u32[]{:S(2)}, u32[]{:S(2)}) collective-permute-start(f32[512,512]{1,0:T(8,128)} %get-tuple-element.1955), channel_id=1, source_target_pairs={{24,40},{25,41},{26,42},{27,43},{28,44},{29,45},{30,46},{31,47},{1... | collective-permute-start | bytes 3145736 | tf_op jit(solution)/shard_map/cond/branch_1_fun/ppermute | solution.py:242
  1066.2 9.9 collective-permute-start.201
  1068.5 7.6 collective-permute-start.202
  1068.9 8.1 collective-permute-start.203
  1081.5 28.0 %collective-permute-start.215 = (f32[512,512]{1,0:T(8,128)}, f32[512,512]{1,0:T(8,128)S(1)}, u32[]{:S(2)}, u32[]{:S(2)}) collective-permute-start(f32[512,512]{1,0:T(8,128)} %get-tuple-element.1980), channel_id=1, source_target_pairs={{32,40},{33,41},{34,42},{35,43},{36,44},{37,45},{38,46},{39,47},{2... | collective-permute-start | bytes 3145736 | tf_op jit(solution)/shard_map/cond/branch_1_fun/ppermute | solution.py:242
  1114.3 8.9 collective-permute-start.209
  1129.5 28.1 %collective-permute-start.223 = (f32[512,512]{1,0:T(8,128)}, f32[512,512]{1,0:T(8,128)S(1)}, u32[]{:S(2)}, u32[]{:S(2)}) collective-permute-start(f32[512,512]{1,0:T(8,128)} %get-tuple-element.1998), channel_id=1, source_target_pairs={{32,48},{33,49},{34,50},{35,51},{36,52},{37,53},{38,54},{39,55},{2... | collective-permute-start | bytes 3145736 | tf_op jit(solution)/shard_map/cond/branch_1_fun/ppermute | solution.py:242
  1162.4 8.7 collective-permute-start.217
  1165.5 7.4 collective-permute-start.219
  1177.2 26.5 %collective-permute-start.231 = (f32[512,512]{1,0:T(8,128)}, f32[512,512]{1,0:T(8,128)S(1)}, u32[]{:S(2)}, u32[]{:S(2)}) collective-permute-start(f32[512,512]{1,0:T(8,128)} %get-tuple-element.2029), channel_id=1, source_target_pairs={{40,48},{41,49},{42,50},{43,51},{44,52},{45,53},{46,54},{47,55},{3... | collective-permute-start | bytes 3145736 | tf_op jit(solution)/shard_map/cond/branch_1_fun/ppermute | solution.py:242
  1209.1 8.0 collective-permute-start.225
  (49 other events, 230.0 us)

commit v3 on v2

v3 whole, which is shorter than its diff:
```python
import functools

import jax
import jax.numpy as jnp
from jax import lax
from jax.experimental import pallas as pl
from jax.experimental.pallas import tpu as pltpu
from jax.sharding import PartitionSpec as P

HB = 8
PANELS = 16
B = 512
ROWS = 8
SHARE = B // ROWS
TALL = HB * SHARE
TILE = 9

NEAR = {1: (0, 0), 2: (1, -1), 3: (2, -2), 4: (2, 2)}
FAR = {2: (0, 0), 3: (1, -1), 5: (2, -2), 6: (2, 2)}


def split(value):
    high = value.astype(jnp.bfloat16)
    low = (value - high.astype(jnp.float32)).astype(jnp.bfloat16)
    return high, low


def dot(left, right):
    return jnp.dot(left, right, preferred_element_type=jnp.float32)


def dot3(left, right):
    return dot(left[0], right[0]) + (dot(left[0], right[1]) + dot(left[1], right[0]))


def exact_rows(onehot, value):
    high = value.astype(jnp.bfloat16)
    rest = value - high.astype(jnp.float32)
    mid = rest.astype(jnp.bfloat16)
    low = (rest - mid.astype(jnp.float32)).astype(jnp.bfloat16)
    return dot(onehot, high) + (dot(onehot, mid) + dot(onehot, low))


def split_into(value, high, low):
    def rows(index, _):
        block = pl.ds(pl.multiple_of(index * SHARE, SHARE), SHARE)
        high[block], low[block] = split(value[block])
        return 0

    lax.fori_loop(0, B // SHARE, rows, 0)


def halves_kernel(value_ref, high_ref, low_ref, value, high, low, sems):
    load = pltpu.make_async_copy(value_ref, value, sems.at[0])
    load.start()
    load.wait()
    split_into(value, high, low)
    store = [pltpu.make_async_copy(high, high_ref, sems.at[0]), pltpu.make_async_copy(low, low_ref, sems.at[1])]
    for copy in store:
        copy.start()
    for copy in store:
        copy.wait()


def inverse_kernel(pivot_ref, y_high_ref, y_low_ref, high_ref, low_ref,
                   pivot, y_high, y_low, high, low, other_high, other_low, result, sems):
    load = [
        pltpu.make_async_copy(pivot_ref, pivot, sems.at[0]),
        pltpu.make_async_copy(y_high_ref, y_high, sems.at[1]),
        pltpu.make_async_copy(y_low_ref, y_low, sems.at[2]),
    ]
    for copy in load:
        copy.start()
    for copy in load:
        copy.wait()
    chunk = 128

    def errors(index, _):
        first = pl.multiple_of(index * chunk, chunk)
        block = pl.ds(first, chunk)
        product = dot3(split(pivot[block]), (y_high[...], y_low[...]))
        row_ids = lax.broadcasted_iota(jnp.int32, (chunk, B), 0) + first
        col_ids = lax.broadcasted_iota(jnp.int32, (chunk, B), 1)
        high[block], low[block] = split(jnp.where(row_ids == col_ids, 1.0, 0.0) - product)
        return 0

    def squares(index, _):
        block = pl.ds(pl.multiple_of(index * chunk, chunk), chunk)
        other_high[block], other_low[block] = split(dot3((high[block], low[block]), (high[...], low[...])))
        base = y_high[block].astype(jnp.float32) + y_low[block].astype(jnp.float32)
        result[block] = base + dot3((y_high[block], y_low[block]), (high[...], low[...]))
        return 0

    def inverses(index, _):
        block = pl.ds(pl.multiple_of(index * chunk, chunk), chunk)
        base = result[block]
        high[block], low[block] = split(base + dot3(split(base), (other_high[...], other_low[...])))
        return 0

    lax.fori_loop(0, B // chunk, errors, 0)
    lax.fori_loop(0, B // chunk, squares, 0)
    lax.fori_loop(0, B // chunk, inverses, 0)
    store = [pltpu.make_async_copy(high, high_ref, sems.at[0]), pltpu.make_async_copy(low, low_ref, sems.at[1])]
    for copy in store:
        copy.start()
    for copy in store:
        copy.wait()


def multiply_kernel(owner, factors_in, cur_in, upper_in, received, high_ref, low_ref, factors, cur, front,
                    upper, multipliers, below, high, low, upper_high, upper_low, sems):
    rows = pl.ds((owner + 1) * SHARE, TALL)
    load = [
        pltpu.make_async_copy(factors_in.at[rows], below, sems.at[0]),
        pltpu.make_async_copy(high_ref, high, sems.at[1]),
        pltpu.make_async_copy(low_ref, low, sems.at[2]),
    ]
    if owner:
        load += [
            pltpu.make_async_copy(upper_in, upper, sems.at[3]),
            pltpu.make_async_copy(received, multipliers, sems.at[4]),
        ]
    for copy in load:
        copy.start()
    if owner:
        load[3].wait()
        split_into(upper, upper_high, upper_low)
    for copy in load[:3] + load[4:]:
        copy.wait()
    if owner:
        chunk = (TALL - SHARE) // 2

        def subtract(index, _):
            first = pl.multiple_of(index * chunk, 32)
            block = pl.ds(first, chunk)
            shifted = pl.ds(pl.multiple_of(first + SHARE, 32), chunk)
            below[block] = below[block] - dot3(split(multipliers[shifted]), (upper_high[...], upper_low[...]))
            return 0

        lax.fori_loop(0, 2, subtract, 0)
    part = 128

    def multiply(index, _):
        block = pl.ds(pl.multiple_of(index * part, part), part)
        below[block] = dot3(split(below[block]), (high[...], low[...]))
        return 0

    lax.fori_loop(0, TALL // part, multiply, 0)
    store = [
        pltpu.make_async_copy(below.at[pl.ds(0, SHARE)], front, sems.at[0]),
        pltpu.make_async_copy(below, cur, sems.at[1]),
        pltpu.make_async_copy(below, factors.at[rows], sems.at[2]),
    ]
    for copy in store:
        copy.start()
    for copy in store:
        copy.wait()


def front_kernel(step, factors_in, upper_in, received, following, upper, multipliers, target, high, low, sems):
    rows = pl.ds((step + 1) * SHARE, SHARE)
    load = [
        pltpu.make_async_copy(upper_in, upper, sems.at[0]),
        pltpu.make_async_copy(received, multipliers, sems.at[1]),
        pltpu.make_async_copy(factors_in.at[rows], target, sems.at[2]),
    ]
    for copy in load:
        copy.start()
    for copy in load:
        copy.wait()
    left = split(multipliers[...])
    split_into(upper, high, low)
    target[...] = target[...] - dot3(left, (high[...], low[...]))
    store = pltpu.make_async_copy(target, following, sems.at[0])
    store.start()
    store.wait()


def lag_of(step, table, panel):
    lag = jnp.int32(0)
    for distance, (amount, _) in table.items():
        if amount:
            lag = jnp.where(panel == step + distance, amount, lag)
    return lag


def update_kernel(step, far, scal, factors_in, cur_in, upper_in, received, factors, cur, following,
                  upper, multipliers, target, high, low, sems):
    panel = scal[0]
    source = step - lag_of(step, FAR if far else NEAR, panel)
    rows = pl.ds(pl.multiple_of((source + 1) * SHARE, SHARE), TALL)
    load = [
        pltpu.make_async_copy(upper_in, upper, sems.at[0]),
        pltpu.make_async_copy(received, multipliers, sems.at[1]),
        pltpu.make_async_copy(factors_in.at[rows], target, sems.at[2]),
    ]
    for copy in load:
        copy.start()
    load[0].wait()
    split_into(upper, high, low)
    load[1].wait()
    if far:
        keep = pltpu.make_async_copy(multipliers, cur, sems.at[3])
        keep.start()
    load[2].wait()
    chunk = 128

    def subtract(index, _):
        block = pl.ds(pl.multiple_of(index * chunk, chunk), chunk)
        target[block] = target[block] - dot3(split(multipliers[block]), (high[...], low[...]))
        return 0

    lax.fori_loop(0, TALL // chunk, subtract, 0)
    store = [
        pltpu.make_async_copy(target.at[pl.ds(0, SHARE)], following, sems.at[0]),
        pltpu.make_async_copy(target, factors.at[rows], sems.at[1]),
    ]
    for copy in store:
        copy.start()
    for copy in store:
        copy.wait()
    if far:
        keep.wait()


def place_kernel(scal, factors_in, pivot_ref, *rest):
    parts, (factors, upper_out), (upper, swapped, picks, sems) = rest[:8], rest[8:10], rest[10:]
    place = scal[1]
    source = scal[2]
    z = place // 2
    core = place % 2
    load = []
    for index, part in enumerate(parts):
        other = core if index < 4 else 1 - core
        offset = (2 * ((z + 4 - index % 4) % 4) + other) * SHARE
        load.append(pltpu.make_async_copy(part, upper.at[pl.ds(pl.multiple_of(offset, SHARE), SHARE)], sems.at[index]))
    load.append(pltpu.make_async_copy(pivot_ref.at[source], picks, sems.at[8]))
    for copy in load:
        copy.start()
    for copy in load:
        copy.wait()
    keep = pltpu.make_async_copy(upper, upper_out, sems.at[0])
    keep.start()
    lanes = lax.broadcasted_iota(jnp.int32, (SHARE, 128), 1)
    swapped[...] = jnp.zeros_like(swapped)

    def pick_rows(group, _):
        onehot = jnp.where(picks[...] == lanes + 128 * group, 1.0, 0.0).astype(jnp.bfloat16)
        block = pl.ds(pl.multiple_of(group * 128, 128), 128)
        swapped[...] = swapped[...] + exact_rows(onehot, upper[block])
        return 0

    lax.fori_loop(0, B // 128, pick_rows, 0)
    at = pl.ds(pl.multiple_of(source * SHARE, SHARE), SHARE)
    store = pltpu.make_async_copy(swapped, factors.at[at], sems.at[1])
    store.start()
    store.wait()
    keep.wait()


ANY = pl.BlockSpec(memory_space=pl.ANY)
SMEM = pl.BlockSpec(memory_space=pltpu.SMEM)


def f32(*shape):
    return pltpu.VMEM(shape, jnp.float32)


def b16(*shape):
    return pltpu.VMEM(shape, jnp.bfloat16)


def like(*arrays):
    return [jax.ShapeDtypeStruct(a.shape, a.dtype) for a in arrays]


def call(kernel, out_shape, scratch, aliases, *operands, scal=None):
    first = [] if scal is None else [scal]
    return pl.pallas_call(
        kernel,
        out_shape=out_shape,
        in_specs=[SMEM] * len(first) + [ANY] * len(operands),
        out_specs=[ANY] * len(out_shape),
        scratch_shapes=scratch,
        input_output_aliases=aliases,
        compiler_params=pltpu.CompilerParams(vmem_limit_bytes=48 << 20),
    )(*first, *operands)


def inverse(pivot, y_high, y_low):
    scratch = [f32(B, B)] + [b16(B, B)] * 6 + [f32(B, B), pltpu.SemaphoreType.DMA((3,))]
    return call(inverse_kernel, like(y_high, y_low), scratch, {}, pivot, y_high, y_low)


def multiply(owner, factors, cur, front, upper, received, high, low):
    scratch = [f32(B, B), f32(TALL, B), f32(TALL, B)] + [b16(B, B)] * 4 + [pltpu.SemaphoreType.DMA((5,))]
    return call(functools.partial(multiply_kernel, owner), like(factors, cur, front), scratch, {0: 0, 1: 1},
                factors, cur, upper, received, high, low)


def advance(step, factors, following, upper, received):
    scratch = [f32(B, B), f32(SHARE, B), f32(SHARE, B), b16(B, B), b16(B, B), pltpu.SemaphoreType.DMA((3,))]
    return call(functools.partial(front_kernel, step), like(following), scratch, {}, factors, upper, received)[0]


def update(step, far, scal, factors, cur, following, upper, received):
    scratch = [f32(B, B), f32(TALL, B), f32(TALL, B), b16(B, B), b16(B, B), pltpu.SemaphoreType.DMA((4,))]
    outs = like(factors, cur, following) if far else like(factors, following)
    kernel = functools.partial(update_kernel if far else near_kernel, step, far)
    return call(kernel, outs, scratch, {1: 0, 2: 1} if far else {1: 0}, factors, cur, upper, received, scal=scal) if far else call(
        kernel, outs, scratch, {1: 0}, factors, upper, received, scal=scal)


def near_kernel(step, far, scal, factors_in, upper_in, received, factors, following, *scratch):
    update_kernel(step, far, scal, factors_in, None, upper_in, received, factors, None, following, *scratch)


def put_in_place(scal, factors, upper, picks, parts):
    scratch = [f32(B, B), f32(SHARE, B), pltpu.VMEM((SHARE, 128), jnp.int32), pltpu.SemaphoreType.DMA((9,))]
    return call(place_kernel, like(factors, upper), scratch, {1: 0}, factors, picks, *parts, scal=scal)


def gather(share):
    turned = [share] + [
        lax.ppermute(share, "row", [(r, (r + 2 * turn) % ROWS) for r in range(ROWS)]) for turn in (1, 2, 3)
    ]
    return turned + [lax.ppermute(part, "row", [(r, r ^ 1) for r in range(ROWS)]) for part in turned]


def send(cur, step, table):
    first = step % TILE - TILE
    pairs = []
    for at in range(first, PANELS + TILE, TILE):
        for distance, (_, sender) in table.items():
            if at + sender in range(PANELS) and at + distance in range(PANELS):
                pairs += [((at + sender) * ROWS + r, (at + distance) * ROWS + r) for r in range(ROWS)]
    return lax.ppermute(cur, ("col", "row"), pairs)


def members(step, tables):
    takers = sorted({
        step + d for table in tables for d, (lag, _) in table.items() if step - lag >= 0 and step + d < PANELS
    })
    inside = set(takers)
    grown = True
    while grown:
        grown = False
        for table in tables:
            for distance, (_, sender) in table.items():
                pair = {step + sender, step + distance}
                if pair <= set(range(PANELS)) and pair & inside and not pair <= inside:
                    inside |= pair
                    grown = True
    return takers, sorted(inside)


def shifted(odd):
    return [(c * ROWS + r, (c + 1) * ROWS + r) for c in range(odd, PANELS - 1, 2) for r in range(ROWS)]


def among(panel, panels):
    hit = panel == panels[0]
    for other in panels[1:]:
        hit = hit | (panel == other)
    return hit


def local(matrix, pivots, seeds):
    panel = lax.axis_index("col").astype(jnp.int32)
    place = lax.axis_index("row").astype(jnp.int32)
    factors = matrix.reshape(-1, B)
    own_pivots = lax.dynamic_index_in_dim(pivots, panel, 0, keepdims=False)
    onehot = (own_pivots[:, None] == jnp.arange(B, dtype=jnp.int32)[None, :]).astype(jnp.float32)
    start = jnp.dot(seeds[0], onehot, precision=lax.Precision.HIGHEST, preferred_element_type=jnp.float32)
    half = jax.ShapeDtypeStruct((B, B), jnp.bfloat16)
    y_high, y_low = call(halves_kernel, [half, half], [f32(B, B), b16(B, B), b16(B, B), pltpu.SemaphoreType.DMA((2,))], {}, start)
    picks = jnp.broadcast_to(
        lax.dynamic_slice_in_dim(pivots, place * SHARE, SHARE, 1)[:, :, None], (PANELS, SHARE, 128)
    )
    first = jnp.maximum(panel - HB, 0)
    following = lax.dynamic_slice_in_dim(factors, first * SHARE, SHARE, 0)
    cur = jnp.zeros((TALL, B), jnp.float32)
    front = jnp.zeros((SHARE, B), jnp.float32)
    where = jnp.stack([panel, place])

    def when(panels, run, *state):
        if not panels:
            return state
        return lax.cond(among(panel, panels), lambda *state: tuple(run(*state)), lambda *state: state, *state)

    def collect(source, factors, upper, following):
        return put_in_place(jnp.stack([panel, place, source]), factors, upper, picks, gather(following))

    upper = jnp.zeros((B, B), jnp.float32)

    def begin(factors, cur, front, upper):
        factors, upper = collect(panel, factors, upper, following)
        factors, cur, front = multiply(0, factors, cur, front, upper, cur, *inverse(upper, y_high, y_low))
        return factors, cur, front, upper

    factors, cur, front, upper = when([0], begin, factors, cur, front, upper)

    for step in range(PANELS - 1):
        coming = step + 1

        def prepare(factors, upper):
            return collect(step, factors, upper, following)

        factors, upper = when([coming], prepare, factors, upper)

        def lead(following):
            arrived = lax.ppermute(front, ("col", "row"), shifted(step % 2))
            return (advance(step, factors, following, upper, arrived),)

        (following,) = when([step, coming], lead, following)
        near, _ = members(step, [NEAR])
        far, _ = members(step, [FAR])
        _, inside = members(step, [NEAR, FAR])

        def exchange(factors, cur, front, upper, following):
            p = send(cur, step, NEAR)
            q = send(cur, step, FAR) if far else None
            source = jnp.where(
                panel == coming, coming, jnp.maximum(step - lag_of(step, FAR | NEAR, panel), 0)
            )

            def bring(factors, fresh):
                return collect(source, factors, upper, following)

            factors, fresh = when(sorted(set(near) | set(far)), bring, factors, upper)
            high, low = inverse(fresh, y_high, y_low)

            def near_update(factors, following):
                return update(step, False, where, factors, cur, following, fresh, p)

            factors, following = when([c for c in near if c != coming], near_update, factors, following)

            def again(factors, fresh):
                return collect(step + 1 - lag_of(step, NEAR, panel), factors, fresh, following)

            factors, fresh = when(sorted(set(near) & set(far)), again, factors, fresh)

            def far_update(factors, new_cur, following):
                return update(step, True, where, factors, new_cur, following, fresh, q)

            factors, new_cur, following = when(far, far_update, factors, cur, following)

            def own(factors, cur, front):
                return multiply(coming, factors, cur, front, upper, p, high, low)

            factors, new_cur, front = when([coming], own, factors, new_cur, front)
            return factors, new_cur, front, fresh, following

        factors, cur, front, upper, following = when(inside, exchange, factors, cur, front, upper, following)
    at = (panel + 1) * SHARE
    own = lax.dynamic_slice_in_dim(factors, at, TALL, 0)
    own = lax.dot_general(
        own, onehot, (((1,), (1,)), ((), ())), precision=lax.Precision.HIGHEST, preferred_element_type=jnp.float32
    )
    factors = lax.dynamic_update_slice_in_dim(factors, own, at, 0)
    return factors.reshape(matrix.shape)


def solution(mesh):
    return jax.shard_map(
        local,
        mesh=mesh,
        in_specs=(P(None, "row", "col"), P(), P("col", None, None)),
        out_specs=P(None, "row", "col"),
        check_vma=False,
    )
```

time: 1260 us -> 1100 us (0.87)
  waiting for transfers between devices: 984 us -> 757 us
  Pallas kernels: 74.7 us -> 121 us
  local copies, waits for them, and re-layouts: 18.6 us -> 43.5 us
  loops' own time: 65.1 us -> 41.3 us
  starting transfers between devices: 99.8 us -> 118 us
    ppermute x8 -> x11, waiting for transfers between devices: 969 us -> 739 us  [send(): return lax.ppermute(cur, ('col', 'row'), pairs)]
    pallas_call x18 -> x25, Pallas kernels: 74.7 us -> 121 us  [call(): pl.pallas_call(kernel, out_shape=out_shape, in_specs=[SMEM] * len(first)...]
    cond x2 -> x38, local copies, waits for them, and re-layouts: 7.72 us -> 33.2 us
    another operation x53 -> x73, loops' own time: 65.1 us -> 41.3 us  [when(): lax.cond(among(panel, panels), lambda *state: tuple(run(*state)), lambda...]
  transfers between devices with their start and end apart: 71 -> 75, of which waited for: 33 -> 28; matrix products, arithmetic and copies ran while one was open for 0% -> 0% of each run, Pallas kernels for 0% -> 8%
where the time goes in v3:
time: 1100 us; the launch traced here: 1080 us
  waiting for transfers between devices  757 us (69%)
  Pallas kernels  121 us (11%)
  starting transfers between devices  118 us (11%)
  local copies, waits for them, and re-layouts  43.5 us (4%)
  loops' own time  41.3 us (4%)
    ppermute x11, waiting for transfers between devices, send(): return lax.ppermute(cur, ('col', 'row'), pairs)  739 us
    pallas_call x25, Pallas kernels, call(): pl.pallas_call(kernel, out_shape=out_shape, in_specs=[SMEM] * len(first)...  121 us
    ppermute x36, starting transfers between devices, gather(): lax.ppermute(part, 'row', [(r, r ^ 1) for r in range(ROWS)])  62.8 us
    another operation x73, loops' own time, when(): lax.cond(among(panel, panels), lambda *state: tuple(run(*state)), lambda...  41.3 us
    ppermute x27, starting transfers between devices, gather(): lax.ppermute(share, 'row', [(r, (r + 2 * turn) % ROWS) for r in range(ROW...  38.1 us
    cond x38, local copies, waits for them, and re-layouts  33.2 us
  transfers between devices with their start and end apart: 75, of which 28 were waited for; matrix products, arithmetic and copies ran while one was open for 0% of the time, Pallas kernels for 8%

profile of v3, /device:TPU:31, one launch (start us, length us, event | category | flops | bytes accessed | tf_op | source)
XLA Modules:
  0.0 1084.5 jit_solution(16670894139871411936)
XLA Ops:
  15.7 9.9 conditional.123
  37.0 9.9 conditional.132
  58.4 9.9 conditional.141
  70.6 600.9 %conditional.146 = (f32[1536,512]{1,0:T(8,128)}, f32[512,512]{1,0:T(8,128)}, f32[64,512]{1,0:T(8,128)S(1)}, f32[512,512]{1,0:T(8,128)}, f32[64,512]{1,0:T(8,128)S(1)}, /*index=5*/f32[64,512]{1,0:T(8,128)S(1)}) conditional(s32[]{:T(128)} %convert_element_type.343, (f32[1536,512]{1,0:T(8,128)}, f32[512,512]{1,0:T(8,128)}, ...), branch_computations={%region_146.147_spmd, %region_147.158_spmd} | conditional | flops 47 | bytes 18089370 | solution.py:389
  72.2 17.2 %conditional.43 = ((f32[1536,512]{1,0:T(8,128)}, f32[512,512]{1,0:T(8,128)})) conditional(s32[]{:T(128)} %convert_element_type.271, (f32[1536,512]{1,0:T(8,128)}, f32[512,512]{1,0:T(8,128)}) %tuple.1091, (s32[]{:T(128)}, s32[]{:T(128)}, pred[]{:T(512)}, pred[]{:T(512)}, pred[]{:T(512)}, /*index=5*/pred[]{:T(512)}, pred[]{:T(512)}, pred[]{:T(512)}, ...), branch_computations={%region_148.148_spmd, %region_149.149_spmd} | conditional | flops 14 | bytes 3670430 | solution.py:389
  98.4 567.5 %collective-permute-done.244 = f32[512,512]{1,0:T(8,128)} collective-permute-done((f32[512,512]{1,0:T(8,128)}, f32[512,512]{1,0:T(8,128)}, u32[]{:S(2)}, u32[]{:S(2)}) %collective-permute-start.244) | collective-permute-done | bytes 1048608 | tf_op jit(solution)/shard_map/cond/branch_1_fun/ppermute | solution.py:337
  671.6 79.5 %conditional.149 = (f32[1536,512]{1,0:T(8,128)}, f32[512,512]{1,0:T(8,128)}, f32[64,512]{1,0:T(8,128)S(1)}, f32[512,512]{1,0:T(8,128)}, f32[64,512]{1,0:T(8,128)S(1)}, /*index=5*/f32[64,512]{1,0:T(8,128)S(1)}) conditional(s32[]{:T(128)} %convert_element_type.341, (f32[1536,512]{1,0:T(8,128)}, f32[512,512]{1,0:T(8,128)}, ...), branch_computations={%region_162.163_spmd, %region_163.174_spmd} | conditional | flops 45 | bytes 18089356 | solution.py:389
  673.3 15.5 %conditional.48 = ((f32[1536,512]{1,0:T(8,128)}, f32[512,512]{1,0:T(8,128)})) conditional(s32[]{:T(128)} %convert_element_type.276, (f32[1536,512]{1,0:T(8,128)}, f32[512,512]{1,0:T(8,128)}) %tuple.1105, (s32[]{:T(128)}, s32[]{:T(128)}, pred[]{:T(512)}, pred[]{:T(512)}, pred[]{:T(512)}, /*index=5*/pred[]{:T(512)}, pred[]{:T(512)}, ...), branch_computations={%region_164.164_spmd, %region_165.165_spmd} | conditional | flops 15 | bytes 3670439 | solution.py:389
  697.8 48.1 %collective-permute-done.267 = f32[512,512]{1,0:T(8,128)} collective-permute-done((f32[512,512]{1,0:T(8,128)}, f32[512,512]{1,0:T(8,128)}, u32[]{:S(2)}, u32[]{:S(2)}) %collective-permute-start.267) | collective-permute-done | bytes 1048608 | tf_op jit(solution)/shard_map/cond/branch_1_fun/ppermute | solution.py:337
  751.3 40.6 %conditional.152 = (f32[1536,512]{1,0:T(8,128)}, f32[512,512]{1,0:T(8,128)}, f32[64,512]{1,0:T(8,128)S(1)}, f32[512,512]{1,0:T(8,128)}, f32[64,512]{1,0:T(8,128)S(1)}, /*index=5*/f32[64,512]{1,0:T(8,128)S(1)}) conditional(s32[]{:T(128)} %convert_element_type.339, (f32[1536,512]{1,0:T(8,128)}, f32[512,512]{1,0:T(8,128)}, ...), branch_computations={%region_178.179_spmd, %region_179.190_spmd} | conditional | flops 42 | bytes 18089336 | solution.py:389
  752.6 16.9 %conditional.53 = ((f32[1536,512]{1,0:T(8,128)}, f32[512,512]{1,0:T(8,128)})) conditional(s32[]{:T(128)} %convert_element_type.280, (f32[1536,512]{1,0:T(8,128)}, f32[512,512]{1,0:T(8,128)}) %tuple.1119, (s32[]{:T(128)}, s32[]{:T(128)}, pred[]{:T(512)}, pred[]{:T(512)}, pred[]{:T(512)}, /*index=5*/pred[]{:T(512)}, f32[64,512]{1,0:T(8,128)S(1)}, ...), branch_computations={%region_180.180_spmd, %region_181.181_spmd} | conditional | flops 16 | bytes 3670448 | solution.py:389
  791.9 112.3 %conditional.155 = (f32[1536,512]{1,0:T(8,128)}, f32[512,512]{1,0:T(8,128)}, f32[64,512]{1,0:T(8,128)S(1)}, f32[512,512]{1,0:T(8,128)}, f32[64,512]{1,0:T(8,128)S(1)}, /*index=5*/f32[64,512]{1,0:T(8,128)S(1)}) conditional(s32[]{:T(128)} %convert_element_type.337, (f32[1536,512]{1,0:T(8,128)}, f32[512,512]{1,0:T(8,128)}, ...), branch_computations={%region_194.195_spmd, %region_195.206_spmd} | conditional | flops 39 | bytes 18089318 | solution.py:389
  793.2 16.9 %conditional.58 = ((f32[1536,512]{1,0:T(8,128)}, f32[512,512]{1,0:T(8,128)})) conditional(s32[]{:T(128)} %convert_element_type.283, (f32[1536,512]{1,0:T(8,128)}, f32[512,512]{1,0:T(8,128)}) %tuple.1133, (s32[]{:T(128)}, s32[]{:T(128)}, pred[]{:T(512)}, pred[]{:T(512)}, pred[]{:T(512)}, /*index=5*/f32[64,512]{1,0:T(8,128)S(1)}, ...), branch_computations={%region_196.196_spmd, %region_197.197_spmd} | conditional | flops 17 | bytes 3670457 | solution.py:389
  819.0 38.4 %collective-permute-done.312 = f32[512,512]{1,0:T(8,128)} collective-permute-done((f32[512,512]{1,0:T(8,128)}, f32[512,512]{1,0:T(8,128)}, u32[]{:S(2)}, u32[]{:S(2)}) %collective-permute-start.312) | collective-permute-done | bytes 1048608 | tf_op jit(solution)/shard_map/cond/branch_1_fun/ppermute | solution.py:337
  862.5 16.9 %conditional.60 = ((f32[1536,512]{1,0:T(8,128)}, f32[512,512]{1,0:T(8,128)})) conditional(s32[]{:T(128)} %convert_element_type.282, (f32[1536,512]{1,0:T(8,128)}, f32[512,512]{1,0:T(8,128)}) %tuple.1137, (s32[]{:T(128)}, s32[]{:T(128)}, f32[64,512]{1,0:T(8,128)S(1)}, f32[1536,512]{1,0:T(8,128)}, s32[16,64,128]{2,1,0:T(8,128)S(1)}) %tuple.1138), branch_computations={%region_200.200_spmd, %region_201.201_spmd} | conditional | flops 13 | bytes 3670406 | solution.py:389
  879.4 19.2 %collective-permute-done.313 = f32[512,512]{1,0:T(8,128)} collective-permute-done((f32[512,512]{1,0:T(8,128)}, f32[512,512]{1,0:T(8,128)}, u32[]{:S(2)}, u32[]{:S(2)}) %collective-permute-start.313) | collective-permute-done | bytes 1048608 | tf_op jit(solution)/shard_map/cond/branch_1_fun/ppermute | solution.py:337
  904.2 111.9 %conditional.158 = (f32[1536,512]{1,0:T(8,128)}, f32[512,512]{1,0:T(8,128)}, f32[64,512]{1,0:T(8,128)S(1)}, f32[512,512]{1,0:T(8,128)}, f32[64,512]{1,0:T(8,128)S(1)}, /*index=5*/f32[64,512]{1,0:T(8,128)S(1)}) conditional(s32[]{:T(128)} %convert_element_type.335, (f32[1536,512]{1,0:T(8,128)}, f32[512,512]{1,0:T(8,128)}, ...), branch_computations={%region_210.211_spmd, %region_211.222_spmd} | conditional | flops 37 | bytes 18089304 | solution.py:389
  905.5 16.3 %conditional.63 = ((f32[1536,512]{1,0:T(8,128)}, f32[512,512]{1,0:T(8,128)})) conditional(s32[]{:T(128)} %convert_element_type.286, (f32[1536,512]{1,0:T(8,128)}, f32[512,512]{1,0:T(8,128)}) %tuple.1147, (s32[]{:T(128)}, s32[]{:T(128)}, pred[]{:T(512)}, pred[]{:T(512)}, f32[64,512]{1,0:T(8,128)S(1)}, /*index=5*/f32[1536,512]{1,0:T(8,128)}, ...), branch_computations={%region_212.212_spmd, %region_213.213_spmd} | conditional | flops 18 | bytes 3670466 | solution.py:389
  930.7 42.9 %collective-permute-done.335 = f32[512,512]{1,0:T(8,128)} collective-permute-done((f32[512,512]{1,0:T(8,128)}, f32[512,512]{1,0:T(8,128)}, u32[]{:S(2)}, u32[]{:S(2)}) %collective-permute-start.335) | collective-permute-done | bytes 1048608 | tf_op jit(solution)/shard_map/cond/branch_1_fun/ppermute | solution.py:337
  978.8 16.3 %conditional.65 = ((f32[1536,512]{1,0:T(8,128)}, f32[512,512]{1,0:T(8,128)})) conditional(s32[]{:T(128)} %convert_element_type.285, (f32[1536,512]{1,0:T(8,128)}, f32[512,512]{1,0:T(8,128)}) %tuple.1151, (s32[]{:T(128)}, s32[]{:T(128)}, f32[64,512]{1,0:T(8,128)S(1)}, f32[1536,512]{1,0:T(8,128)}, s32[16,64,128]{2,1,0:T(8,128)S(1)}) %tuple.1152), branch_computations={%region_216.216_spmd, %region_217.217_spmd} | conditional | flops 13 | bytes 3670406 | solution.py:389
  995.0 15.9 %collective-permute-done.336 = f32[512,512]{1,0:T(8,128)} collective-permute-done((f32[512,512]{1,0:T(8,128)}, f32[512,512]{1,0:T(8,128)}, u32[]{:S(2)}, u32[]{:S(2)}) %collective-permute-start.336) | collective-permute-done | bytes 1048608 | tf_op jit(solution)/shard_map/cond/branch_1_fun/ppermute | solution.py:337
  1016.1 19.6 %conditional.159 = (f32[1536,512]{1,0:T(8,128)}, f32[512,512]{1,0:T(8,128)}, f32[1536,512]{1,0:T(8,128)}) conditional(s32[]{:T(128)} %convert_element_type.334, (f32[1536,512]{1,0:T(8,128)}, f32[512,512]{1,0:T(8,128)}) %tuple.1311, (s32[]{:T(128)}, s32[]{:T(128)}, f32[64,512]{1,0:T(8,128)S(1)}, f32[1536,512]{1,0:T(8,128)}, ...), branch_computations={%region_222.223_spmd, %region_223.224_spmd} | conditional | flops 6 | bytes 9961800 | solution.py:389
  1044.4 36.4 %conditional.161 = (f32[1536,512]{1,0:T(8,128)}) conditional(s32[]{:T(128)} %convert_element_type.333, f32[1536,512]{1,0:T(8,128)} %get-tuple-element.3866, (s32[]{:T(128)}, f32[1536,512]{1,0:T(8,128)}, f32[512,512]{1,0:T(8,128)}, s32[]{:T(128)}, f32[64,512]{1,0:T(8,128)S(1)}, /*index=5*/s32[16,64,128]{2,1,0:T(8,128)S(1)}, ...), branch_computations={%region_226.227_spmd, %region_227.232_spmd} | conditional | flops 21 | bytes 24642212 | solution.py:389
  1045.7 19.6 %conditional.68 = (f32[1536,512]{1,0:T(8,128)}, f32[512,512]{1,0:T(8,128)S(1)}, f32[1536,512]{1,0:T(8,128)}) conditional(s32[]{:T(128)} %convert_element_type.287, (f32[1536,512]{1,0:T(8,128)}, f32[512,512]{1,0:T(8,128)}) %tuple.1162, (s32[]{:T(128)}, s32[]{:T(128)}, pred[]{:T(512)}, f32[64,512]{1,0:T(8,128)S(1)}, f32[1536,512]{1,0:T(8,128)}, ...), branch_computations={%region_228.228_spmd, %region_229.229_spmd} | conditional | flops 19 | bytes 14156279 | solution.py:389
  (291 shorter events, 396.9 us)
Async XLA Ops:
  70.6 27.8 %collective-permute-start.243 = (f32[512,512]{1,0:T(8,128)}, f32[512,512]{1,0:T(8,128)}, u32[]{:S(2)}, u32[]{:S(2)}) collective-permute-start(f32[512,512]{1,0:T(8,128)} %get-tuple-element.3276), channel_id=1, source_target_pairs={{0,8},{1,9},{2,10},{3,11},{4,12},{5,13},{6,14},{7,15},{16,32},{17,... | collective-permute-start | bytes 3145736 | tf_op jit(solution)/shard_map/cond/branch_1_fun/ppermute | solution.py:337
  73.9 9.0 collective-permute-start.230
  89.5 576.5 %collective-permute-start.244 = (f32[512,512]{1,0:T(8,128)}, f32[512,512]{1,0:T(8,128)}, u32[]{:S(2)}, u32[]{:S(2)}) collective-permute-start(f32[512,512]{1,0:T(8,128)} %get-tuple-element.3276), channel_id=1, source_target_pairs={{0,16},{1,17},{2,18},{3,19},{4,20},{5,21},{6,22},{7,23},{16,48},{1... | collective-permute-start | bytes 3145736 | tf_op jit(solution)/shard_map/cond/branch_1_fun/ppermute | solution.py:337
  671.6 26.1 %collective-permute-start.266 = (f32[512,512]{1,0:T(8,128)}, f32[512,512]{1,0:T(8,128)}, u32[]{:S(2)}, u32[]{:S(2)}) collective-permute-start(f32[512,512]{1,0:T(8,128)} %get-tuple-element.3351), channel_id=1, source_target_pairs={{8,16},{9,17},{10,18},{11,19},{12,20},{13,21},{14,22},{15,23},{0,2... | collective-permute-start | bytes 3145736 | tf_op jit(solution)/shard_map/cond/branch_1_fun/ppermute | solution.py:337
  688.8 57.1 %collective-permute-start.267 = (f32[512,512]{1,0:T(8,128)}, f32[512,512]{1,0:T(8,128)}, u32[]{:S(2)}, u32[]{:S(2)}) collective-permute-start(f32[512,512]{1,0:T(8,128)} %get-tuple-element.3351), channel_id=1, source_target_pairs={{8,24},{9,25},{10,26},{11,27},{12,28},{13,29},{14,30},{15,31},{0,3... | collective-permute-start | bytes 3145736 | tf_op jit(solution)/shard_map/cond/branch_1_fun/ppermute | solution.py:337
  751.3 34.4 %collective-permute-start.289 = (f32[512,512]{1,0:T(8,128)}, f32[512,512]{1,0:T(8,128)}, u32[]{:S(2)}, u32[]{:S(2)}) collective-permute-start(f32[512,512]{1,0:T(8,128)} %get-tuple-element.3425), channel_id=1, source_target_pairs={{16,24},{17,25},{18,26},{19,27},{20,28},{21,29},{22,30},{23,31},{8... | collective-permute-start | bytes 3145736 | tf_op jit(solution)/shard_map/cond/branch_1_fun/ppermute | solution.py:337
  752.7 8.6 collective-permute-start.275
  753.4 8.9 collective-permute-start.276
  756.0 8.3 collective-permute-start.277
  769.5 21.3 %collective-permute-start.290 = (f32[512,512]{1,0:T(8,128)}, f32[512,512]{1,0:T(8,128)}, u32[]{:S(2)}, u32[]{:S(2)}) collective-permute-start(f32[512,512]{1,0:T(8,128)} %get-tuple-element.3425), channel_id=1, source_target_pairs={{16,32},{17,33},{18,34},{19,35},{20,36},{21,37},{22,38},{23,39},{8... | collective-permute-start | bytes 3145736 | tf_op jit(solution)/shard_map/cond/branch_1_fun/ppermute | solution.py:337
  791.9 65.5 %collective-permute-start.312 = (f32[512,512]{1,0:T(8,128)}, f32[512,512]{1,0:T(8,128)}, u32[]{:S(2)}, u32[]{:S(2)}) collective-permute-start(f32[512,512]{1,0:T(8,128)} %get-tuple-element.3498), channel_id=1, source_target_pairs={{24,32},{25,33},{26,34},{27,35},{28,36},{29,37},{30,38},{31,39},{1... | collective-permute-start | bytes 3145736 | tf_op jit(solution)/shard_map/cond/branch_1_fun/ppermute | solution.py:337
  794.3 8.5 collective-permute-start.299
  796.5 8.3 collective-permute-start.300
  797.0 8.5 collective-permute-start.301
  810.1 88.6 %collective-permute-start.313 = (f32[512,512]{1,0:T(8,128)}, f32[512,512]{1,0:T(8,128)}, u32[]{:S(2)}, u32[]{:S(2)}) collective-permute-start(f32[512,512]{1,0:T(8,128)} %get-tuple-element.3498), channel_id=1, source_target_pairs={{24,40},{25,41},{26,42},{27,43},{28,44},{29,45},{30,46},{31,47},{1... | collective-permute-start | bytes 3145736 | tf_op jit(solution)/shard_map/cond/branch_1_fun/ppermute | solution.py:337
  862.5 8.6 collective-permute-start.305
  863.2 8.9 collective-permute-start.306
  865.8 8.3 collective-permute-start.307
  904.2 69.4 %collective-permute-start.335 = (f32[512,512]{1,0:T(8,128)}, f32[512,512]{1,0:T(8,128)}, u32[]{:S(2)}, u32[]{:S(2)}) collective-permute-start(f32[512,512]{1,0:T(8,128)} %get-tuple-element.3570), channel_id=1, source_target_pairs={{32,40},{33,41},{34,42},{35,43},{36,44},{37,45},{38,46},{39,47},{2... | collective-permute-start | bytes 3145736 | tf_op jit(solution)/shard_map/cond/branch_1_fun/ppermute | solution.py:337
  906.6 8.1 collective-permute-start.322
  921.8 89.1 %collective-permute-start.336 = (f32[512,512]{1,0:T(8,128)}, f32[512,512]{1,0:T(8,128)}, u32[]{:S(2)}, u32[]{:S(2)}) collective-permute-start(f32[512,512]{1,0:T(8,128)} %get-tuple-element.3570), channel_id=1, source_target_pairs={{32,48},{33,49},{34,50},{35,51},{36,52},{37,53},{38,54},{39,55},{2... | collective-permute-start | bytes 3145736 | tf_op jit(solution)/shard_map/cond/branch_1_fun/ppermute | solution.py:337
  979.5 8.4 collective-permute-start.329
  1017.2 8.1 collective-permute-start.338
  1044.4 26.6 %collective-permute-start.351 = (f32[512,512]{1,0:T(8,128)}, f32[512,512]{1,0:T(8,128)}, u32[]{:S(2)}, u32[]{:S(2)}) collective-permute-start(f32[512,512]{1,0:T(8,128)} %get-tuple-element.3624), channel_id=1, source_target_pairs={{40,48},{41,49},{42,50},{43,51},{44,52},{45,53},{46,54},{47,55},{3... | collective-permute-start | bytes 3145736 | tf_op jit(solution)/shard_map/cond/branch_1_fun/ppermute | solution.py:337
  (61 other events, 325.7 us)

commit v4 on v3

--- a/solution.py
+++ b/solution.py
@@ -211,19 +211,33 @@
         return 0
 
     lax.fori_loop(0, TALL // chunk, subtract, 0)
-    store = [
-        pltpu.make_async_copy(target.at[pl.ds(0, SHARE)], following, sems.at[0]),
-        pltpu.make_async_copy(target, factors.at[rows], sems.at[1]),
-    ]
-    for copy in store:
-        copy.start()
-    for copy in store:
-        copy.wait()
+    head = pl.ds(0, SHARE)
+    tail = pl.ds(SHARE, TALL - SHARE)
+    after = pl.ds(pl.multiple_of((source + 2) * SHARE, SHARE), TALL - SHARE)
+
+    def put_head():
+        first = pl.ds(pl.multiple_of((source + 1) * SHARE, SHARE), SHARE)
+        store = [
+            pltpu.make_async_copy(target.at[head], following, sems.at[0]),
+            pltpu.make_async_copy(target.at[head], factors.at[first], sems.at[2]),
+        ]
+        for copy in store:
+            copy.start()
+        for copy in store:
+            copy.wait()
+
+    rest = pltpu.make_async_copy(target.at[tail], factors.at[after], sems.at[1])
+    rest.start()
     if far:
+        pl.when(panel != step + 2)(put_head)
         keep.wait()
-
-
-def place_kernel(scal, factors_in, pivot_ref, *rest):
+    else:
+        put_head()
+    rest.wait()
+
+
+def place_kernel(scal, factors_in, upper_in, pivot_ref, *rest):
+    del upper_in
     parts, (factors, upper_out), (upper, swapped, picks, sems) = rest[:8], rest[8:10], rest[10:]
     place = scal[1]
     source = scal[2]
@@ -317,14 +331,15 @@
 
 def put_in_place(scal, factors, upper, picks, parts):
     scratch = [f32(B, B), f32(SHARE, B), pltpu.VMEM((SHARE, 128), jnp.int32), pltpu.SemaphoreType.DMA((9,))]
-    return call(place_kernel, like(factors, upper), scratch, {1: 0}, factors, picks, *parts, scal=scal)
+    return call(place_kernel, like(factors, upper), scratch, {1: 0, 2: 1}, factors, upper, picks, *parts, scal=scal)
 
 
 def gather(share):
-    turned = [share] + [
-        lax.ppermute(share, "row", [(r, (r + 2 * turn) % ROWS) for r in range(ROWS)]) for turn in (1, 2, 3)
-    ]
-    return turned + [lax.ppermute(part, "row", [(r, r ^ 1) for r in range(ROWS)]) for part in turned]
+    swap = [(r, r ^ 1) for r in range(ROWS)]
+    turned = [lax.ppermute(share, "row", [(r, (r + 2 * turn) % ROWS) for r in range(ROWS)]) for turn in (1, 2, 3)]
+    beside = lax.ppermute(share, "row", swap)
+    *turned, beside = lax.optimization_barrier((*turned, beside))
+    return [share, *turned, beside] + [lax.ppermute(part, "row", swap) for part in turned]
 
 
 def send(cur, step, table):
@@ -354,8 +369,11 @@
     return takers, sorted(inside)
 
 
-def shifted(odd):
-    return [(c * ROWS + r, (c + 1) * ROWS + r) for c in range(odd, PANELS - 1, 2) for r in range(ROWS)]
+def shifted(amount, group):
+    return [
+        (c * ROWS + r, (c + amount) * ROWS + r)
+        for c in range(PANELS - amount) if c // amount % 2 == group for r in range(ROWS)
+    ]
 
 
 def among(panel, panels):
@@ -392,24 +410,23 @@
         return put_in_place(jnp.stack([panel, place, source]), factors, upper, picks, gather(following))
 
     upper = jnp.zeros((B, B), jnp.float32)
-
-    def begin(factors, cur, front, upper):
-        factors, upper = collect(panel, factors, upper, following)
-        factors, cur, front = multiply(0, factors, cur, front, upper, cur, *inverse(upper, y_high, y_low))
-        return factors, cur, front, upper
-
-    factors, cur, front, upper = when([0], begin, factors, cur, front, upper)
+    fresh = jnp.zeros((B, B), jnp.float32)
+
+    def prepare(factors, upper):
+        return collect(0, factors, upper, following)
+
+    factors, upper = when([0, 1], prepare, factors, upper)
+
+    def begin(factors, cur, front):
+        return multiply(0, factors, cur, front, upper, cur, *inverse(upper, y_high, y_low))
+
+    factors, cur, front = when([0], begin, factors, cur, front)
 
     for step in range(PANELS - 1):
         coming = step + 1
 
-        def prepare(factors, upper):
-            return collect(step, factors, upper, following)
-
-        factors, upper = when([coming], prepare, factors, upper)
-
         def lead(following):
-            arrived = lax.ppermute(front, ("col", "row"), shifted(step % 2))
+            arrived = lax.ppermute(front, ("col", "row"), shifted(1, step % 2))
             return (advance(step, factors, following, upper, arrived),)
 
         (following,) = when([step, coming], lead, following)
@@ -417,7 +434,7 @@
         far, _ = members(step, [FAR])
         _, inside = members(step, [NEAR, FAR])
 
-        def exchange(factors, cur, front, upper, following):
+        def exchange(factors, cur, front, upper, fresh, following):
             p = send(cur, step, NEAR)
             q = send(cur, step, FAR) if far else None
             source = jnp.where(
@@ -425,9 +442,9 @@
             )
 
             def bring(factors, fresh):
-                return collect(source, factors, upper, following)
-
-            factors, fresh = when(sorted(set(near) | set(far)), bring, factors, upper)
+                return collect(source, factors, fresh, following)
+
+            factors, fresh = when(sorted(set(near) | set(far)), bring, factors, fresh)
             high, low = inverse(fresh, y_high, y_low)
 
             def near_update(factors, following):
@@ -439,19 +456,32 @@
                 return collect(step + 1 - lag_of(step, NEAR, panel), factors, fresh, following)
 
             factors, fresh = when(sorted(set(near) & set(far)), again, factors, fresh)
-
-            def far_update(factors, new_cur, following):
-                return update(step, True, where, factors, new_cur, following, fresh, q)
-
-            factors, new_cur, following = when(far, far_update, factors, cur, following)
+            if far:
+                def second(following):
+                    arrived = lax.ppermute(front, ("col", "row"), shifted(2, step // 2 % 2))
+                    return (advance(step, factors, following, fresh, arrived),)
+
+                (following,) = when([step, step + 2], second, following)
+
+                def ahead(factors, upper):
+                    return collect(coming, factors, upper, following)
+
+                factors, upper = when([step + 2], ahead, factors, upper)
+
+            def far_update(factors, cur, following):
+                return update(step, True, where, factors, cur, following, fresh, q)
+
+            factors, cur, following = when(far, far_update, factors, cur, following)
 
             def own(factors, cur, front):
                 return multiply(coming, factors, cur, front, upper, p, high, low)
 
-            factors, new_cur, front = when([coming], own, factors, new_cur, front)
-            return factors, new_cur, front, fresh, following
-
-        factors, cur, front, upper, following = when(inside, exchange, factors, cur, front, upper, following)
+            factors, cur, front = when([coming], own, factors, cur, front)
+            return factors, cur, front, upper, fresh, following
+
+        factors, cur, front, upper, fresh, following = when(
+            inside, exchange, factors, cur, front, upper, fresh, following
+        )
     at = (panel + 1) * SHARE
     own = lax.dynamic_slice_in_dim(factors, at, TALL, 0)
     own = lax.dot_general(

time: 1100 us -> 1140 us (1.036)
  waiting for transfers between devices: 757 us -> 807 us
  loops' own time: 41.3 us -> 61.7 us
  local copies, waits for them, and re-layouts: 43.5 us -> 24.7 us
    ppermute x11, waiting for transfers between devices: 739 us -> 760 us  [send(): return lax.ppermute(cur, ('col', 'row'), pairs)]
    cond x38 -> x14, local copies, waits for them, and re-layouts: 33.2 us -> 12.6 us
    another operation x73 -> x69, loops' own time: 41.3 us -> 61.7 us  [when(): lax.cond(among(panel, panels), lambda *state: tuple(run(*state)), lambda...]
    ppermute x37 -> x38, waiting for transfers between devices: 14.5 us -> 32.7 us  [the longest x1 15.2 us: second(): arrived = lax.ppermute(front, ('col', 'row'), shifted(2, step // 2 % 2))]
    ppermute x37 -> x38, starting transfers between devices: 64.1 us -> 61.6 us  [the longest x27 32.1 us: gather(): lax.ppermute(part, 'row', swap)]
    pallas_call x25 -> x26, Pallas kernels: 121 us -> 122 us  [call(): pl.pallas_call(kernel, out_shape=out_shape, in_specs=[SMEM] * len(first)...]
  transfers between devices with their start and end apart: 75 -> 76, of which waited for: 28 -> 51; matrix products, arithmetic and copies ran while one was open for 0% -> 0% of each run, Pallas kernels for 8% -> 8%
where the time goes in v4:
time: 1140 us; the launch traced here: 1130 us
  waiting for transfers between devices  807 us (71%)
  Pallas kernels  122 us (11%)
  starting transfers between devices  110 us (10%)
  loops' own time  61.7 us (5%)
  local copies, waits for them, and re-layouts  24.7 us (2%)
    ppermute x11, waiting for transfers between devices, send(): return lax.ppermute(cur, ('col', 'row'), pairs)  760 us
    pallas_call x26, Pallas kernels, call(): pl.pallas_call(kernel, out_shape=out_shape, in_specs=[SMEM] * len(first)...  122 us
    another operation x69, loops' own time, when(): lax.cond(among(panel, panels), lambda *state: tuple(run(*state)), lambda...  61.7 us
    ppermute x27, starting transfers between devices, gather(): lax.ppermute(share, 'row', [(r, (r + 2 * turn) % ROWS) for r in range(ROW...  33.2 us
    ppermute x27, starting transfers between devices, gather(): lax.ppermute(part, 'row', swap)  32.1 us
    ppermute x9, starting transfers between devices, gather(): beside = lax.ppermute(share, 'row', swap)  27 us
  transfers between devices with their start and end apart: 76, of which 51 were waited for; matrix products, arithmetic and copies ran while one was open for 0% of the time, Pallas kernels for 8%

profile of v4, /device:TPU:31, one launch (start us, length us, event | category | flops | bytes accessed | tf_op | source)
XLA Modules:
  0.0 1130.3 jit_solution(17099872165855014903)
XLA Ops:
  27.5 14.9 %conditional.141 = ((f32[1536,512]{1,0:T(8,128)}, f32[512,512]{1,0:T(8,128)}, f32[64,512]{1,0:T(8,128)S(1)}, f32[512,512]{1,0:T(8,128)}, f32[512,512]{1,0:T(8,128)}, /*index=5*/f32[64,512]{1,0:T(8,128)S(1)})) conditional(s32[]{:T(128)} %convert_element_type.377, (f32[1536,512]{1,0:T(8,128)}, f32[512,512]{1,0:T(8,128)}, f32[64,512]{1,0:T(8,128)S(1)}, ...), branch_computations={%region_74.75_spmd, %region_75.90_spmd} | conditional | flops 57 | bytes 22022024 | solution.py:407
  57.2 14.8 %conditional.149 = ((f32[1536,512]{1,0:T(8,128)}, f32[512,512]{1,0:T(8,128)}, f32[64,512]{1,0:T(8,128)S(1)}, f32[512,512]{1,0:T(8,128)}, f32[512,512]{1,0:T(8,128)}, /*index=5*/f32[64,512]{1,0:T(8,128)S(1)})) conditional(s32[]{:T(128)} %convert_element_type.373, (f32[1536,512]{1,0:T(8,128)}, f32[512,512]{1,0:T(8,128)}, ...), branch_computations={%region_146.147_spmd, %region_147.162_spmd} | conditional | flops 57 | bytes 22022024 | solution.py:407
  72.0 617.0 %conditional.151 = ((f32[1536,512]{1,0:T(8,128)}, f32[512,512]{1,0:T(8,128)}, f32[64,512]{1,0:T(8,128)S(1)}, f32[512,512]{1,0:T(8,128)}, f32[512,512]{1,0:T(8,128)}, /*index=5*/f32[64,512]{1,0:T(8,128)S(1)})) conditional(s32[]{:T(128)} %convert_element_type.372, (f32[1536,512]{1,0:T(8,128)}, f32[512,512]{1,0:T(8,128)}, ...), branch_computations={%region_164.165_spmd, %region_165.180_spmd} | conditional | flops 57 | bytes 22022024 | solution.py:407
  73.7 17.4 %conditional.61 = ((f32[1536,512]{1,0:T(8,128)}, f32[512,512]{1,0:T(8,128)})) conditional(s32[]{:T(128)} %convert_element_type.312, (f32[1536,512]{1,0:T(8,128)}, f32[512,512]{1,0:T(8,128)}) %tuple.1148, (s32[]{:T(128)}, s32[]{:T(128)}, pred[]{:T(512)}, pred[]{:T(512)}, pred[]{:T(512)}, /*index=5*/pred[]{:T(512)}, pred[]{:T(512)}, pred[]{:T(512)}, ...), branch_computations={%region_166.166_spmd, %region_167.167_spmd} | conditional | flops 14 | bytes 3670430 | solution.py:407
  100.1 583.9 %collective-permute-done.258 = f32[512,512]{1,0:T(8,128)} collective-permute-done((f32[512,512]{1,0:T(8,128)}, f32[512,512]{1,0:T(8,128)}, u32[]{:S(2)}, u32[]{:S(2)}) %collective-permute-start.258) | collective-permute-done | bytes 1048608 | tf_op jit(solution)/shard_map/cond/branch_1_fun/ppermute | solution.py:352
  689.1 85.1 %conditional.153 = ((f32[1536,512]{1,0:T(8,128)}, f32[512,512]{1,0:T(8,128)}, f32[64,512]{1,0:T(8,128)S(1)}, f32[512,512]{1,0:T(8,128)}, f32[512,512]{1,0:T(8,128)}, /*index=5*/f32[64,512]{1,0:T(8,128)S(1)})) conditional(s32[]{:T(128)} %convert_element_type.371, (f32[1536,512]{1,0:T(8,128)}, f32[512,512]{1,0:T(8,128)}, ...), branch_computations={%region_182.183_spmd, %region_183.198_spmd} | conditional | flops 55 | bytes 22022010 | solution.py:407
  690.8 15.9 %conditional.68 = ((f32[1536,512]{1,0:T(8,128)}, f32[512,512]{1,0:T(8,128)})) conditional(s32[]{:T(128)} %convert_element_type.319, (f32[1536,512]{1,0:T(8,128)}, f32[512,512]{1,0:T(8,128)}) %tuple.1167, (s32[]{:T(128)}, s32[]{:T(128)}, pred[]{:T(512)}, pred[]{:T(512)}, pred[]{:T(512)}, /*index=5*/pred[]{:T(512)}, pred[]{:T(512)}, ...), branch_computations={%region_184.184_spmd, %region_185.185_spmd} | conditional | flops 15 | bytes 3670439 | solution.py:407
  715.7 53.1 %collective-permute-done.281 = f32[512,512]{1,0:T(8,128)} collective-permute-done((f32[512,512]{1,0:T(8,128)}, f32[512,512]{1,0:T(8,128)}, u32[]{:S(2)}, u32[]{:S(2)}) %collective-permute-start.281) | collective-permute-done | bytes 1048608 | tf_op jit(solution)/shard_map/cond/branch_1_fun/ppermute | solution.py:352
  774.2 42.8 %conditional.155 = ((f32[1536,512]{1,0:T(8,128)}, f32[512,512]{1,0:T(8,128)}, f32[64,512]{1,0:T(8,128)S(1)}, f32[512,512]{1,0:T(8,128)}, f32[512,512]{1,0:T(8,128)}, /*index=5*/f32[64,512]{1,0:T(8,128)S(1)})) conditional(s32[]{:T(128)} %convert_element_type.370, (f32[1536,512]{1,0:T(8,128)}, f32[512,512]{1,0:T(8,128)}, ...), branch_computations={%region_200.201_spmd, %region_201.216_spmd} | conditional | flops 52 | bytes 22021992 | solution.py:407
  775.5 17.6 %conditional.75 = ((f32[1536,512]{1,0:T(8,128)}, f32[512,512]{1,0:T(8,128)})) conditional(s32[]{:T(128)} %convert_element_type.325, (f32[1536,512]{1,0:T(8,128)}, f32[512,512]{1,0:T(8,128)}) %tuple.1186, (s32[]{:T(128)}, s32[]{:T(128)}, pred[]{:T(512)}, pred[]{:T(512)}, pred[]{:T(512)}, /*index=5*/pred[]{:T(512)}, f32[64,512]{1,0:T(8,128)S(1)}, ...), branch_computations={%region_202.202_spmd, %region_203.203_spmd} | conditional | flops 16 | bytes 3670448 | solution.py:407
  817.0 120.5 %conditional.157 = ((f32[1536,512]{1,0:T(8,128)}, f32[512,512]{1,0:T(8,128)}, f32[64,512]{1,0:T(8,128)S(1)}, f32[512,512]{1,0:T(8,128)}, f32[512,512]{1,0:T(8,128)}, /*index=5*/f32[64,512]{1,0:T(8,128)S(1)})) conditional(s32[]{:T(128)} %convert_element_type.369, (f32[1536,512]{1,0:T(8,128)}, f32[512,512]{1,0:T(8,128)}, ...), branch_computations={%region_218.219_spmd, %region_219.234_spmd} | conditional | flops 49 | bytes 22021972 | solution.py:407
  818.3 17.7 %conditional.82 = ((f32[1536,512]{1,0:T(8,128)}, f32[512,512]{1,0:T(8,128)})) conditional(s32[]{:T(128)} %convert_element_type.330, (f32[1536,512]{1,0:T(8,128)}, f32[512,512]{1,0:T(8,128)}) %tuple.1205, (s32[]{:T(128)}, s32[]{:T(128)}, pred[]{:T(512)}, pred[]{:T(512)}, pred[]{:T(512)}, /*index=5*/f32[64,512]{1,0:T(8,128)S(1)}, ...), branch_computations={%region_220.220_spmd, %region_221.221_spmd} | conditional | flops 17 | bytes 3670457 | solution.py:407
  844.9 43.0 %collective-permute-done.326 = f32[512,512]{1,0:T(8,128)} collective-permute-done((f32[512,512]{1,0:T(8,128)}, f32[512,512]{1,0:T(8,128)}, u32[]{:S(2)}, u32[]{:S(2)}) %collective-permute-start.326) | collective-permute-done | bytes 1048608 | tf_op jit(solution)/shard_map/cond/branch_1_fun/ppermute | solution.py:352
  892.9 17.6 %conditional.84 = ((f32[1536,512]{1,0:T(8,128)}, f32[512,512]{1,0:T(8,128)})) conditional(s32[]{:T(128)} %convert_element_type.328, (f32[1536,512]{1,0:T(8,128)}, f32[512,512]{1,0:T(8,128)}) %tuple.1209, (s32[]{:T(128)}, s32[]{:T(128)}, f32[64,512]{1,0:T(8,128)S(1)}, f32[1536,512]{1,0:T(8,128)}, f32[512,512]{1,0:T(8,128)}, ...), branch_computations={%region_224.224_spmd, %region_225.225_spmd} | conditional | flops 13 | bytes 3670406 | solution.py:407
  910.5 21.9 %collective-permute-done.327 = f32[512,512]{1,0:T(8,128)} collective-permute-done((f32[512,512]{1,0:T(8,128)}, f32[512,512]{1,0:T(8,128)}, u32[]{:S(2)}, u32[]{:S(2)}) %collective-permute-start.327) | collective-permute-done | bytes 1048608 | tf_op jit(solution)/shard_map/cond/branch_1_fun/ppermute | solution.py:352
  937.6 142.3 %conditional.159 = (f32[1536,512]{1,0:T(8,128)}, f32[512,512]{1,0:T(8,128)}, f32[64,512]{1,0:T(8,128)S(1)}, f32[512,512]{1,0:T(8,128)}, f32[512,512]{1,0:T(8,128...) conditional(s32[]{:T(128)} %convert_element_type.368, (f32[1536,512]{1,0:T(8,128)}, f32[512,512]{1,0:T(8,128)}, ...), branch_computations={%region_236.237_spmd, %region_237.252_spmd} | conditional | flops 46 | bytes 28313408 | solution.py:407
  938.9 16.9 %conditional.89 = ((f32[1536,512]{1,0:T(8,128)}, f32[512,512]{1,0:T(8,128)})) conditional(s32[]{:T(128)} %convert_element_type.334, (f32[1536,512]{1,0:T(8,128)}, f32[512,512]{1,0:T(8,128)}) %tuple.1227, (s32[]{:T(128)}, s32[]{:T(128)}, pred[]{:T(512)}, pred[]{:T(512)}, f32[64,512]{1,0:T(8,128)S(1)}, /*index=5*/f32[1536,512]{1,0:T(8,128)}, ...), branch_computations={%region_238.238_spmd, %region_239.239_spmd} | conditional | flops 18 | bytes 3670466 | solution.py:407
  964.7 49.8 %collective-permute-done.349 = f32[512,512]{1,0:T(8,128)} collective-permute-done((f32[512,512]{1,0:T(8,128)}, f32[512,512]{1,0:T(8,128)}, u32[]{:S(2)}, u32[]{:S(2)}) %collective-permute-start.349) | collective-permute-done | bytes 1048608 | tf_op jit(solution)/shard_map/cond/branch_1_fun/ppermute | solution.py:352
  1019.4 16.9 %conditional.91 = ((f32[1536,512]{1,0:T(8,128)}, f32[512,512]{1,0:T(8,128)})) conditional(s32[]{:T(128)} %convert_element_type.333, (f32[1536,512]{1,0:T(8,128)}, f32[512,512]{1,0:T(8,128)}) %tuple.1231, (s32[]{:T(128)}, s32[]{:T(128)}, f32[64,512]{1,0:T(8,128)S(1)}, f32[1536,512]{1,0:T(8,128)}, f32[512,512]{1,0:T(8,128)}, ...), branch_computations={%region_242.242_spmd, %region_243.243_spmd} | conditional | flops 13 | bytes 3670406 | solution.py:407
  1036.4 18.5 %conditional.92 = (f32[64,512]{1,0:T(8,128)S(1)}) conditional(s32[]{:T(128)} %convert_element_type.335, f32[64,512]{1,0:T(8,128)S(1)} %get-tuple-element.4103, (f32[64,512]{1,0:T(8,128)S(1)}, f32[1536,512]{1,0:T(8,128)}, f32[512,512]{1,0:T(8,128)}) %tuple.1234), branch_computations={%region_244.244_spmd, %region_245.245_spmd} | conditional | bytes 524336 | solution.py:407
  1037.7 15.2 %collective-permute-done.27.received = f32[64,512]{1,0:T(8,128)S(1)} collective-permute-done((f32[64,512]{1,0:T(8,128)S(1)}, f32[64,512]{1,0:T(8,128)S(1)}, u32[]{:S(2)}, u32[]{:S(2)}) %collective-permute-start.27) | collective-permute-done | bytes 131104 | tf_op jit(solution)/shard_map/cond/branch_1_fun/cond/branch_1_fun/ppermute | solution.py:461
  1054.9 16.2 %conditional.93 = ((f32[1536,512]{1,0:T(8,128)}, f32[512,512]{1,0:T(8,128)})) conditional(s32[]{:T(128)} %convert_element_type.333, (f32[1536,512]{1,0:T(8,128)}, f32[512,512]{1,0:T(8,128)}) %tuple.1233, (s32[]{:T(128)}, s32[]{:T(128)}, f32[64,512]{1,0:T(8,128)S(1)}, f32[1536,512]{1,0:T(8,128)}, f32[512,512]{1,0:T(8,128)}, ...), branch_computations={%region_246.246_spmd, %region_247.247_spmd} | conditional | flops 6 | bytes 3670328 | solution.py:407
  1088.6 37.8 %conditional.161 = (f32[1536,512]{1,0:T(8,128)}) conditional(s32[]{:T(128)} %convert_element_type.367, f32[1536,512]{1,0:T(8,128)} %get-tuple-element.4339, (s32[]{:T(128)}, f32[1536,512]{1,0:T(8,128)}, f32[512,512]{1,0:T(8,128)}, s32[]{:T(128)}, f32[64,512]{1,0:T(8,128)S(1)}, /*index=5*/s32[16,64,128]{2,1,0:T(8,128)S(1)}, ...), branch_computations={%region_254.255_spmd, %region_255.260_spmd} | conditional | flops 21 | bytes 20447888 | solution.py:407
  1089.9 19.9 %conditional.96 = (f32[1536,512]{1,0:T(8,128)}, f32[512,512]{1,0:T(8,128)}, f32[1536,512]{1,0:T(8,128)}) conditional(s32[]{:T(128)} %convert_element_type.336, (f32[1536,512]{1,0:T(8,128)}, f32[512,512]{1,0:T(8,128)}) %tuple.1244, (s32[]{:T(128)}, s32[]{:T(128)}, pred[]{:T(512)}, f32[64,512]{1,0:T(8,128)S(1)}, f32[1536,512]{1,0:T(8,128)}, ...), branch_computations={%region_256.256_spmd, %region_257.257_spmd} | conditional | flops 19 | bytes 9961947 | solution.py:407
  (267 shorter events, 387.4 us)
Async XLA Ops:
  72.0 28.0 %collective-permute-start.257 = (f32[512,512]{1,0:T(8,128)}, f32[512,512]{1,0:T(8,128)}, u32[]{:S(2)}, u32[]{:S(2)}) collective-permute-start(f32[512,512]{1,0:T(8,128)} %get-tuple-element.3739), channel_id=1, source_target_pairs={{0,8},{1,9},{2,10},{3,11},{4,12},{5,13},{6,14},{7,15},{16,32},{17,... | collective-permute-start | bytes 3145736 | tf_op jit(solution)/shard_map/cond/branch_1_fun/ppermute | solution.py:352
  73.7 7.2 collective-permute-start.236
  75.4 9.0 collective-permute-start.237
  91.1 592.9 %collective-permute-start.258 = (f32[512,512]{1,0:T(8,128)}, f32[512,512]{1,0:T(8,128)}, u32[]{:S(2)}, u32[]{:S(2)}) collective-permute-start(f32[512,512]{1,0:T(8,128)} %get-tuple-element.3739), channel_id=1, source_target_pairs={{0,16},{1,17},{2,18},{3,19},{4,20},{5,21},{6,22},{7,23},{16,48},{1... | collective-permute-start | bytes 3145736 | tf_op jit(solution)/shard_map/cond/branch_1_fun/ppermute | solution.py:352
  689.1 26.5 %collective-permute-start.280 = (f32[512,512]{1,0:T(8,128)}, f32[512,512]{1,0:T(8,128)}, u32[]{:S(2)}, u32[]{:S(2)}) collective-permute-start(f32[512,512]{1,0:T(8,128)} %get-tuple-element.3828), channel_id=1, source_target_pairs={{8,16},{9,17},{10,18},{11,19},{12,20},{13,21},{14,22},{15,23},{0,2... | collective-permute-start | bytes 3145736 | tf_op jit(solution)/shard_map/cond/branch_1_fun/ppermute | solution.py:352
  690.9 8.5 collective-permute-start.260
  706.7 62.1 %collective-permute-start.281 = (f32[512,512]{1,0:T(8,128)}, f32[512,512]{1,0:T(8,128)}, u32[]{:S(2)}, u32[]{:S(2)}) collective-permute-start(f32[512,512]{1,0:T(8,128)} %get-tuple-element.3828), channel_id=1, source_target_pairs={{8,24},{9,25},{10,26},{11,27},{12,28},{13,29},{14,30},{15,31},{0,3... | collective-permute-start | bytes 3145736 | tf_op jit(solution)/shard_map/cond/branch_1_fun/ppermute | solution.py:352
  774.2 36.8 %collective-permute-start.303 = (f32[512,512]{1,0:T(8,128)}, f32[512,512]{1,0:T(8,128)}, u32[]{:S(2)}, u32[]{:S(2)}) collective-permute-start(f32[512,512]{1,0:T(8,128)} %get-tuple-element.3916), channel_id=1, source_target_pairs={{16,24},{17,25},{18,26},{19,27},{20,28},{21,29},{22,30},{23,31},{8... | collective-permute-start | bytes 3145736 | tf_op jit(solution)/shard_map/cond/branch_1_fun/ppermute | solution.py:352
  775.5 7.5 collective-permute-start.282
  775.9 7.2 collective-permute-start.283
  793.1 22.9 %collective-permute-start.304 = (f32[512,512]{1,0:T(8,128)}, f32[512,512]{1,0:T(8,128)}, u32[]{:S(2)}, u32[]{:S(2)}) collective-permute-start(f32[512,512]{1,0:T(8,128)} %get-tuple-element.3916), channel_id=1, source_target_pairs={{16,32},{17,33},{18,34},{19,35},{20,36},{21,37},{22,38},{23,39},{8... | collective-permute-start | bytes 3145736 | tf_op jit(solution)/shard_map/cond/branch_1_fun/ppermute | solution.py:352
  817.0 70.9 %collective-permute-start.326 = (f32[512,512]{1,0:T(8,128)}, f32[512,512]{1,0:T(8,128)}, u32[]{:S(2)}, u32[]{:S(2)}) collective-permute-start(f32[512,512]{1,0:T(8,128)} %get-tuple-element.4003), channel_id=1, source_target_pairs={{24,32},{25,33},{26,34},{27,35},{28,36},{29,37},{30,38},{31,39},{1... | collective-permute-start | bytes 3145736 | tf_op jit(solution)/shard_map/cond/branch_1_fun/ppermute | solution.py:352
  818.3 7.5 collective-permute-start.305
  818.6 7.3 collective-permute-start.306
  836.0 96.3 %collective-permute-start.327 = (f32[512,512]{1,0:T(8,128)}, f32[512,512]{1,0:T(8,128)}, u32[]{:S(2)}, u32[]{:S(2)}) collective-permute-start(f32[512,512]{1,0:T(8,128)} %get-tuple-element.4003), channel_id=1, source_target_pairs={{24,40},{25,41},{26,42},{27,43},{28,44},{29,45},{30,46},{31,47},{1... | collective-permute-start | bytes 3145736 | tf_op jit(solution)/shard_map/cond/branch_1_fun/ppermute | solution.py:352
  892.9 7.6 collective-permute-start.312
  893.2 7.3 collective-permute-start.313
  937.6 76.9 %collective-permute-start.349 = (f32[512,512]{1,0:T(8,128)}, f32[512,512]{1,0:T(8,128)}, u32[]{:S(2)}, u32[]{:S(2)}) collective-permute-start(f32[512,512]{1,0:T(8,128)} %get-tuple-element.4101), channel_id=1, source_target_pairs={{32,40},{33,41},{34,42},{35,43},{36,44},{37,45},{38,46},{39,47},{2... | collective-permute-start | bytes 3145736 | tf_op jit(solution)/shard_map/cond/branch_1_fun/ppermute | solution.py:352
  955.8 115.2 %collective-permute-start.350 = (f32[512,512]{1,0:T(8,128)}, f32[512,512]{1,0:T(8,128)}, u32[]{:S(2)}, u32[]{:S(2)}) collective-permute-start(f32[512,512]{1,0:T(8,128)} %get-tuple-element.4101), channel_id=1, source_target_pairs={{32,48},{33,49},{34,50},{35,51},{36,52},{37,53},{38,54},{39,55},{2... | collective-permute-start | bytes 3145736 | tf_op jit(solution)/shard_map/cond/branch_1_fun/ppermute | solution.py:352
  1019.5 7.0 collective-permute-start.335
  1036.4 16.5 %collective-permute-start.27 = (f32[64,512]{1,0:T(8,128)S(1)}, f32[64,512]{1,0:T(8,128)S(1)}, u32[]{:S(2)}, u32[]{:S(2)}) collective-permute-start(f32[64,512]{1,0:T(8,128)S(1)} %get-tuple-element.4064), channel_id=1, source_target_pairs={{0,16},{1,17},{2,18},{3,19},{4,20},{5,21},{6,22},{7,23},{8,24},{9,... | collective-permute-start | bytes 393224 | tf_op jit(solution)/shard_map/cond/branch_1_fun/cond/branch_1_fun/ppermute | solution.py:461
  1055.2 7.2 collective-permute-start.343
  1088.6 28.0 %collective-permute-start.358 = (f32[512,512]{1,0:T(8,128)}, f32[512,512]{1,0:T(8,128)}, u32[]{:S(2)}, u32[]{:S(2)}) collective-permute-start(f32[512,512]{1,0:T(8,128)} %get-tuple-element.4155), channel_id=1, source_target_pairs={{40,48},{41,49},{42,50},{43,51},{44,52},{45,53},{46,54},{47,55},{3... | collective-permute-start | bytes 3145736 | tf_op jit(solution)/shard_map/cond/branch_1_fun/ppermute | solution.py:352
  1090.2 8.0 collective-permute-start.352
  (61 other events, 264.8 us)

commit v5 on v4

--- a/solution.py
+++ b/solution.py
@@ -15,7 +15,7 @@
 TALL = HB * SHARE
 TILE = 9
 
-NEAR = {1: (0, 0), 2: (1, -1), 3: (2, -2), 4: (2, 2)}
+NEAR = {2: (1, -1), 3: (2, -2), 4: (2, 2)}
 FAR = {2: (0, 0), 3: (1, -1), 5: (2, -2), 6: (2, 2)}
 
 
@@ -62,10 +62,10 @@
         copy.wait()
 
 
-def inverse_kernel(pivot_ref, y_high_ref, y_low_ref, high_ref, low_ref,
+def inverse_kernel(owner, pivot_ref, y_high_ref, y_low_ref, high_ref, low_ref,
                    pivot, y_high, y_low, high, low, other_high, other_low, result, sems):
     load = [
-        pltpu.make_async_copy(pivot_ref, pivot, sems.at[0]),
+        pltpu.make_async_copy(pivot_ref.at[pl.ds(owner % 2 * B, B)], pivot, sems.at[0]),
         pltpu.make_async_copy(y_high_ref, y_high, sems.at[1]),
         pltpu.make_async_copy(y_low_ref, y_low, sems.at[2]),
     ]
@@ -117,7 +117,7 @@
     ]
     if owner:
         load += [
-            pltpu.make_async_copy(upper_in, upper, sems.at[3]),
+            pltpu.make_async_copy(upper_in.at[pl.ds((owner - 1) % 2 * B, B)], upper, sems.at[3]),
             pltpu.make_async_copy(received, multipliers, sems.at[4]),
         ]
     for copy in load:
@@ -160,7 +160,7 @@
 def front_kernel(step, factors_in, upper_in, received, following, upper, multipliers, target, high, low, sems):
     rows = pl.ds((step + 1) * SHARE, SHARE)
     load = [
-        pltpu.make_async_copy(upper_in, upper, sems.at[0]),
+        pltpu.make_async_copy(upper_in.at[pl.ds(step % 2 * B, B)], upper, sems.at[0]),
         pltpu.make_async_copy(received, multipliers, sems.at[1]),
         pltpu.make_async_copy(factors_in.at[rows], target, sems.at[2]),
     ]
@@ -184,56 +184,65 @@
     return lag
 
 
-def update_kernel(step, far, scal, factors_in, cur_in, upper_in, received, factors, cur, following,
+def update_kernel(step, far, scal, factors_in, cur_in, following_in, upper_in, received, factors, cur, following,
                   upper, multipliers, target, high, low, sems):
     panel = scal[0]
-    source = step - lag_of(step, FAR if far else NEAR, panel)
-    rows = pl.ds(pl.multiple_of((source + 1) * SHARE, SHARE), TALL)
-    load = [
-        pltpu.make_async_copy(upper_in, upper, sems.at[0]),
-        pltpu.make_async_copy(received, multipliers, sems.at[1]),
-        pltpu.make_async_copy(factors_in.at[rows], target, sems.at[2]),
-    ]
-    for copy in load:
-        copy.start()
-    load[0].wait()
-    split_into(upper, high, low)
-    load[1].wait()
-    if far:
-        keep = pltpu.make_async_copy(multipliers, cur, sems.at[3])
-        keep.start()
-    load[2].wait()
-    chunk = 128
-
-    def subtract(index, _):
-        block = pl.ds(pl.multiple_of(index * chunk, chunk), chunk)
-        target[block] = target[block] - dot3(split(multipliers[block]), (high[...], low[...]))
-        return 0
-
-    lax.fori_loop(0, TALL // chunk, subtract, 0)
-    head = pl.ds(0, SHARE)
-    tail = pl.ds(SHARE, TALL - SHARE)
-    after = pl.ds(pl.multiple_of((source + 2) * SHARE, SHARE), TALL - SHARE)
-
-    def put_head():
-        first = pl.ds(pl.multiple_of((source + 1) * SHARE, SHARE), SHARE)
-        store = [
-            pltpu.make_async_copy(target.at[head], following, sems.at[0]),
-            pltpu.make_async_copy(target.at[head], factors.at[first], sems.at[2]),
+    table = FAR if far else NEAR
+    source = step - lag_of(step, table, panel)
+    takes = jnp.bool_(False)
+    for distance, (amount, _) in table.items():
+        if step - amount >= 0:
+            takes = takes | (panel == step + distance)
+
+    @pl.when(takes)
+    def _():
+        rows = pl.ds(pl.multiple_of((source + 1) * SHARE, SHARE), TALL)
+        slot = pl.ds(pl.multiple_of(lax.rem(source, 2) * B, B), B)
+        load = [
+            pltpu.make_async_copy(upper_in.at[slot], upper, sems.at[0]),
+            pltpu.make_async_copy(received, multipliers, sems.at[1]),
+            pltpu.make_async_copy(factors_in.at[rows], target, sems.at[2]),
         ]
-        for copy in store:
+        for copy in load:
             copy.start()
-        for copy in store:
-            copy.wait()
-
-    rest = pltpu.make_async_copy(target.at[tail], factors.at[after], sems.at[1])
-    rest.start()
-    if far:
-        pl.when(panel != step + 2)(put_head)
-        keep.wait()
-    else:
-        put_head()
-    rest.wait()
+        load[0].wait()
+        split_into(upper, high, low)
+        load[1].wait()
+        if far:
+            keep = pltpu.make_async_copy(multipliers, cur, sems.at[3])
+            keep.start()
+        load[2].wait()
+        chunk = 128
+
+        def subtract(index, _):
+            block = pl.ds(pl.multiple_of(index * chunk, chunk), chunk)
+            target[block] = target[block] - dot3(split(multipliers[block]), (high[...], low[...]))
+            return 0
+
+        lax.fori_loop(0, TALL // chunk, subtract, 0)
+        head = pl.ds(0, SHARE)
+        tail = pl.ds(SHARE, TALL - SHARE)
+        after = pl.ds(pl.multiple_of((source + 2) * SHARE, SHARE), TALL - SHARE)
+
+        def put_head():
+            first = pl.ds(pl.multiple_of((source + 1) * SHARE, SHARE), SHARE)
+            store = [
+                pltpu.make_async_copy(target.at[head], following, sems.at[0]),
+                pltpu.make_async_copy(target.at[head], factors.at[first], sems.at[2]),
+            ]
+            for copy in store:
+                copy.start()
+            for copy in store:
+                copy.wait()
+
+        rest = pltpu.make_async_copy(target.at[tail], factors.at[after], sems.at[1])
+        rest.start()
+        if far:
+            pl.when(panel != step + 2)(put_head)
+            keep.wait()
+        else:
+            put_head()
+        rest.wait()
 
 
 def place_kernel(scal, factors_in, upper_in, pivot_ref, *rest):
@@ -253,7 +262,8 @@
         copy.start()
     for copy in load:
         copy.wait()
-    keep = pltpu.make_async_copy(upper, upper_out, sems.at[0])
+    slot = pl.ds(pl.multiple_of(lax.rem(source, 2) * B, B), B)
+    keep = pltpu.make_async_copy(upper, upper_out.at[slot], sems.at[0])
     keep.start()
     lanes = lax.broadcasted_iota(jnp.int32, (SHARE, 128), 1)
     swapped[...] = jnp.zeros_like(swapped)
@@ -301,9 +311,9 @@
     )(*first, *operands)
 
 
-def inverse(pivot, y_high, y_low):
+def inverse(owner, pivot, y_high, y_low):
     scratch = [f32(B, B)] + [b16(B, B)] * 6 + [f32(B, B), pltpu.SemaphoreType.DMA((3,))]
-    return call(inverse_kernel, like(y_high, y_low), scratch, {}, pivot, y_high, y_low)
+    return call(functools.partial(inverse_kernel, owner), like(y_high, y_low), scratch, {}, pivot, y_high, y_low)
 
 
 def multiply(owner, factors, cur, front, upper, received, high, low):
@@ -317,16 +327,17 @@
     return call(functools.partial(front_kernel, step), like(following), scratch, {}, factors, upper, received)[0]
 
 
+def near_kernel(step, far, scal, factors_in, following_in, upper_in, received, factors, following, *scratch):
+    update_kernel(step, far, scal, factors_in, None, following_in, upper_in, received, factors, None, following, *scratch)
+
+
 def update(step, far, scal, factors, cur, following, upper, received):
     scratch = [f32(B, B), f32(TALL, B), f32(TALL, B), b16(B, B), b16(B, B), pltpu.SemaphoreType.DMA((4,))]
-    outs = like(factors, cur, following) if far else like(factors, following)
-    kernel = functools.partial(update_kernel if far else near_kernel, step, far)
-    return call(kernel, outs, scratch, {1: 0, 2: 1} if far else {1: 0}, factors, cur, upper, received, scal=scal) if far else call(
-        kernel, outs, scratch, {1: 0}, factors, upper, received, scal=scal)
-
-
-def near_kernel(step, far, scal, factors_in, upper_in, received, factors, following, *scratch):
-    update_kernel(step, far, scal, factors_in, None, upper_in, received, factors, None, following, *scratch)
+    if far:
+        return call(functools.partial(update_kernel, step, far), like(factors, cur, following), scratch,
+                    {1: 0, 2: 1, 3: 2}, factors, cur, following, upper, received, scal=scal)
+    return call(functools.partial(near_kernel, step, far), like(factors, following), scratch,
+                {1: 0, 2: 1}, factors, following, upper, received, scal=scal)
 
 
 def put_in_place(scal, factors, upper, picks, parts):
@@ -409,78 +420,86 @@
     def collect(source, factors, upper, following):
         return put_in_place(jnp.stack([panel, place, source]), factors, upper, picks, gather(following))
 
-    upper = jnp.zeros((B, B), jnp.float32)
-    fresh = jnp.zeros((B, B), jnp.float32)
+    upper = jnp.zeros((2 * B, B), jnp.float32)
 
     def prepare(factors, upper):
         return collect(0, factors, upper, following)
 
-    factors, upper = when([0, 1], prepare, factors, upper)
+    factors, upper = when([0, 1, 2], prepare, factors, upper)
 
     def begin(factors, cur, front):
-        return multiply(0, factors, cur, front, upper, cur, *inverse(upper, y_high, y_low))
+        return multiply(0, factors, cur, front, upper, cur, *inverse(0, upper, y_high, y_low))
 
     factors, cur, front = when([0], begin, factors, cur, front)
 
+    high, low = y_high, y_low
+    bulk = jnp.zeros((TALL, B), jnp.float32)
     for step in range(PANELS - 1):
         coming = step + 1
+        near, near_inside = members(step, [NEAR])
+        far, far_inside = members(step, [FAR])
+
+        def approach(factors, upper, following):
+            p = send(cur, step, NEAR)
+            source = step - lag_of(step, NEAR, panel)
+
+            def bring(factors, upper):
+                return collect(source, factors, upper, following)
+
+            factors, upper = when(near, bring, factors, upper)
+            factors, following = update(step, False, where, factors, cur, following, upper, p)
+
+            def again(factors, upper):
+                return collect(source + 1, factors, upper, following)
+
+            factors, upper = when(sorted(set(near) & set(far)), again, factors, upper)
+            return factors, upper, following
+
+        factors, upper, following = when(near_inside, approach, factors, upper, following)
 
         def lead(following):
             arrived = lax.ppermute(front, ("col", "row"), shifted(1, step % 2))
             return (advance(step, factors, following, upper, arrived),)
 
         (following,) = when([step, coming], lead, following)
-        near, _ = members(step, [NEAR])
-        far, _ = members(step, [FAR])
-        _, inside = members(step, [NEAR, FAR])
-
-        def exchange(factors, cur, front, upper, fresh, following):
-            p = send(cur, step, NEAR)
+
+        def second(following):
+            arrived = lax.ppermute(front, ("col", "row"), shifted(2, step // 2 % 2))
+            return (advance(step, factors, following, upper, arrived),)
+
+        if far:
+            (following,) = when([step, step + 2], second, following)
+
+        def exchange(factors, cur, front, upper, following, bulk, high, low):
             q = send(cur, step, FAR) if far else None
-            source = jnp.where(
-                panel == coming, coming, jnp.maximum(step - lag_of(step, FAR | NEAR, panel), 0)
-            )
-
-            def bring(factors, fresh):
-                return collect(source, factors, fresh, following)
-
-            factors, fresh = when(sorted(set(near) | set(far)), bring, factors, fresh)
-            high, low = inverse(fresh, y_high, y_low)
-
-            def near_update(factors, following):
-                return update(step, False, where, factors, cur, following, fresh, p)
-
-            factors, following = when([c for c in near if c != coming], near_update, factors, following)
-
-            def again(factors, fresh):
-                return collect(step + 1 - lag_of(step, NEAR, panel), factors, fresh, following)
-
-            factors, fresh = when(sorted(set(near) & set(far)), again, factors, fresh)
+            source = jnp.where(panel <= step + 2, coming, jnp.maximum(step - lag_of(step, FAR, panel), 0))
+
+            def bring(factors, upper):
+                return collect(source, factors, upper, following)
+
+            factors, upper = when(sorted(set(far) - set(near) | set(far) & {step + 2} | {coming}), bring, factors, upper)
+
+            def critical(bulk, high, low):
+                bulk = lax.ppermute(cur, ("col", "row"), shifted(1, step % 2))
+                high, low = inverse(coming, upper, y_high, y_low)
+                return bulk, high, low
+
+            bulk, high, low = when([step, coming], critical, bulk, high, low)
             if far:
-                def second(following):
-                    arrived = lax.ppermute(front, ("col", "row"), shifted(2, step // 2 % 2))
-                    return (advance(step, factors, following, fresh, arrived),)
-
-                (following,) = when([step, step + 2], second, following)
-
-                def ahead(factors, upper):
-                    return collect(coming, factors, upper, following)
-
-                factors, upper = when([step + 2], ahead, factors, upper)
-
-            def far_update(factors, cur, following):
-                return update(step, True, where, factors, cur, following, fresh, q)
-
-            factors, cur, following = when(far, far_update, factors, cur, following)
+                def far_update(factors, cur, following):
+                    return update(step, True, where, factors, cur, following, upper, q)
+
+                factors, cur, following = when(far, far_update, factors, cur, following)
 
             def own(factors, cur, front):
-                return multiply(coming, factors, cur, front, upper, p, high, low)
+                return multiply(coming, factors, cur, front, upper, bulk, high, low)
 
             factors, cur, front = when([coming], own, factors, cur, front)
-            return factors, cur, front, upper, fresh, following
-
-        factors, cur, front, upper, fresh, following = when(
-            inside, exchange, factors, cur, front, upper, fresh, following
+            return factors, cur, front, upper, following, bulk, high, low
+
+        inside = sorted(set(far_inside) | {step, coming})
+        factors, cur, front, upper, following, bulk, high, low = when(
+            inside, exchange, factors, cur, front, upper, following, bulk, high, low
         )
     at = (panel + 1) * SHARE
     own = lax.dynamic_slice_in_dim(factors, at, TALL, 0)

time: 1140 us -> 1400 us (1.23)
  waiting for transfers between devices: 807 us -> 1090 us
  Pallas kernels: 122 us -> 85 us
  loops' own time: 61.7 us -> 77.6 us
    ppermute x11 -> x7, waiting for transfers between devices: 760 us -> 1030 us  [send(): return lax.ppermute(cur, ('col', 'row'), pairs)]
    pallas_call x26 -> x21, Pallas kernels: 122 us -> 85 us  [call(): pl.pallas_call(kernel, out_shape=out_shape, in_specs=[SMEM] * len(first)...]
    ppermute x0 -> x1, waiting for transfers between devices: none -> 17.6 us  [critical(): bulk = lax.ppermute(cur, ('col', 'row'), shifted(1, step % 2))]
    another operation x69 -> x84, loops' own time: 61.7 us -> 77.6 us  [when(): lax.cond(among(panel, panels), lambda *state: tuple(run(*state)), lambda...]
  transfers between devices with their start and end apart: 76 -> 73, of which waited for: 51 -> 51; matrix products, arithmetic and copies ran while one was open for 0% -> 0% of each run, Pallas kernels for 8% -> 2%
where the time goes in v5:
time: 1400 us; the launch traced here: 1390 us
  waiting for transfers between devices  1090 us (78%)
  starting transfers between devices  109 us (8%)
  Pallas kernels  85 us (6%)
  loops' own time  77.6 us (6%)
  local copies, waits for them, and re-layouts  25.2 us (2%)
    ppermute x7, waiting for transfers between devices, send(): return lax.ppermute(cur, ('col', 'row'), pairs)  1030 us
    pallas_call x21, Pallas kernels, call(): pl.pallas_call(kernel, out_shape=out_shape, in_specs=[SMEM] * len(first)...  85 us
    another operation x84, loops' own time, when(): lax.cond(among(panel, panels), lambda *state: tuple(run(*state)), lambda...  77.6 us
    ppermute x27, starting transfers between devices, gather(): lax.ppermute(share, 'row', [(r, (r + 2 * turn) % ROWS) for r in range(ROW...  33.3 us
    ppermute x27, starting transfers between devices, gather(): lax.ppermute(part, 'row', swap)  32.9 us
    ppermute x9, starting transfers between devices, gather(): beside = lax.ppermute(share, 'row', swap)  30.2 us
  transfers between devices with their start and end apart: 73, of which 51 were waited for; matrix products, arithmetic and copies ran while one was open for 0% of the time, Pallas kernels for 2%

profile of v5, /device:TPU:31, one launch (start us, length us, event | category | flops | bytes accessed | tf_op | source)
XLA Modules:
  0.0 1389.7 jit_solution(4988948554786440248)
XLA Ops:
  34.0 13.4 conditional.161
  79.0 858.1 %conditional.184 = ((f32[1536,512]{1,0:T(8,128)}, f32[512,512]{1,0:T(8,128)}, f32[64,512]{1,0:T(8,128)S(1)}, f32[1024,512]{1,0:T(8,128)}, f32[64,512]{1,0:T(8,12...) conditional(s32[]{:T(128)} %convert_element_type.432, ...), branch_computations={%region_188.189_spmd, %region_189.198_spmd} | conditional | flops 30 | bytes 12059604 | solution.py:418
  80.4 17.5 %conditional.54 = ((f32[1536,512]{1,0:T(8,128)}, f32[1024,512]{1,0:T(8,128)})) conditional(s32[]{:T(128)} %convert_element_type.339, (f32[1536,512]{1,0:T(8,128)}, f32[1024,512]{1,0:T(8,128)}) %tuple.1002, (s32[]{:T(128)}, s32[]{:T(128)}, pred[]{:T(512)}, pred[]{:T(512)}, pred[]{:T(512)}, /*index=5*/f32[64,512]{1,0:T(8,128)S(1)}, ...), branch_computations={%region_190.190_spmd, %region_191.191_spmd} | conditional | flops 13 | bytes 3670413 | solution.py:418
  97.9 834.2 %collective-permute-done.265 = f32[512,512]{1,0:T(8,128)} collective-permute-done((f32[512,512]{1,0:T(8,128)}, f32[512,512]{1,0:T(8,128)}, u32[]{:S(2)}, u32[]{:S(2)}) %collective-permute-start.265) | collective-permute-done | bytes 1048608 | tf_op jit(solution)/shard_map/cond/branch_1_fun/ppermute | solution.py:363
  948.1 32.2 %conditional.188 = ((f32[1536,512]{1,0:T(8,128)}, f32[512,512]{1,0:T(8,128)}, f32[64,512]{1,0:T(8,128)S(1)}, f32[1024,512]{1,0:T(8,128)}, f32[64,512]{1,0:T(8,12...) conditional(s32[]{:T(128)} %convert_element_type.430, ...), branch_computations={%region_208.209_spmd, %region_209.218_spmd} | conditional | flops 28 | bytes 12059590 | solution.py:418
  949.5 16.0 %conditional.60 = ((f32[1536,512]{1,0:T(8,128)}, f32[1024,512]{1,0:T(8,128)})) conditional(s32[]{:T(128)} %convert_element_type.345, (f32[1536,512]{1,0:T(8,128)}, f32[1024,512]{1,0:T(8,128)}) %tuple.1020, (s32[]{:T(128)}, s32[]{:T(128)}, pred[]{:T(512)}, pred[]{:T(512)}, f32[64,512]{1,0:T(8,128)S(1)}, /*index=5*/f32[1536,512]{1,0:T(8,128)}, ...), branch_computations={%region_210.210_spmd, %region_211.211_spmd} | conditional | flops 14 | bytes 3670422 | solution.py:418
  980.4 33.7 %conditional.189 = ((f32[1536,512]{1,0:T(8,128)}, f32[1024,512]{1,0:T(8,128)}, f32[64,512]{1,0:T(8,128)S(1)})) conditional(s32[]{:T(128)} %convert_element_type.429, (f32[1536,512]{1,0:T(8,128)}, f32[1024,512]{1,0:T(8,128)}, f32[64,512]{1,0:T(8,128)S(1)}) %tuple.1236, (s32[]{:T(128)}, f32[1536,512]{1,0:T(8,128)}, f32[1024,512]{1,0:T(8,128)}, ...), branch_computations={%region_218.219_spmd, %region_219.224_spmd} | conditional | flops 24 | bytes 12059570 | solution.py:418
  981.7 16.9 %conditional.64 = ((f32[1536,512]{1,0:T(8,128)}, f32[1024,512]{1,0:T(8,128)})) conditional(s32[]{:T(128)} %convert_element_type.348, (f32[1536,512]{1,0:T(8,128)}, f32[1024,512]{1,0:T(8,128)}) %tuple.1031, (s32[]{:T(128)}, s32[]{:T(128)}, s32[]{:T(128)}, f32[64,512]{1,0:T(8,128)S(1)}, f32[1536,512]{1,0:T(8,128)}, ...), branch_computations={%region_220.220_spmd, %region_221.221_spmd} | conditional | flops 6 | bytes 3670328 | solution.py:418
  1014.3 114.6 %conditional.193 = ((f32[1536,512]{1,0:T(8,128)}, f32[1024,512]{1,0:T(8,128)}, f32[64,512]{1,0:T(8,128)S(1)})) conditional(s32[]{:T(128)} %convert_element_type.427, (f32[1536,512]{1,0:T(8,128)}, f32[1024,512]{1,0:T(8,128)}, f32[64,512]{1,0:T(8,128)S(1)}) %tuple.1241, (s32[]{:T(128)}, f32[1536,512]{1,0:T(8,128)}, f32[1024,512]{1,0:T(8,128)}, ...), branch_computations={%region_238.239_spmd, %region_239.244_spmd} | conditional | flops 22 | bytes 12059562 | solution.py:418
  1015.6 18.2 %conditional.70 = ((f32[1536,512]{1,0:T(8,128)}, f32[1024,512]{1,0:T(8,128)})) conditional(s32[]{:T(128)} %convert_element_type.353, (f32[1536,512]{1,0:T(8,128)}, f32[1024,512]{1,0:T(8,128)}) %tuple.1049, (s32[]{:T(128)}, s32[]{:T(128)}, s32[]{:T(128)}, f32[64,512]{1,0:T(8,128)S(1)}, f32[1536,512]{1,0:T(8,128)}, ...), branch_computations={%region_240.240_spmd, %region_241.241_spmd} | conditional | flops 6 | bytes 3670328 | solution.py:418
  1033.8 72.4 %collective-permute-done.326.received = f32[512,512]{1,0:T(8,128)S(1)} collective-permute-done((f32[512,512]{1,0:T(8,128)}, f32[512,512]{1,0:T(8,128)S(1)}, u32[]{:S(2)}, u32[]{:S(2)}) %collective-permute-start.326) | collective-permute-done | bytes 1048608 | tf_op jit(solution)/shard_map/cond/branch_1_fun/ppermute | solution.py:363
  1110.9 17.9 %conditional.71 = ((f32[1536,512]{1,0:T(8,128)}, f32[1024,512]{1,0:T(8,128)})) conditional(s32[]{:T(128)} %convert_element_type.353, (f32[1536,512]{1,0:T(8,128)}, f32[1024,512]{1,0:T(8,128)}) %tuple.1051, (s32[]{:T(128)}, s32[]{:T(128)}, s32[]{:T(128)}, f32[64,512]{1,0:T(8,128)S(1)}, f32[1536,512]{1,0:T(8,128)}, ...), branch_computations={%region_242.242_spmd, %region_243.243_spmd} | conditional | flops 7 | bytes 3670340 | solution.py:418
  1128.9 45.5 %conditional.196 = ((f32[1536,512]{1,0:T(8,128)}, f32[512,512]{1,0:T(8,128)}, f32[64,512]{1,0:T(8,128)S(1)}, f32[1024,512]{1,0:T(8,128)}, f32[64,512]{1,0:T(8,12...) conditional(s32[]{:T(128)} %convert_element_type.426, ...), branch_computations={%region_248.249_spmd, %region_249.258_spmd} | conditional | flops 26 | bytes 12059576 | solution.py:418
  1130.2 39.2 %collective-permute-done.334 = f32[512,512]{1,0:T(8,128)} collective-permute-done((f32[512,512]{1,0:T(8,128)}, f32[512,512]{1,0:T(8,128)}, u32[]{:S(2)}, u32[]{:S(2)}) %collective-permute-start.334) | collective-permute-done | bytes 1048608 | tf_op jit(solution)/shard_map/cond/branch_1_fun/ppermute | solution.py:363
  1174.4 98.4 %conditional.197 = ((f32[1536,512]{1,0:T(8,128)}, f32[1024,512]{1,0:T(8,128)}, f32[64,512]{1,0:T(8,128)S(1)})) conditional(s32[]{:T(128)} %convert_element_type.425, (f32[1536,512]{1,0:T(8,128)}, f32[1024,512]{1,0:T(8,128)}, f32[64,512]{1,0:T(8,128)S(1)}) %tuple.1246, (s32[]{:T(128)}, f32[1536,512]{1,0:T(8,128)}, f32[1024,512]{1,0:T(8,128)}, ...), branch_computations={%region_258.259_spmd, %region_259.264_spmd} | conditional | flops 21 | bytes 12059559 | solution.py:418
  1175.8 17.8 %conditional.76 = ((f32[1536,512]{1,0:T(8,128)}, f32[1024,512]{1,0:T(8,128)})) conditional(s32[]{:T(128)} %convert_element_type.358, (f32[1536,512]{1,0:T(8,128)}, f32[1024,512]{1,0:T(8,128)}) %tuple.1067, (s32[]{:T(128)}, s32[]{:T(128)}, s32[]{:T(128)}, f32[64,512]{1,0:T(8,128)S(1)}, f32[1536,512]{1,0:T(8,128)}, ...), branch_computations={%region_260.260_spmd, %region_261.261_spmd} | conditional | flops 6 | bytes 3670328 | solution.py:418
  1193.6 57.7 %collective-permute-done.349.received = f32[512,512]{1,0:T(8,128)S(1)} collective-permute-done((f32[512,512]{1,0:T(8,128)}, f32[512,512]{1,0:T(8,128)S(1)}, u32[]{:S(2)}, u32[]{:S(2)}) %collective-permute-start.349) | collective-permute-done | bytes 1048608 | tf_op jit(solution)/shard_map/cond/branch_1_fun/ppermute | solution.py:363
  1256.0 16.6 %conditional.77 = ((f32[1536,512]{1,0:T(8,128)}, f32[1024,512]{1,0:T(8,128)})) conditional(s32[]{:T(128)} %convert_element_type.358, (f32[1536,512]{1,0:T(8,128)}, f32[1024,512]{1,0:T(8,128)}) %tuple.1069, (s32[]{:T(128)}, s32[]{:T(128)}, s32[]{:T(128)}, f32[64,512]{1,0:T(8,128)S(1)}, f32[1536,512]{1,0:T(8,128)}, ...), branch_computations={%region_262.262_spmd, %region_263.263_spmd} | conditional | flops 7 | bytes 3670340 | solution.py:418
  1283.1 36.1 %conditional.200 = (f32[1536,512]{1,0:T(8,128)}, f32[512,512]{1,0:T(8,128)}, f32[64,512]{1,0:T(8,128)S(1)}, f32[1024,512]{1,0:T(8,128)}, f32[512,512]{1,0:T(8,12...) conditional(s32[]{:T(128)} %convert_element_type.424, ...), branch_computations={%region_268.269_spmd, %region_269.278_spmd} | conditional | flops 25 | bytes 18351020 | solution.py:418
  1284.4 16.0 %conditional.78 = ((f32[1536,512]{1,0:T(8,128)}, f32[1024,512]{1,0:T(8,128)})) conditional(s32[]{:T(128)} %convert_element_type.361, (f32[1536,512]{1,0:T(8,128)}, f32[1024,512]{1,0:T(8,128)}) %tuple.1077, (s32[]{:T(128)}, s32[]{:T(128)}, f32[64,512]{1,0:T(8,128)S(1)}, f32[1536,512]{1,0:T(8,128)}, f32[1024,512]{1,0:T(8,128)}, ...), branch_computations={%region_270.270_spmd, %region_271.271_spmd} | conditional | flops 16 | bytes 3670440 | solution.py:418
  1328.1 57.7 %conditional.202 = (f32[1536,512]{1,0:T(8,128)}) conditional(s32[]{:T(128)} %convert_element_type.423, f32[1536,512]{1,0:T(8,128)} %get-tuple-element.4816, (s32[]{:T(128)}, f32[1536,512]{1,0:T(8,128)}, f32[1024,512]{1,0:T(8,128)}, s32[]{:T(128)}, f32[64,512]{1,0:T(8,128)S(1)}, /*index=5*/s32[16,64,128]{2,1,0:T(8,128)S(1)}, ...), branch_computations={%region_280.281_spmd, %region_281.288_spmd} | conditional | flops 21 | bytes 20447952 | solution.py:418
  1328.1 21.0 %conditional.82 = (f32[1536,512]{1,0:T(8,128)}, f32[1024,512]{1,0:T(8,128)}, f32[1536,512]{1,0:T(8,128)}) conditional(s32[]{:T(128)} %convert_element_type.363, (f32[1536,512]{1,0:T(8,128)}, f32[1024,512]{1,0:T(8,128)}) %tuple.1090, (s32[]{:T(128)}, s32[]{:T(128)}, f32[64,512]{1,0:T(8,128)S(1)}, f32[1536,512]{1,0:T(8,128)}, ...), branch_computations={%region_282.282_spmd, %region_283.283_spmd} | conditional | flops 16 | bytes 9961912 | solution.py:418
  1349.1 26.6 %conditional.83 = ((f32[512,512]{1,0:T(8,128)}, bf16[512,512]{1,0:T(8,128)(2,1)}, bf16[512,512]{1,0:T(8,128)(2,1)})) conditional(s32[]{:T(128)} %convert_element_type.364, (f32[512,512]{1,0:T(8,128)}, bf16[512,512]{1,0:T(8,128)(2,1)}, bf16[512,512]{1,0:T(8,128)(2,1)}) %tuple.1092, (f32[512,512]{1,0:T(8,128)}, f32[1024,512]{1,0:T(8,128)}, ...), branch_computations={%region_284.284_spmd, %region_285.285_spmd} | conditional | bytes 4194376 | solution.py:418
  1358.1 17.6 %collective-permute-done.43 = f32[512,512]{1,0:T(8,128)} collective-permute-done((f32[512,512]{1,0:T(8,128)}, f32[512,512]{1,0:T(8,128)}, u32[]{:S(2)}, u32[]{:S(2)}) %collective-permute-start.43) | collective-permute-done | bytes 1048608 | tf_op jit(solution)/shard_map/cond/branch_1_fun/cond/branch_1_fun/ppermute | solution.py:483
  (269 shorter events, 407.0 us)
Async XLA Ops:
  79.1 853.1 %collective-permute-start.265 = (f32[512,512]{1,0:T(8,128)}, f32[512,512]{1,0:T(8,128)}, u32[]{:S(2)}, u32[]{:S(2)}) collective-permute-start(f32[512,512]{1,0:T(8,128)} %get-tuple-element.4042), channel_id=1, source_target_pairs={{0,16},{1,17},{2,18},{3,19},{4,20},{5,21},{6,22},{7,23},{16,48},{1... | collective-permute-start | bytes 3145736 | tf_op jit(solution)/shard_map/cond/branch_1_fun/ppermute | solution.py:363
  80.4 7.3 collective-permute-start.258
  82.1 9.0 collective-permute-start.259
  948.2 27.2 %collective-permute-start.288 = (f32[512,512]{1,0:T(8,128)}, f32[512,512]{1,0:T(8,128)}, u32[]{:S(2)}, u32[]{:S(2)}) collective-permute-start(f32[512,512]{1,0:T(8,128)} %get-tuple-element.4139), channel_id=1, source_target_pairs={{8,24},{9,25},{10,26},{11,27},{12,28},{13,29},{14,30},{15,31},{0,3... | collective-permute-start | bytes 3145736 | tf_op jit(solution)/shard_map/cond/branch_1_fun/ppermute | solution.py:363
  950.0 7.6 collective-permute-start.282
  980.4 28.9 %collective-permute-start.303 = (f32[512,512]{1,0:T(8,128)}, f32[512,512]{1,0:T(8,128)S(1)}, u32[]{:S(2)}, u32[]{:S(2)}) collective-permute-start(f32[512,512]{1,0:T(8,128)} %get-tuple-element.4188), channel_id=1, source_target_pairs={{8,32},{9,33},{10,34},{11,35},{12,36},{13,37},{14,38},{15,39},{0,4... | collective-permute-start | bytes 3145736 | tf_op jit(solution)/shard_map/cond/branch_1_fun/ppermute | solution.py:363
  981.7 6.9 collective-permute-start.289
  1014.3 91.9 %collective-permute-start.326 = (f32[512,512]{1,0:T(8,128)}, f32[512,512]{1,0:T(8,128)S(1)}, u32[]{:S(2)}, u32[]{:S(2)}) collective-permute-start(f32[512,512]{1,0:T(8,128)} %get-tuple-element.4284), channel_id=1, source_target_pairs={{16,40},{17,41},{18,42},{19,43},{20,44},{21,45},{22,46},{23,47},{8... | collective-permute-start | bytes 3145736 | tf_op jit(solution)/shard_map/cond/branch_1_fun/ppermute | solution.py:363
  1015.7 8.1 collective-permute-start.312
  1016.2 7.6 collective-permute-start.313
  1111.0 8.2 collective-permute-start.319
  1111.1 8.0 collective-permute-start.320
  1128.9 40.6 %collective-permute-start.334 = (f32[512,512]{1,0:T(8,128)}, f32[512,512]{1,0:T(8,128)}, u32[]{:S(2)}, u32[]{:S(2)}) collective-permute-start(f32[512,512]{1,0:T(8,128)} %get-tuple-element.4331), channel_id=1, source_target_pairs={{24,40},{25,41},{26,42},{27,43},{28,44},{29,45},{30,46},{31,47},{1... | collective-permute-start | bytes 3145736 | tf_op jit(solution)/shard_map/cond/branch_1_fun/ppermute | solution.py:363
  1174.5 76.9 %collective-permute-start.349 = (f32[512,512]{1,0:T(8,128)}, f32[512,512]{1,0:T(8,128)S(1)}, u32[]{:S(2)}, u32[]{:S(2)}) collective-permute-start(f32[512,512]{1,0:T(8,128)} %get-tuple-element.4380), channel_id=1, source_target_pairs={{24,48},{25,49},{26,50},{27,51},{28,52},{29,53},{30,54},{31,55},{1... | collective-permute-start | bytes 3145736 | tf_op jit(solution)/shard_map/cond/branch_1_fun/ppermute | solution.py:363
  1175.8 7.5 collective-permute-start.335
  1176.3 7.0 collective-permute-start.336
  1256.0 7.0 collective-permute-start.342
  1256.2 6.7 collective-permute-start.343
  1272.9 8.2 collective-permute-start.40
  1283.1 27.2 %collective-permute-start.357 = (f32[512,512]{1,0:T(8,128)}, f32[512,512]{1,0:T(8,128)}, u32[]{:S(2)}, u32[]{:S(2)}) collective-permute-start(f32[512,512]{1,0:T(8,128)} %get-tuple-element.4440), channel_id=1, source_target_pairs={{32,48},{33,49},{34,50},{35,51},{36,52},{37,53},{38,54},{39,55},{2... | collective-permute-start | bytes 3145736 | tf_op jit(solution)/shard_map/cond/branch_1_fun/ppermute | solution.py:363
  1285.0 8.2 collective-permute-start.351
  1319.1 6.9 collective-permute-start.42
  1328.1 7.2 collective-permute-start.358
  1349.1 26.6 %collective-permute-start.43 = (f32[512,512]{1,0:T(8,128)}, f32[512,512]{1,0:T(8,128)}, u32[]{:S(2)}, u32[]{:S(2)}) collective-permute-start(f32[512,512]{1,0:T(8,128)} %get-tuple-element.4476), channel_id=1, source_target_pairs={{0,8},{1,9},{2,10},{3,11},{4,12},{5,13},{6,14},{7,15},{16,24},{17,... | collective-permute-start | bytes 3145736 | tf_op jit(solution)/shard_map/cond/branch_1_fun/cond/branch_1_fun/ppermute | solution.py:483
  (53 other events, 247.5 us)

commit v6 on v4

--- a/solution.py
+++ b/solution.py
@@ -161,7 +161,7 @@
     rows = pl.ds((step + 1) * SHARE, SHARE)
     load = [
         pltpu.make_async_copy(upper_in, upper, sems.at[0]),
-        pltpu.make_async_copy(received, multipliers, sems.at[1]),
+        pltpu.make_async_copy(received.at[pl.ds(0, SHARE)], multipliers, sems.at[1]),
         pltpu.make_async_copy(factors_in.at[rows], target, sems.at[2]),
     ]
     for copy in load:
@@ -236,44 +236,60 @@
     rest.wait()
 
 
-def place_kernel(scal, factors_in, upper_in, pivot_ref, *rest):
+def place_kernel(scal, upper_in, *rest):
+    parts, (upper_out, upper, sems) = rest[:8], rest[8:]
     del upper_in
-    parts, (factors, upper_out), (upper, swapped, picks, sems) = rest[:8], rest[8:10], rest[10:]
     place = scal[1]
-    source = scal[2]
     z = place // 2
     core = place % 2
     load = []
     for index, part in enumerate(parts):
         other = core if index < 4 else 1 - core
         offset = (2 * ((z + 4 - index % 4) % 4) + other) * SHARE
-        load.append(pltpu.make_async_copy(part, upper.at[pl.ds(pl.multiple_of(offset, SHARE), SHARE)], sems.at[index]))
-    load.append(pltpu.make_async_copy(pivot_ref.at[source], picks, sems.at[8]))
+        at = pl.ds(pl.multiple_of(offset, SHARE), SHARE)
+        load.append(pltpu.make_async_copy(part, upper.at[at], sems.at[index]))
     for copy in load:
         copy.start()
     for copy in load:
         copy.wait()
     keep = pltpu.make_async_copy(upper, upper_out, sems.at[0])
     keep.start()
-    lanes = lax.broadcasted_iota(jnp.int32, (SHARE, 128), 1)
-    swapped[...] = jnp.zeros_like(swapped)
-
-    def pick_rows(group, _):
-        onehot = jnp.where(picks[...] == lanes + 128 * group, 1.0, 0.0).astype(jnp.bfloat16)
-        block = pl.ds(pl.multiple_of(group * 128, 128), 128)
-        swapped[...] = swapped[...] + exact_rows(onehot, upper[block])
-        return 0
-
-    lax.fori_loop(0, B // 128, pick_rows, 0)
-    at = pl.ds(pl.multiple_of(source * SHARE, SHARE), SHARE)
-    store = pltpu.make_async_copy(swapped, factors.at[at], sems.at[1])
-    store.start()
-    store.wait()
     keep.wait()
+
+
+def swap_kernel(scal, factors_in, upper_in, pivot_ref, factors, upper, swapped, picks, sems):
+    del factors_in
+    source = scal[2]
+
+    @pl.when(source >= 0)
+    def _():
+        load = [
+            pltpu.make_async_copy(upper_in, upper, sems.at[0]),
+            pltpu.make_async_copy(pivot_ref.at[source], picks, sems.at[1]),
+        ]
+        for copy in load:
+            copy.start()
+        for copy in load:
+            copy.wait()
+        lanes = lax.broadcasted_iota(jnp.int32, (SHARE, 128), 1)
+        swapped[...] = jnp.zeros_like(swapped)
+
+        def pick_rows(group, _):
+            onehot = jnp.where(picks[...] == lanes + 128 * group, 1.0, 0.0).astype(jnp.bfloat16)
+            block = pl.ds(pl.multiple_of(group * 128, 128), 128)
+            swapped[...] = swapped[...] + exact_rows(onehot, upper[block])
+            return 0
+
+        lax.fori_loop(0, B // 128, pick_rows, 0)
+        at = pl.ds(pl.multiple_of(source * SHARE, SHARE), SHARE)
+        store = pltpu.make_async_copy(swapped, factors.at[at], sems.at[0])
+        store.start()
+        store.wait()
 
 
 ANY = pl.BlockSpec(memory_space=pl.ANY)
 SMEM = pl.BlockSpec(memory_space=pltpu.SMEM)
+HBM = pl.BlockSpec(memory_space=pltpu.HBM)
 
 
 def f32(*shape):
@@ -286,6 +302,10 @@
 
 def like(*arrays):
     return [jax.ShapeDtypeStruct(a.shape, a.dtype) for a in arrays]
+
+
+def space(array):
+    return HBM if array.shape[0] > TALL else ANY
 
 
 def call(kernel, out_shape, scratch, aliases, *operands, scal=None):
@@ -293,8 +313,8 @@
     return pl.pallas_call(
         kernel,
         out_shape=out_shape,
-        in_specs=[SMEM] * len(first) + [ANY] * len(operands),
-        out_specs=[ANY] * len(out_shape),
+        in_specs=[SMEM] * len(first) + [space(a) for a in operands],
+        out_specs=[space(a) for a in out_shape],
         scratch_shapes=scratch,
         input_output_aliases=aliases,
         compiler_params=pltpu.CompilerParams(vmem_limit_bytes=48 << 20),
@@ -329,9 +349,14 @@
     update_kernel(step, far, scal, factors_in, None, upper_in, received, factors, None, following, *scratch)
 
 
-def put_in_place(scal, factors, upper, picks, parts):
-    scratch = [f32(B, B), f32(SHARE, B), pltpu.VMEM((SHARE, 128), jnp.int32), pltpu.SemaphoreType.DMA((9,))]
-    return call(place_kernel, like(factors, upper), scratch, {1: 0, 2: 1}, factors, upper, picks, *parts, scal=scal)
+def put_in_place(scal, upper, parts):
+    scratch = [f32(B, B), pltpu.SemaphoreType.DMA((8,))]
+    return call(place_kernel, like(upper), scratch, {1: 0}, upper, *parts, scal=scal)[0]
+
+
+def put_swapped(scal, factors, upper, picks):
+    scratch = [f32(B, B), f32(SHARE, B), pltpu.VMEM((SHARE, 128), jnp.int32), pltpu.SemaphoreType.DMA((2,))]
+    return call(swap_kernel, like(factors), scratch, {1: 0}, factors, upper, picks, scal=scal)[0]
 
 
 def gather(share):
@@ -406,14 +431,18 @@
             return state
         return lax.cond(among(panel, panels), lambda *state: tuple(run(*state)), lambda *state: state, *state)
 
-    def collect(source, factors, upper, following):
-        return put_in_place(jnp.stack([panel, place, source]), factors, upper, picks, gather(following))
+    def collect(upper, following):
+        return put_in_place(where, upper, gather(following))
+
+    def store_swapped(source, factors, upper):
+        return put_swapped(jnp.stack([panel, place, source]), factors, upper, picks)
 
     upper = jnp.zeros((B, B), jnp.float32)
     fresh = jnp.zeros((B, B), jnp.float32)
 
     def prepare(factors, upper):
-        return collect(0, factors, upper, following)
+        upper = collect(upper, following)
+        return store_swapped(jnp.int32(0), factors, upper), upper
 
     factors, upper = when([0, 1], prepare, factors, upper)
 
@@ -437,15 +466,18 @@
         def exchange(factors, cur, front, upper, fresh, following):
             p = send(cur, step, NEAR)
             q = send(cur, step, FAR) if far else None
-            source = jnp.where(
-                panel == coming, coming, jnp.maximum(step - lag_of(step, FAR | NEAR, panel), 0)
-            )
-
-            def bring(factors, fresh):
-                return collect(source, factors, fresh, following)
-
-            factors, fresh = when(sorted(set(near) | set(far)), bring, factors, fresh)
+            source = jnp.maximum(step - lag_of(step, FAR | NEAR, panel), 0)
+            takers = sorted(set(near) | set(far))
+
+            (fresh,) = when(takers, lambda fresh: (collect(fresh, following),), fresh)
             high, low = inverse(fresh, y_high, y_low)
+            others = [c for c in takers if c != coming]
+            mine = panel == step
+            stored = jnp.where(among(panel, others), source, -1) if others else jnp.int32(-1)
+            if step:
+                stored = jnp.where(mine, step, stored)
+                factors = store_swapped(jnp.where(mine, step - 1, -1), factors, upper)
+            factors = store_swapped(stored, factors, fresh)
 
             def near_update(factors, following):
                 return update(step, False, where, factors, cur, following, fresh, p)
@@ -453,25 +485,23 @@
             factors, following = when([c for c in near if c != coming], near_update, factors, following)
 
             def again(factors, fresh):
-                return collect(step + 1 - lag_of(step, NEAR, panel), factors, fresh, following)
+                fresh = collect(fresh, following)
+                return store_swapped(source + 1, factors, fresh), fresh
 
             factors, fresh = when(sorted(set(near) & set(far)), again, factors, fresh)
-            if far:
-                def second(following):
-                    arrived = lax.ppermute(front, ("col", "row"), shifted(2, step // 2 % 2))
-                    return (advance(step, factors, following, fresh, arrived),)
-
-                (following,) = when([step, step + 2], second, following)
-
-                def ahead(factors, upper):
-                    return collect(coming, factors, upper, following)
-
-                factors, upper = when([step + 2], ahead, factors, upper)
+
+            def far_next(factors, cur, upper, following):
+                row = advance(step, factors, following, fresh, q)
+                parts = gather(row)
+                factors, cur, following = update(step, True, where, factors, cur, following, fresh, q)
+                return factors, cur, put_in_place(where, upper, parts), following
 
             def far_update(factors, cur, following):
                 return update(step, True, where, factors, cur, following, fresh, q)
 
-            factors, cur, following = when(far, far_update, factors, cur, following)
+            if far:
+                factors, cur, upper, following = when([step + 2], far_next, factors, cur, upper, following)
+                factors, cur, following = when([c for c in far if c != step + 2], far_update, factors, cur, following)
 
             def own(factors, cur, front):
                 return multiply(coming, factors, cur, front, upper, p, high, low)
@@ -482,6 +512,9 @@
         factors, cur, front, upper, fresh, following = when(
             inside, exchange, factors, cur, front, upper, fresh, following
         )
+    last = PANELS - 1
+    factors = store_swapped(jnp.where(panel == last, last, -1), factors, fresh)
+    factors = store_swapped(jnp.where(panel == last, last - 1, -1), factors, upper)
     at = (panel + 1) * SHARE
     own = lax.dynamic_slice_in_dim(factors, at, TALL, 0)
     own = lax.dot_general(

time: 1140 us -> 1120 us (0.982)
  waiting for transfers between devices: 807 us -> 754 us
  Pallas kernels: 122 us -> 151 us
    ppermute x11, waiting for transfers between devices: 760 us -> 726 us  [send(): return lax.ppermute(cur, ('col', 'row'), pairs)]
    pallas_call x26 -> x42, Pallas kernels: 122 us -> 151 us  [call(): pl.pallas_call(kernel, out_shape=out_shape, in_specs=[SMEM] * len(first)...]
    ppermute x1 -> x0, waiting for transfers between devices: 15.2 us -> none  [second(): arrived = lax.ppermute(front, ('col', 'row'), shifted(2, step // 2 % 2))]
    another operation x69 -> x63, loops' own time: 61.7 us -> 62.7 us  [when(): lax.cond(among(panel, panels), lambda *state: tuple(run(*state)), lambda...]
  transfers between devices with their start and end apart: 76 -> 75, of which waited for: 51 -> 34; matrix products, arithmetic and copies ran while one was open for 0% -> 2% of each run, Pallas kernels for 8% -> 11%
where the time goes in v6:
time: 1120 us; the launch traced here: 1110 us
  waiting for transfers between devices  754 us (67%)
  Pallas kernels  151 us (13%)
  starting transfers between devices  105 us (9%)
  loops' own time  62.7 us (6%)
  local copies, waits for them, and re-layouts  31.3 us (3%)
    ppermute x11, waiting for transfers between devices, send(): return lax.ppermute(cur, ('col', 'row'), pairs)  726 us
    pallas_call x42, Pallas kernels, call(): pl.pallas_call(kernel, out_shape=out_shape, in_specs=[SMEM] * len(first)...  151 us
    another operation x63, loops' own time, when(): lax.cond(among(panel, panels), lambda *state: tuple(run(*state)), lambda...  62.7 us
    ppermute x27, starting transfers between devices, gather(): lax.ppermute(share, 'row', [(r, (r + 2 * turn) % ROWS) for r in range(ROW...  33.6 us
    ppermute x27, starting transfers between devices, gather(): lax.ppermute(part, 'row', swap)  31.2 us
    ppermute x9, starting transfers between devices, gather(): beside = lax.ppermute(share, 'row', swap)  23.3 us
  transfers between devices with their start and end apart: 75, of which 34 were waited for; matrix products, arithmetic and copies ran while one was open for 2% of the time, Pallas kernels for 11%

profile of v6, /device:TPU:31, one launch (start us, length us, event | category | flops | bytes accessed | tf_op | source)
XLA Modules:
  0.0 1109.3 jit_solution(13245138727678725719)
XLA Ops:
  12.6 15.1 %conditional.121 = ((f32[1536,512]{1,0:T(8,128)}, f32[512,512]{1,0:T(8,128)}, f32[64,512]{1,0:T(8,128)S(1)}, f32[512,512]{1,0:T(8,128)}, f32[512,512]{1,0:T(8,128)}, /*index=5*/f32[64,512]{1,0:T(8,128)S(1)})) conditional(s32[]{:T(128)} %convert_element_type.339, (f32[1536,512]{1,0:T(8,128)}, f32[512,512]{1,0:T(8,128)}, f32[64,512]{1,0:T(8,128)S(1)}, ...), branch_computations={%region_32.33_spmd, %region_33.46_spmd} | conditional | flops 53 | bytes 21497614 | solution.py:432
  27.9 15.1 %conditional.125 = ((f32[1536,512]{1,0:T(8,128)}, f32[512,512]{1,0:T(8,128)}, f32[64,512]{1,0:T(8,128)S(1)}, f32[512,512]{1,0:T(8,128)}, f32[512,512]{1,0:T(8,128)}, /*index=5*/f32[64,512]{1,0:T(8,128)S(1)})) conditional(s32[]{:T(128)} %convert_element_type.337, (f32[1536,512]{1,0:T(8,128)}, f32[512,512]{1,0:T(8,128)}, f32[64,512]{1,0:T(8,128)S(1)}, ...), branch_computations={%region_64.65_spmd, %region_65.78_spmd} | conditional | flops 53 | bytes 21497614 | solution.py:432
  43.1 14.9 %conditional.129 = ((f32[1536,512]{1,0:T(8,128)}, f32[512,512]{1,0:T(8,128)}, f32[64,512]{1,0:T(8,128)S(1)}, f32[512,512]{1,0:T(8,128)}, f32[512,512]{1,0:T(8,128)}, /*index=5*/f32[64,512]{1,0:T(8,128)S(1)})) conditional(s32[]{:T(128)} %convert_element_type.335, (f32[1536,512]{1,0:T(8,128)}, f32[512,512]{1,0:T(8,128)}, f32[64,512]{1,0:T(8,128)S(1)}, ...), branch_computations={%region_96.97_spmd, %region_97.110_spmd} | conditional | flops 53 | bytes 21497614 | solution.py:432
  58.1 15.1 %conditional.133 = ((f32[1536,512]{1,0:T(8,128)}, f32[512,512]{1,0:T(8,128)}, f32[64,512]{1,0:T(8,128)S(1)}, f32[512,512]{1,0:T(8,128)}, f32[512,512]{1,0:T(8,128)}, /*index=5*/f32[64,512]{1,0:T(8,128)S(1)})) conditional(s32[]{:T(128)} %convert_element_type.333, (f32[1536,512]{1,0:T(8,128)}, f32[512,512]{1,0:T(8,128)}, ...), branch_computations={%region_128.129_spmd, %region_129.142_spmd} | conditional | flops 53 | bytes 21497614 | solution.py:432
  73.3 607.7 %conditional.135 = ((f32[1536,512]{1,0:T(8,128)}, f32[512,512]{1,0:T(8,128)}, f32[64,512]{1,0:T(8,128)S(1)}, f32[512,512]{1,0:T(8,128)}, f32[512,512]{1,0:T(8,128)}, /*index=5*/f32[64,512]{1,0:T(8,128)S(1)})) conditional(s32[]{:T(128)} %convert_element_type.332, (f32[1536,512]{1,0:T(8,128)}, f32[512,512]{1,0:T(8,128)}, ...), branch_computations={%region_144.145_spmd, %region_145.158_spmd} | conditional | flops 53 | bytes 21497614 | solution.py:432
  74.9 16.7 %conditional.51 = (f32[512,512]{1,0:T(8,128)}) conditional(s32[]{:T(128)} %convert_element_type.275, f32[512,512]{1,0:T(8,128)} %get-tuple-element.2934, (f32[64,512]{1,0:T(8,128)S(1)}, s32[2]{0:T(128)S(1)}, f32[512,512]{1,0:T(8,128)}) %tuple.753), branch_computations={%region_146.146_spmd, %region_147.147_spmd} | conditional | bytes 3670304 | solution.py:432
  104.9 571.2 %collective-permute-done.307 = f32[512,512]{1,0:T(8,128)} collective-permute-done((f32[512,512]{1,0:T(8,128)}, f32[512,512]{1,0:T(8,128)}, u32[]{:S(2)}, u32[]{:S(2)}) %collective-permute-start.307) | collective-permute-done | bytes 1048608 | tf_op jit(solution)/shard_map/cond/branch_1_fun/ppermute | solution.py:377
  681.1 81.1 %conditional.137 = ((f32[1536,512]{1,0:T(8,128)}, f32[512,512]{1,0:T(8,128)}, f32[64,512]{1,0:T(8,128)S(1)}, f32[512,512]{1,0:T(8,128)}, f32[512,512]{1,0:T(8,128)}, /*index=5*/f32[64,512]{1,0:T(8,128)S(1)})) conditional(s32[]{:T(128)} %convert_element_type.331, (f32[1536,512]{1,0:T(8,128)}, f32[512,512]{1,0:T(8,128)}, ...), branch_computations={%region_160.161_spmd, %region_161.174_spmd} | conditional | flops 50 | bytes 21497604 | solution.py:432
  682.7 15.3 %conditional.57 = (f32[512,512]{1,0:T(8,128)}) conditional(s32[]{:T(128)} %convert_element_type.281, f32[512,512]{1,0:T(8,128)} %get-tuple-element.3012, (f32[64,512]{1,0:T(8,128)S(1)}, s32[2]{0:T(128)S(1)}, f32[512,512]{1,0:T(8,128)}) %tuple.770), branch_computations={%region_162.162_spmd, %region_163.163_spmd} | conditional | bytes 3670304 | solution.py:432
  711.2 45.5 %collective-permute-done.316 = f32[512,512]{1,0:T(8,128)} collective-permute-done((f32[512,512]{1,0:T(8,128)}, f32[512,512]{1,0:T(8,128)}, u32[]{:S(2)}, u32[]{:S(2)}) %collective-permute-start.316) | collective-permute-done | bytes 1048608 | tf_op jit(solution)/shard_map/cond/branch_1_fun/ppermute | solution.py:377
  762.2 44.5 %conditional.139 = ((f32[1536,512]{1,0:T(8,128)}, f32[512,512]{1,0:T(8,128)}, f32[64,512]{1,0:T(8,128)S(1)}, f32[512,512]{1,0:T(8,128)}, f32[512,512]{1,0:T(8,128)}, /*index=5*/f32[64,512]{1,0:T(8,128)S(1)})) conditional(s32[]{:T(128)} %convert_element_type.330, (f32[1536,512]{1,0:T(8,128)}, f32[512,512]{1,0:T(8,128)}, ...), branch_computations={%region_176.177_spmd, %region_177.190_spmd} | conditional | flops 47 | bytes 25691892 | solution.py:432
  763.5 17.6 %conditional.63 = (f32[512,512]{1,0:T(8,128)}) conditional(s32[]{:T(128)} %convert_element_type.287, f32[512,512]{1,0:T(8,128)} %get-tuple-element.3090, (f32[64,512]{1,0:T(8,128)S(1)}, s32[2]{0:T(128)S(1)}, f32[512,512]{1,0:T(8,128)}) %tuple.787), branch_computations={%region_178.178_spmd, %region_179.179_spmd} | conditional | bytes 5767456 | solution.py:432
  806.7 116.4 %conditional.141 = ((f32[1536,512]{1,0:T(8,128)}, f32[512,512]{1,0:T(8,128)}, f32[64,512]{1,0:T(8,128)S(1)}, f32[512,512]{1,0:T(8,128)}, f32[512,512]{1,0:T(8,128)}, /*index=5*/f32[64,512]{1,0:T(8,128)S(1)})) conditional(s32[]{:T(128)} %convert_element_type.329, (f32[1536,512]{1,0:T(8,128)}, f32[512,512]{1,0:T(8,128)}, ...), branch_computations={%region_192.193_spmd, %region_193.206_spmd} | conditional | flops 44 | bytes 25691880 | solution.py:432
  808.0 18.2 %conditional.69 = (f32[512,512]{1,0:T(8,128)}) conditional(s32[]{:T(128)} %convert_element_type.292, f32[512,512]{1,0:T(8,128)} %get-tuple-element.3168, (f32[64,512]{1,0:T(8,128)S(1)}, s32[2]{0:T(128)S(1)}, f32[512,512]{1,0:T(8,128)}) %tuple.804), branch_computations={%region_194.194_spmd, %region_195.195_spmd} | conditional | bytes 5767456 | solution.py:432
  839.4 35.4 %collective-permute-done.333 = f32[512,512]{1,0:T(8,128)} collective-permute-done((f32[512,512]{1,0:T(8,128)}, f32[512,512]{1,0:T(8,128)}, u32[]{:S(2)}, u32[]{:S(2)}) %collective-permute-start.333) | collective-permute-done | bytes 1048608 | tf_op jit(solution)/shard_map/cond/branch_1_fun/ppermute | solution.py:377
  879.8 21.2 %conditional.71 = (f32[1536,512]{1,0:T(8,128)}, f32[512,512]{1,0:T(8,128)}) conditional(s32[]{:T(128)} %convert_element_type.291, (f32[1536,512]{1,0:T(8,128)}, f32[512,512]{1,0:T(8,128)}) %tuple.807, (s32[]{:T(128)}, s32[]{:T(128)}, s32[]{:T(128)}, f32[64,512]{1,0:T(8,128)S(1)}, s32[2]{0:T(128)S(1)}, /*index=5*/f32[512,512]{1,0:T(8,128)}, ...), branch_computations={%region_198.198_spmd, %region_199.199_spmd} | conditional | flops 7 | bytes 5767500 | solution.py:432
  901.0 16.9 %collective-permute-done.334 = f32[512,512]{1,0:T(8,128)} collective-permute-done((f32[512,512]{1,0:T(8,128)}, f32[512,512]{1,0:T(8,128)}, u32[]{:S(2)}, u32[]{:S(2)}) %collective-permute-start.334) | collective-permute-done | bytes 1048608 | tf_op jit(solution)/shard_map/cond/branch_1_fun/ppermute | solution.py:377
  923.2 132.4 %conditional.143 = ((f32[1536,512]{1,0:T(8,128)}, f32[512,512]{1,0:T(8,128)}, f32[64,512]{1,0:T(8,128)S(1)}, f32[512,512]{1,0:T(8,128)}, f32[512,512]{1,0:T(8,128)}, /*index=5*/f32[64,512]{1,0:T(8,128)S(1)})) conditional(s32[]{:T(128)} %convert_element_type.328, (f32[1536,512]{1,0:T(8,128)}, f32[512,512]{1,0:T(8,128)}, ...), branch_computations={%region_208.209_spmd, %region_209.220_spmd} | conditional | flops 40 | bytes 25691792 | solution.py:432
  924.5 17.4 %conditional.75 = (f32[512,512]{1,0:T(8,128)}) conditional(s32[]{:T(128)} %convert_element_type.295, f32[512,512]{1,0:T(8,128)} %get-tuple-element.3241, (f32[64,512]{1,0:T(8,128)S(1)}, s32[2]{0:T(128)S(1)}, f32[512,512]{1,0:T(8,128)}) %tuple.821), branch_computations={%region_210.210_spmd, %region_211.211_spmd} | conditional | bytes 5767456 | solution.py:432
  955.1 39.9 %collective-permute-done.342 = f32[512,512]{1,0:T(8,128)} collective-permute-done((f32[512,512]{1,0:T(8,128)}, f32[512,512]{1,0:T(8,128)}, u32[]{:S(2)}, u32[]{:S(2)}) %collective-permute-start.342) | collective-permute-done | bytes 1048608 | tf_op jit(solution)/shard_map/cond/branch_1_fun/ppermute | solution.py:377
  1000.0 20.5 %conditional.77 = (f32[1536,512]{1,0:T(8,128)}, f32[512,512]{1,0:T(8,128)}) conditional(s32[]{:T(128)} %convert_element_type.294, (f32[1536,512]{1,0:T(8,128)}, f32[512,512]{1,0:T(8,128)}) %tuple.824, (s32[]{:T(128)}, s32[]{:T(128)}, s32[]{:T(128)}, f32[64,512]{1,0:T(8,128)S(1)}, s32[2]{0:T(128)S(1)}, /*index=5*/f32[512,512]{1,0:T(8,128)}, ...), branch_computations={%region_214.214_spmd, %region_215.215_spmd} | conditional | flops 7 | bytes 5767500 | solution.py:432
  1034.0 21.5 %conditional.78 = ((f32[1536,512]{1,0:T(8,128)}, f32[512,512]{1,0:T(8,128)}, f32[512,512]{1,0:T(8,128)}, f32[64,512]{1,0:T(8,128)S(1)})) conditional(s32[]{:T(128)} %convert_element_type.294, (f32[1536,512]{1,0:T(8,128)}, f32[512,512]{1,0:T(8,128)}, f32[512,512]{1,0:T(8,128)}, f32[64,512]{1,0:T(8,128)S(1)}) %tuple.826, (s32[2]{0:T(128)S(1)}, ...), branch_computations={%region_216.216_spmd, %region_217.217_spmd} | conditional | bytes 3670336 | solution.py:432
  1064.6 34.0 %conditional.145 = ((f32[1536,512]{1,0:T(8,128)}, f32[512,512]{1,0:T(8,128)})) conditional(s32[]{:T(128)} %convert_element_type.327, (f32[1536,512]{1,0:T(8,128)}, f32[512,512]{1,0:T(8,128)}) %tuple.926, (s32[]{:T(128)}, s32[]{:T(128)}, f32[1536,512]{1,0:T(8,128)}, f32[512,512]{1,0:T(8,128)}, s32[16,64,128]{2,1,0:T(8,128)S(1)}, ...), branch_computations={%region_222.223_spmd, %region_223.228_spmd} | conditional | flops 17 | bytes 12059153 | solution.py:432
  1065.9 16.4 %conditional.80 = (f32[512,512]{1,0:T(8,128)}) conditional(s32[]{:T(128)} %convert_element_type.296, f32[512,512]{1,0:T(8,128)} %get-tuple-element.3283, (f32[64,512]{1,0:T(8,128)S(1)}, s32[2]{0:T(128)S(1)}, f32[512,512]{1,0:T(8,128)}) %tuple.832), branch_computations={%region_224.224_spmd, %region_225.225_spmd} | conditional | bytes 5767456 | solution.py:432
  (286 shorter events, 386.9 us)
Async XLA Ops:
  73.3 31.5 %collective-permute-start.306 = (f32[512,512]{1,0:T(8,128)}, f32[512,512]{1,0:T(8,128)}, u32[]{:S(2)}, u32[]{:S(2)}) collective-permute-start(f32[512,512]{1,0:T(8,128)} %get-tuple-element.2937), channel_id=1, source_target_pairs={{0,8},{1,9},{2,10},{3,11},{4,12},{5,13},{6,14},{7,15},{16,32},{17,... | collective-permute-start | bytes 3145736 | tf_op jit(solution)/shard_map/cond/branch_1_fun/ppermute | solution.py:377
  74.9 7.2 collective-permute-start.136
  76.6 9.0 collective-permute-start.137
  91.7 584.4 %collective-permute-start.307 = (f32[512,512]{1,0:T(8,128)}, f32[512,512]{1,0:T(8,128)}, u32[]{:S(2)}, u32[]{:S(2)}) collective-permute-start(f32[512,512]{1,0:T(8,128)} %get-tuple-element.2937), channel_id=1, source_target_pairs={{0,16},{1,17},{2,18},{3,19},{4,20},{5,21},{6,22},{7,23},{16,48},{1... | collective-permute-start | bytes 3145736 | tf_op jit(solution)/shard_map/cond/branch_1_fun/ppermute | solution.py:377
  681.1 30.1 %collective-permute-start.315 = (f32[512,512]{1,0:T(8,128)}, f32[512,512]{1,0:T(8,128)}, u32[]{:S(2)}, u32[]{:S(2)}) collective-permute-start(f32[512,512]{1,0:T(8,128)} %get-tuple-element.3015), channel_id=1, source_target_pairs={{8,16},{9,17},{10,18},{11,19},{12,20},{13,21},{14,22},{15,23},{0,2... | collective-permute-start | bytes 3145736 | tf_op jit(solution)/shard_map/cond/branch_1_fun/ppermute | solution.py:377
  683.0 8.5 collective-permute-start.152
  698.0 58.7 %collective-permute-start.316 = (f32[512,512]{1,0:T(8,128)}, f32[512,512]{1,0:T(8,128)}, u32[]{:S(2)}, u32[]{:S(2)}) collective-permute-start(f32[512,512]{1,0:T(8,128)} %get-tuple-element.3015), channel_id=1, source_target_pairs={{8,24},{9,25},{10,26},{11,27},{12,28},{13,29},{14,30},{15,31},{0,3... | collective-permute-start | bytes 3145736 | tf_op jit(solution)/shard_map/cond/branch_1_fun/ppermute | solution.py:377
  762.2 36.2 %collective-permute-start.324 = (f32[512,512]{1,0:T(8,128)}, f32[512,512]{1,0:T(8,128)}, u32[]{:S(2)}, u32[]{:S(2)}) collective-permute-start(f32[512,512]{1,0:T(8,128)} %get-tuple-element.3093), channel_id=1, source_target_pairs={{16,24},{17,25},{18,26},{19,27},{20,28},{21,29},{22,30},{23,31},{8... | collective-permute-start | bytes 3145736 | tf_op jit(solution)/shard_map/cond/branch_1_fun/ppermute | solution.py:377
  763.6 7.0 collective-permute-start.167
  781.1 24.5 %collective-permute-start.325 = (f32[512,512]{1,0:T(8,128)}, f32[512,512]{1,0:T(8,128)}, u32[]{:S(2)}, u32[]{:S(2)}) collective-permute-start(f32[512,512]{1,0:T(8,128)} %get-tuple-element.3093), channel_id=1, source_target_pairs={{16,32},{17,33},{18,34},{19,35},{20,36},{21,37},{22,38},{23,39},{8... | collective-permute-start | bytes 3145736 | tf_op jit(solution)/shard_map/cond/branch_1_fun/ppermute | solution.py:377
  806.7 68.1 %collective-permute-start.333 = (f32[512,512]{1,0:T(8,128)}, f32[512,512]{1,0:T(8,128)}, u32[]{:S(2)}, u32[]{:S(2)}) collective-permute-start(f32[512,512]{1,0:T(8,128)} %get-tuple-element.3171), channel_id=1, source_target_pairs={{24,32},{25,33},{26,34},{27,35},{28,36},{29,37},{30,38},{31,39},{1... | collective-permute-start | bytes 3145736 | tf_op jit(solution)/shard_map/cond/branch_1_fun/ppermute | solution.py:377
  808.0 7.3 collective-permute-start.181
  808.3 7.3 collective-permute-start.182
  826.3 91.7 %collective-permute-start.334 = (f32[512,512]{1,0:T(8,128)}, f32[512,512]{1,0:T(8,128)}, u32[]{:S(2)}, u32[]{:S(2)}) collective-permute-start(f32[512,512]{1,0:T(8,128)} %get-tuple-element.3171), channel_id=1, source_target_pairs={{24,40},{25,41},{26,42},{27,43},{28,44},{29,45},{30,46},{31,47},{1... | collective-permute-start | bytes 3145736 | tf_op jit(solution)/shard_map/cond/branch_1_fun/ppermute | solution.py:377
  879.8 7.1 collective-permute-start.326
  923.2 71.8 %collective-permute-start.342 = (f32[512,512]{1,0:T(8,128)}, f32[512,512]{1,0:T(8,128)}, u32[]{:S(2)}, u32[]{:S(2)}) collective-permute-start(f32[512,512]{1,0:T(8,128)} %get-tuple-element.3244), channel_id=1, source_target_pairs={{32,40},{33,41},{34,42},{35,43},{36,44},{37,45},{38,46},{39,47},{2... | collective-permute-start | bytes 3145736 | tf_op jit(solution)/shard_map/cond/branch_1_fun/ppermute | solution.py:377
  925.2 7.0 collective-permute-start.197
  941.9 92.1 %collective-permute-start.343 = (f32[512,512]{1,0:T(8,128)}, f32[512,512]{1,0:T(8,128)}, u32[]{:S(2)}, u32[]{:S(2)}) collective-permute-start(f32[512,512]{1,0:T(8,128)} %get-tuple-element.3244), channel_id=1, source_target_pairs={{32,48},{33,49},{34,50},{35,51},{36,52},{37,53},{38,54},{39,55},{2... | collective-permute-start | bytes 3145736 | tf_op jit(solution)/shard_map/cond/branch_1_fun/ppermute | solution.py:377
  1000.3 6.9 collective-permute-start.336
  1036.7 7.5 collective-permute-start.204
  1044.7 7.8 collective-permute-start.207
  1055.6 7.0 collective-permute-start.210
  1064.6 28.2 %collective-permute-start.344 = (f32[512,512]{1,0:T(8,128)}, f32[512,512]{1,0:T(8,128)S(1)}, u32[]{:S(2)}, u32[]{:S(2)}) collective-permute-start(f32[512,512]{1,0:T(8,128)} %get-tuple-element.3286), channel_id=1, source_target_pairs={{40,48},{41,49},{42,50},{43,51},{44,52},{45,53},{46,54},{47,55},{3... | collective-permute-start | bytes 3145736 | tf_op jit(solution)/shard_map/cond/branch_1_fun/ppermute | solution.py:377
  1066.1 8.7 collective-permute-start.212
  (60 other events, 280.5 us)

commit v7 on v6

--- a/solution.py
+++ b/solution.py
@@ -211,29 +211,16 @@
         return 0
 
     lax.fori_loop(0, TALL // chunk, subtract, 0)
-    head = pl.ds(0, SHARE)
-    tail = pl.ds(SHARE, TALL - SHARE)
-    after = pl.ds(pl.multiple_of((source + 2) * SHARE, SHARE), TALL - SHARE)
-
-    def put_head():
-        first = pl.ds(pl.multiple_of((source + 1) * SHARE, SHARE), SHARE)
-        store = [
-            pltpu.make_async_copy(target.at[head], following, sems.at[0]),
-            pltpu.make_async_copy(target.at[head], factors.at[first], sems.at[2]),
-        ]
-        for copy in store:
-            copy.start()
-        for copy in store:
-            copy.wait()
-
-    rest = pltpu.make_async_copy(target.at[tail], factors.at[after], sems.at[1])
-    rest.start()
+    store = [
+        pltpu.make_async_copy(target.at[pl.ds(0, SHARE)], following, sems.at[0]),
+        pltpu.make_async_copy(target, factors.at[rows], sems.at[1]),
+    ]
+    for copy in store:
+        copy.start()
+    for copy in store:
+        copy.wait()
     if far:
-        pl.when(panel != step + 2)(put_head)
         keep.wait()
-    else:
-        put_head()
-    rest.wait()
 
 
 def place_kernel(scal, upper_in, *rest):
@@ -469,8 +456,11 @@
             source = jnp.maximum(step - lag_of(step, FAR | NEAR, panel), 0)
             takers = sorted(set(near) | set(far))
 
-            (fresh,) = when(takers, lambda fresh: (collect(fresh, following),), fresh)
+            following, fresh = when(
+                takers, lambda following, fresh: (following, collect(fresh, following)), following, fresh
+            )
             high, low = inverse(fresh, y_high, y_low)
+            factors, high, low = lax.optimization_barrier((factors, high, low))
             others = [c for c in takers if c != coming]
             mine = panel == step
             stored = jnp.where(among(panel, others), source, -1) if others else jnp.int32(-1)
@@ -490,18 +480,14 @@
 
             factors, fresh = when(sorted(set(near) & set(far)), again, factors, fresh)
 
-            def far_next(factors, cur, upper, following):
-                row = advance(step, factors, following, fresh, q)
-                parts = gather(row)
-                factors, cur, following = update(step, True, where, factors, cur, following, fresh, q)
-                return factors, cur, put_in_place(where, upper, parts), following
-
             def far_update(factors, cur, following):
                 return update(step, True, where, factors, cur, following, fresh, q)
 
             if far:
-                factors, cur, upper, following = when([step + 2], far_next, factors, cur, upper, following)
-                factors, cur, following = when([c for c in far if c != step + 2], far_update, factors, cur, following)
+                factors, cur, following = when(far, far_update, factors, cur, following)
+                following, upper = when(
+                    [step + 2], lambda following, upper: (following, collect(upper, following)), following, upper
+                )
 
             def own(factors, cur, front):
                 return multiply(coming, factors, cur, front, upper, p, high, low)

time: 1120 us -> 1090 us (0.973)
  waiting for transfers between devices: 754 us -> 703 us
  local copies, waits for them, and re-layouts: 31.3 us -> 50.8 us
    ppermute x11, waiting for transfers between devices: 726 us -> 676 us  [send(): return lax.ppermute(cur, ('col', 'row'), pairs)]
    cond x19 -> x31, local copies, waits for them, and re-layouts: 19.3 us -> 38.8 us
    pallas_call x42 -> x41, Pallas kernels: 151 us -> 148 us  [call(): pl.pallas_call(kernel, out_shape=out_shape, in_specs=[SMEM] * len(first)...]
    another operation x63 -> x64, loops' own time: 62.7 us -> 60.9 us  [when(): lax.cond(among(panel, panels), lambda *state: tuple(run(*state)), lambda...]
  transfers between devices with their start and end apart: 75 -> 75, of which waited for: 34 -> 39; matrix products, arithmetic and copies ran while one was open for 2% -> 3% of each run, Pallas kernels for 11% -> 10%
where the time goes in v7:
time: 1090 us; the launch traced here: 1080 us
  waiting for transfers between devices  703 us (64%)
  Pallas kernels  148 us (14%)
  starting transfers between devices  108 us (10%)
  loops' own time  60.9 us (6%)
  local copies, waits for them, and re-layouts  50.8 us (5%)
    ppermute x11, waiting for transfers between devices, send(): return lax.ppermute(cur, ('col', 'row'), pairs)  676 us
    pallas_call x41, Pallas kernels, call(): pl.pallas_call(kernel, out_shape=out_shape, in_specs=[SMEM] * len(first)...  148 us
    another operation x64, loops' own time, when(): lax.cond(among(panel, panels), lambda *state: tuple(run(*state)), lambda...  60.9 us
    cond x31, local copies, waits for them, and re-layouts  38.8 us
    ppermute x27, starting transfers between devices, gather(): lax.ppermute(share, 'row', [(r, (r + 2 * turn) % ROWS) for r in range(ROW...  32.4 us
    ppermute x27, starting transfers between devices, gather(): lax.ppermute(part, 'row', swap)  32.2 us
    ppermute x9, starting transfers between devices, gather(): beside = lax.ppermute(share, 'row', swap)  27.2 us
  transfers between devices with their start and end apart: 75, of which 39 were waited for; matrix products, arithmetic and copies ran while one was open for 3% of the time, Pallas kernels for 10%

profile of v7, /device:TPU:31, one launch (start us, length us, event | category | flops | bytes accessed | tf_op | source)
XLA Modules:
  0.0 1077.3 jit_solution(8211303024799954428)
XLA Ops:
  12.6 14.5 %conditional.123 = ((f32[1536,512]{1,0:T(8,128)}, f32[512,512]{1,0:T(8,128)}, f32[64,512]{1,0:T(8,128)S(1)}, f32[512,512]{1,0:T(8,128)}, f32[512,512]{1,0:T(8,128)}, /*index=5*/f32[64,512]{1,0:T(8,128)S(1)})) conditional(s32[]{:T(128)} %convert_element_type.337, (f32[1536,512]{1,0:T(8,128)}, f32[512,512]{1,0:T(8,128)}, f32[64,512]{1,0:T(8,128)S(1)}, ...), branch_computations={%region_34.35_spmd, %region_35.48_spmd} | conditional | flops 53 | bytes 21497526 | solution.py:419
  27.3 14.6 %conditional.127 = ((f32[1536,512]{1,0:T(8,128)}, f32[512,512]{1,0:T(8,128)}, f32[64,512]{1,0:T(8,128)S(1)}, f32[512,512]{1,0:T(8,128)}, f32[512,512]{1,0:T(8,128)}, /*index=5*/f32[64,512]{1,0:T(8,128)S(1)})) conditional(s32[]{:T(128)} %convert_element_type.335, (f32[1536,512]{1,0:T(8,128)}, f32[512,512]{1,0:T(8,128)}, f32[64,512]{1,0:T(8,128)S(1)}, ...), branch_computations={%region_66.67_spmd, %region_67.80_spmd} | conditional | flops 53 | bytes 21497526 | solution.py:419
  42.0 14.6 %conditional.131 = ((f32[1536,512]{1,0:T(8,128)}, f32[512,512]{1,0:T(8,128)}, f32[64,512]{1,0:T(8,128)S(1)}, f32[512,512]{1,0:T(8,128)}, f32[512,512]{1,0:T(8,128)}, /*index=5*/f32[64,512]{1,0:T(8,128)S(1)})) conditional(s32[]{:T(128)} %convert_element_type.333, (f32[1536,512]{1,0:T(8,128)}, f32[512,512]{1,0:T(8,128)}, f32[64,512]{1,0:T(8,128)S(1)}, ...), branch_computations={%region_98.99_spmd, %region_99.112_spmd} | conditional | flops 53 | bytes 25691820 | solution.py:419
  56.7 14.8 %conditional.135 = ((f32[1536,512]{1,0:T(8,128)}, f32[512,512]{1,0:T(8,128)}, f32[64,512]{1,0:T(8,128)S(1)}, f32[512,512]{1,0:T(8,128)}, f32[512,512]{1,0:T(8,128)}, /*index=5*/f32[64,512]{1,0:T(8,128)S(1)})) conditional(s32[]{:T(128)} %convert_element_type.331, (f32[1536,512]{1,0:T(8,128)}, f32[512,512]{1,0:T(8,128)}, ...), branch_computations={%region_130.131_spmd, %region_131.144_spmd} | conditional | flops 53 | bytes 25691820 | solution.py:419
  71.6 600.3 %conditional.137 = ((f32[1536,512]{1,0:T(8,128)}, f32[512,512]{1,0:T(8,128)}, f32[64,512]{1,0:T(8,128)S(1)}, f32[512,512]{1,0:T(8,128)}, f32[512,512]{1,0:T(8,128)}, /*index=5*/f32[64,512]{1,0:T(8,128)S(1)})) conditional(s32[]{:T(128)} %convert_element_type.330, (f32[1536,512]{1,0:T(8,128)}, f32[512,512]{1,0:T(8,128)}, ...), branch_computations={%region_146.147_spmd, %region_147.160_spmd} | conditional | flops 53 | bytes 25691820 | solution.py:419
  73.2 16.8 %conditional.52 = (f32[512,512]{1,0:T(8,128)}) conditional(s32[]{:T(128)} %convert_element_type.274, f32[512,512]{1,0:T(8,128)} %get-tuple-element.2827, (f32[64,512]{1,0:T(8,128)S(1)}, s32[2]{0:T(128)S(1)}, f32[512,512]{1,0:T(8,128)}) %tuple.785), branch_computations={%region_148.148_spmd, %region_149.149_spmd} | conditional | bytes 3670304 | solution.py:419
  107.8 557.9 %collective-permute-done.336 = f32[512,512]{1,0:T(8,128)} collective-permute-done((f32[512,512]{1,0:T(8,128)}, f32[512,512]{1,0:T(8,128)}, u32[]{:S(2)}, u32[]{:S(2)}) %collective-permute-start.336) | collective-permute-done | bytes 1048608 | tf_op jit(solution)/shard_map/cond/branch_1_fun/ppermute | solution.py:364
  671.9 76.7 %conditional.139 = ((f32[1536,512]{1,0:T(8,128)}, f32[512,512]{1,0:T(8,128)}, f32[64,512]{1,0:T(8,128)S(1)}, f32[512,512]{1,0:T(8,128)}, f32[512,512]{1,0:T(8,128)}, /*index=5*/f32[64,512]{1,0:T(8,128)S(1)})) conditional(s32[]{:T(128)} %convert_element_type.329, (f32[1536,512]{1,0:T(8,128)}, f32[512,512]{1,0:T(8,128)}, ...), branch_computations={%region_162.163_spmd, %region_163.176_spmd} | conditional | flops 50 | bytes 25691812 | solution.py:419
  673.5 15.3 %conditional.58 = (f32[512,512]{1,0:T(8,128)}) conditional(s32[]{:T(128)} %convert_element_type.280, f32[512,512]{1,0:T(8,128)} %get-tuple-element.2905, (f32[64,512]{1,0:T(8,128)S(1)}, s32[2]{0:T(128)S(1)}, f32[512,512]{1,0:T(8,128)}) %tuple.803), branch_computations={%region_164.164_spmd, %region_165.165_spmd} | conditional | bytes 3670304 | solution.py:419
  706.7 35.4 %collective-permute-done.338 = f32[512,512]{1,0:T(8,128)} collective-permute-done((f32[512,512]{1,0:T(8,128)}, f32[512,512]{1,0:T(8,128)}, u32[]{:S(2)}, u32[]{:S(2)}) %collective-permute-start.338) | collective-permute-done | bytes 1048608 | tf_op jit(solution)/shard_map/cond/branch_1_fun/ppermute | solution.py:364
  748.6 44.8 %conditional.141 = ((f32[1536,512]{1,0:T(8,128)}, f32[512,512]{1,0:T(8,128)}, f32[64,512]{1,0:T(8,128)S(1)}, f32[512,512]{1,0:T(8,128)}, f32[512,512]{1,0:T(8,128)}, /*index=5*/f32[64,512]{1,0:T(8,128)S(1)})) conditional(s32[]{:T(128)} %convert_element_type.328, (f32[1536,512]{1,0:T(8,128)}, f32[512,512]{1,0:T(8,128)}, ...), branch_computations={%region_178.179_spmd, %region_179.192_spmd} | conditional | flops 46 | bytes 29886104 | solution.py:419
  750.0 17.0 %conditional.64 = (f32[512,512]{1,0:T(8,128)}) conditional(s32[]{:T(128)} %convert_element_type.285, f32[512,512]{1,0:T(8,128)} %get-tuple-element.2983, (f32[64,512]{1,0:T(8,128)S(1)}, s32[2]{0:T(128)S(1)}, f32[512,512]{1,0:T(8,128)}) %tuple.821), branch_computations={%region_180.180_spmd, %region_181.181_spmd} | conditional | bytes 7864608 | solution.py:419
  793.4 105.3 %conditional.143 = ((f32[1536,512]{1,0:T(8,128)}, f32[512,512]{1,0:T(8,128)}, f32[64,512]{1,0:T(8,128)S(1)}, f32[512,512]{1,0:T(8,128)}, f32[512,512]{1,0:T(8,128)}, /*index=5*/f32[64,512]{1,0:T(8,128)S(1)})) conditional(s32[]{:T(128)} %convert_element_type.327, (f32[1536,512]{1,0:T(8,128)}, f32[512,512]{1,0:T(8,128)}, ...), branch_computations={%region_194.195_spmd, %region_195.208_spmd} | conditional | flops 43 | bytes 29886092 | solution.py:419
  794.7 17.3 %conditional.70 = (f32[512,512]{1,0:T(8,128)}) conditional(s32[]{:T(128)} %convert_element_type.289, f32[512,512]{1,0:T(8,128)} %get-tuple-element.3061, (f32[64,512]{1,0:T(8,128)S(1)}, s32[2]{0:T(128)S(1)}, f32[512,512]{1,0:T(8,128)}) %tuple.839), branch_computations={%region_196.196_spmd, %region_197.197_spmd} | conditional | bytes 7864608 | solution.py:419
  825.1 28.2 %collective-permute-done.341 = f32[512,512]{1,0:T(8,128)} collective-permute-done((f32[512,512]{1,0:T(8,128)}, f32[512,512]{1,0:T(8,128)}, u32[]{:S(2)}, u32[]{:S(2)}) %collective-permute-start.341) | collective-permute-done | bytes 1048608 | tf_op jit(solution)/shard_map/cond/branch_1_fun/ppermute | solution.py:364
  858.5 22.5 %conditional.72 = (f32[1536,512]{1,0:T(8,128)}, f32[512,512]{1,0:T(8,128)}) conditional(s32[]{:T(128)} %convert_element_type.288, (f32[1536,512]{1,0:T(8,128)}, f32[512,512]{1,0:T(8,128)}) %tuple.843, (s32[]{:T(128)}, s32[]{:T(128)}, s32[]{:T(128)}, f32[64,512]{1,0:T(8,128)S(1)}, s32[2]{0:T(128)S(1)}, /*index=5*/f32[512,512]{1,0:T(8,128)}, ...), branch_computations={%region_200.200_spmd, %region_201.201_spmd} | conditional | flops 7 | bytes 5767500 | solution.py:419
  883.3 9.1 collective-permute-done.342
  898.8 123.7 %conditional.145 = ((f32[1536,512]{1,0:T(8,128)}, f32[512,512]{1,0:T(8,128)}, f32[64,512]{1,0:T(8,128)S(1)}, f32[512,512]{1,0:T(8,128)}, f32[512,512]{1,0:T(8,128)}, /*index=5*/f32[64,512]{1,0:T(8,128)S(1)})) conditional(s32[]{:T(128)} %convert_element_type.326, (f32[1536,512]{1,0:T(8,128)}, f32[512,512]{1,0:T(8,128)}, ...), branch_computations={%region_210.211_spmd, %region_211.224_spmd} | conditional | flops 40 | bytes 29886080 | solution.py:419
  900.1 16.5 %conditional.76 = (f32[512,512]{1,0:T(8,128)}) conditional(s32[]{:T(128)} %convert_element_type.293, f32[512,512]{1,0:T(8,128)} %get-tuple-element.3139, (f32[64,512]{1,0:T(8,128)S(1)}, s32[2]{0:T(128)S(1)}, f32[512,512]{1,0:T(8,128)}) %tuple.857), branch_computations={%region_212.212_spmd, %region_213.213_spmd} | conditional | bytes 7864608 | solution.py:419
  929.7 37.2 %collective-permute-done.343 = f32[512,512]{1,0:T(8,128)} collective-permute-done((f32[512,512]{1,0:T(8,128)}, f32[512,512]{1,0:T(8,128)}, u32[]{:S(2)}, u32[]{:S(2)}) %collective-permute-start.343) | collective-permute-done | bytes 1048608 | tf_op jit(solution)/shard_map/cond/branch_1_fun/ppermute | solution.py:364
  972.1 21.9 %conditional.78 = (f32[1536,512]{1,0:T(8,128)}, f32[512,512]{1,0:T(8,128)}) conditional(s32[]{:T(128)} %convert_element_type.292, (f32[1536,512]{1,0:T(8,128)}, f32[512,512]{1,0:T(8,128)}) %tuple.861, (s32[]{:T(128)}, s32[]{:T(128)}, s32[]{:T(128)}, f32[64,512]{1,0:T(8,128)S(1)}, s32[2]{0:T(128)S(1)}, /*index=5*/f32[512,512]{1,0:T(8,128)}, ...), branch_computations={%region_216.216_spmd, %region_217.217_spmd} | conditional | flops 7 | bytes 5767500 | solution.py:419
  1007.0 15.5 %conditional.80 = (f32[512,512]{1,0:T(8,128)}) conditional(s32[]{:T(128)} %convert_element_type.292, f32[512,512]{1,0:T(8,128)} %get-tuple-element.3147.upper_in, (f32[64,512]{1,0:T(8,128)S(1)}, s32[2]{0:T(128)S(1)}, f32[512,512]{1,0:T(8,128)}) %tuple.866), branch_computations={%region_220.220_spmd, %region_221.221_spmd} | conditional | bytes 3670304 | solution.py:419
  1031.2 35.3 %conditional.147 = ((f32[1536,512]{1,0:T(8,128)}, f32[512,512]{1,0:T(8,128)})) conditional(s32[]{:T(128)} %convert_element_type.325, (f32[1536,512]{1,0:T(8,128)}, f32[512,512]{1,0:T(8,128)}) %tuple.965, (s32[]{:T(128)}, s32[]{:T(128)}, f32[512,512]{1,0:T(8,128)}, f32[64,512]{1,0:T(8,128)S(1)}, s32[2]{0:T(128)S(1)}, ...), branch_computations={%region_226.227_spmd, %region_227.232_spmd} | conditional | flops 17 | bytes 14156333 | solution.py:419
  1032.5 16.5 %conditional.82 = (f32[512,512]{1,0:T(8,128)}) conditional(s32[]{:T(128)} %convert_element_type.294, f32[512,512]{1,0:T(8,128)} %get-tuple-element.3184, (f32[64,512]{1,0:T(8,128)S(1)}, s32[2]{0:T(128)S(1)}, f32[512,512]{1,0:T(8,128)}) %tuple.870), branch_computations={%region_228.228_spmd, %region_229.229_spmd} | conditional | bytes 5767456 | solution.py:419
  (298 shorter events, 408.0 us)
Async XLA Ops:
  71.6 31.6 %collective-permute-start.335 = (f32[512,512]{1,0:T(8,128)}, f32[512,512]{1,0:T(8,128)}, u32[]{:S(2)}, u32[]{:S(2)}) collective-permute-start(f32[512,512]{1,0:T(8,128)} %get-tuple-element.2837), channel_id=1, source_target_pairs={{0,8},{1,9},{2,10},{3,11},{4,12},{5,13},{6,14},{7,15},{16,32},{17,... | collective-permute-start | bytes 3145736 | tf_op jit(solution)/shard_map/cond/branch_1_fun/ppermute | solution.py:364
  73.2 7.2 collective-permute-start.136
  74.9 9.0 collective-permute-start.137
  90.0 575.7 %collective-permute-start.336 = (f32[512,512]{1,0:T(8,128)}, f32[512,512]{1,0:T(8,128)}, u32[]{:S(2)}, u32[]{:S(2)}) collective-permute-start(f32[512,512]{1,0:T(8,128)} %get-tuple-element.2837), channel_id=1, source_target_pairs={{0,16},{1,17},{2,18},{3,19},{4,20},{5,21},{6,22},{7,23},{16,48},{1... | collective-permute-start | bytes 3145736 | tf_op jit(solution)/shard_map/cond/branch_1_fun/ppermute | solution.py:364
  671.9 30.1 %collective-permute-start.337 = (f32[512,512]{1,0:T(8,128)}, f32[512,512]{1,0:T(8,128)}, u32[]{:S(2)}, u32[]{:S(2)}) collective-permute-start(f32[512,512]{1,0:T(8,128)} %get-tuple-element.2915), channel_id=1, source_target_pairs={{8,16},{9,17},{10,18},{11,19},{12,20},{13,21},{14,22},{15,23},{0,2... | collective-permute-start | bytes 3145736 | tf_op jit(solution)/shard_map/cond/branch_1_fun/ppermute | solution.py:364
  673.8 8.5 collective-permute-start.152
  688.9 53.2 %collective-permute-start.338 = (f32[512,512]{1,0:T(8,128)}, f32[512,512]{1,0:T(8,128)}, u32[]{:S(2)}, u32[]{:S(2)}) collective-permute-start(f32[512,512]{1,0:T(8,128)} %get-tuple-element.2915), channel_id=1, source_target_pairs={{8,24},{9,25},{10,26},{11,27},{12,28},{13,29},{14,30},{15,31},{0,3... | collective-permute-start | bytes 3145736 | tf_op jit(solution)/shard_map/cond/branch_1_fun/ppermute | solution.py:364
  748.7 34.0 %collective-permute-start.339 = (f32[512,512]{1,0:T(8,128)}, f32[512,512]{1,0:T(8,128)}, u32[]{:S(2)}, u32[]{:S(2)}) collective-permute-start(f32[512,512]{1,0:T(8,128)} %get-tuple-element.2993), channel_id=1, source_target_pairs={{16,24},{17,25},{18,26},{19,27},{20,28},{21,29},{22,30},{23,31},{8... | collective-permute-start | bytes 3145736 | tf_op jit(solution)/shard_map/cond/branch_1_fun/ppermute | solution.py:364
  750.0 7.2 collective-permute-start.166
  750.3 6.9 collective-permute-start.167
  767.0 25.3 %collective-permute-start.340 = (f32[512,512]{1,0:T(8,128)}, f32[512,512]{1,0:T(8,128)}, u32[]{:S(2)}, u32[]{:S(2)}) collective-permute-start(f32[512,512]{1,0:T(8,128)} %get-tuple-element.2993), channel_id=1, source_target_pairs={{16,32},{17,33},{18,34},{19,35},{20,36},{21,37},{22,38},{23,39},{8... | collective-permute-start | bytes 3145736 | tf_op jit(solution)/shard_map/cond/branch_1_fun/ppermute | solution.py:364
  793.4 60.0 %collective-permute-start.341 = (f32[512,512]{1,0:T(8,128)}, f32[512,512]{1,0:T(8,128)}, u32[]{:S(2)}, u32[]{:S(2)}) collective-permute-start(f32[512,512]{1,0:T(8,128)} %get-tuple-element.3071), channel_id=1, source_target_pairs={{24,32},{25,33},{26,34},{27,35},{28,36},{29,37},{30,38},{31,39},{1... | collective-permute-start | bytes 3145736 | tf_op jit(solution)/shard_map/cond/branch_1_fun/ppermute | solution.py:364
  794.7 7.6 collective-permute-start.181
  794.8 7.5 collective-permute-start.182
  812.0 80.4 %collective-permute-start.342 = (f32[512,512]{1,0:T(8,128)}, f32[512,512]{1,0:T(8,128)}, u32[]{:S(2)}, u32[]{:S(2)}) collective-permute-start(f32[512,512]{1,0:T(8,128)} %get-tuple-element.3071), channel_id=1, source_target_pairs={{24,40},{25,41},{26,42},{27,43},{28,44},{29,45},{30,46},{31,47},{1... | collective-permute-start | bytes 3145736 | tf_op jit(solution)/shard_map/cond/branch_1_fun/ppermute | solution.py:364
  858.5 7.6 collective-permute-start.304
  858.8 7.3 collective-permute-start.305
  898.8 68.2 %collective-permute-start.343 = (f32[512,512]{1,0:T(8,128)}, f32[512,512]{1,0:T(8,128)}, u32[]{:S(2)}, u32[]{:S(2)}) collective-permute-start(f32[512,512]{1,0:T(8,128)} %get-tuple-element.3149), channel_id=1, source_target_pairs={{32,40},{33,41},{34,42},{35,43},{36,44},{37,45},{38,46},{39,47},{2... | collective-permute-start | bytes 3145736 | tf_op jit(solution)/shard_map/cond/branch_1_fun/ppermute | solution.py:364
  900.1 6.9 collective-permute-start.196
  916.6 85.3 %collective-permute-start.344 = (f32[512,512]{1,0:T(8,128)}, f32[512,512]{1,0:T(8,128)}, u32[]{:S(2)}, u32[]{:S(2)}) collective-permute-start(f32[512,512]{1,0:T(8,128)} %get-tuple-element.3149), channel_id=1, source_target_pairs={{32,48},{33,49},{34,50},{35,51},{36,52},{37,53},{38,54},{39,55},{2... | collective-permute-start | bytes 3145736 | tf_op jit(solution)/shard_map/cond/branch_1_fun/ppermute | solution.py:364
  972.1 6.9 collective-permute-start.311
  1007.3 7.0 collective-permute-start.204
  1031.2 29.1 %collective-permute-start.318 = (f32[512,512]{1,0:T(8,128)}, f32[512,512]{1,0:T(8,128)S(1)}, u32[]{:S(2)}, u32[]{:S(2)}) collective-permute-start(f32[512,512]{1,0:T(8,128)} %get-tuple-element.3194), channel_id=1, source_target_pairs={{40,48},{41,49},{42,50},{43,51},{44,52},{45,53},{46,54},{47,55},{3... | collective-permute-start | bytes 3145736 | tf_op jit(solution)/shard_map/cond/branch_1_fun/ppermute | solution.py:364
  1032.9 7.9 collective-permute-start.212
  (61 other events, 235.1 us)
